TPU v7x, 128 devices: a whole 4x4x4 slice. The times are simulated.
128 devices in a mesh: clip: 8 (over y, core), seq: 16 (over z, x).
Axes of the slice: x: 4, y: 4, z: 4, core: 2. Of those that a mesh axis runs over, the one named last changes fastest.
Arguments:
- query_raw: bfloat16 [8, 2048, 4096], P('clip', 'seq'), may hold values from -16 to 16
- key_raw: bfloat16 [8, 2048, 4096], P('clip', 'seq'), may hold values from -16 to 16
- value: bfloat16 [8, 2048, 4096], P('clip', 'seq'), may hold values from -6 to 6
- upstream: bfloat16 [8, 2048, 4096], P('clip', 'seq'), may hold values from -6 to 6
- query_gain: float32 [4096], replicated, may hold values from 0.5 to 1.5
- key_gain: float32 [4096], replicated, may hold values from 0.5 to 1.5
- key_blocks: int32 [8, 32, 16, 4], P('clip'), may hold values from 0 to 15, as said below
- live: int32 [8, 32], P('clip'), may hold values from 2 to 4, as said below
Outputs:
- attended: bfloat16 [8, 2048, 4096], P('clip', 'seq')
- grad_query: bfloat16 [8, 2048, 4096], P('clip', 'seq')
- grad_key: bfloat16 [8, 2048, 4096], P('clip', 'seq')
- grad_value: bfloat16 [8, 2048, 4096], P('clip', 'seq')
- grad_query_gain: float32 [4096], replicated
- grad_key_gain: float32 [4096], replicated
Inputs may be any that keep to these rules, and one draw needn't show every extreme that they name: key_blocks[c, h, b, 0] equals b, and the 4 entries of one row are distinct. Only the first live[c, h] entries of a row are selected. `live`: in every clip at least one head uses all 4 entries.
All inputs are finite; a program needn't handle non-finite values.
Results may differ from a plain program's by a relative error of at most 0.035.
Values may be sent and summed in bfloat16 or wider, within the bound.
No kernel may reach another device: no remote copies, remote signals or barrier semaphores. Data moves between devices by JAX's collectives and lax.ppermute only.
A program may use at most 128 MiB of HBM per device.

v0:
```python
import jax
import jax.numpy as jnp
from jax import lax
from jax.sharding import PartitionSpec as P

BLK = 128


EPSILON = 1e-06
blocks_per_step = 4


def in_one_piece(arrays, axis, split_dim, concat_dim, along):
    ends, at = ([], 0)
    for a in arrays[:-1]:
        at += a.shape[along]
        ends.append(at)
    both = jnp.concatenate(arrays, axis=along)
    return tuple(
        jnp.split(
            lax.all_to_all(both, axis, split_axis=split_dim, concat_axis=concat_dim, tiled=True),
            ends,
            axis=along,
        )
    )


def in_blocks(x, dim, devices):
    before, after = (x.shape[:dim], x.shape[dim + 1 :])
    return jnp.moveaxis(x.reshape(*before, devices, -1, *after), dim, 0)


def summed_on_arrival(x, axis, dim):
    tiles = in_blocks(x, dim, lax.axis_size(axis))
    arrived = lax.all_to_all(tiles, axis, split_axis=0, concat_axis=0, tiled=True)
    return arrived.sum(axis=0)


def copy_for_each(x, axis):
    copies = jnp.broadcast_to(x, (lax.axis_size(axis), *x.shape))
    return lax.all_to_all(copies, axis, split_axis=0, concat_axis=0, tiled=True)


def in_order(tiles, dim):
    shape = list(tiles.shape[1:])
    shape[dim] *= tiles.shape[0]
    return jnp.moveaxis(tiles, 0, dim).reshape(shape)


def gather_directly(x, axis, dim):
    tiles = copy_for_each(x, axis)
    return in_order(tiles, dim)


def norm_forward(raw, gain):
    values = raw.astype(jnp.float32)
    inverse = lax.rsqrt(jnp.mean(values * values, axis=-1, keepdims=True) + EPSILON)
    unit_rows = values * inverse
    return (unit_rows, inverse, (unit_rows * gain).astype(jnp.bfloat16))


def norm_backward(unit_rows, inverse, gain, upstream):
    incoming = upstream.astype(jnp.float32)
    scaled = incoming * gain
    inner_mean = jnp.mean(scaled * unit_rows, axis=-1, keepdims=True)
    unscaled_gradient = (inverse * (scaled - unit_rows * inner_mean)).astype(jnp.bfloat16)
    grad_gain = jnp.sum(incoming * unit_rows, axis=0)
    return (unscaled_gradient, grad_gain)


def head_pass(queries, key_rows, values, upstream, block_lists, used_count):
    length, head_width = queries.shape
    block_count = length // BLK
    score_scale = head_width ** (-0.5)
    slot_count = block_lists.shape[1]
    q_blocks = queries.reshape(block_count, BLK, head_width)
    k_blocks = key_rows.reshape(block_count, BLK, head_width)
    v_blocks = values.reshape(block_count, BLK, head_width)
    u_blocks = upstream.reshape(block_count, BLK, head_width)
    selected = jnp.arange(slot_count, dtype=jnp.int32) < used_count

    def group_step(carry, index):
        first_block = index * blocks_per_step
        row_lists = lax.dynamic_slice_in_dim(block_lists, first_block, blocks_per_step, 0)
        q_four = lax.dynamic_slice_in_dim(q_blocks, first_block, blocks_per_step, 0)
        u_four = lax.dynamic_slice_in_dim(u_blocks, first_block, blocks_per_step, 0)
        k_chosen = k_blocks[row_lists]
        v_chosen = v_blocks[row_lists]
        scores = (
            jnp.einsum("gqd,gskd->gqsk", q_four, k_chosen, preferred_element_type=jnp.float32)
            * score_scale
        )
        scores = jnp.where(selected[None, None, :, None], scores, -jnp.inf)
        row_max = jnp.max(scores, axis=(2, 3), keepdims=True)
        raised = jnp.exp(scores - row_max)
        weights = raised / jnp.sum(raised, axis=(2, 3), keepdims=True)
        weights_low = weights.astype(jnp.bfloat16)
        attended = jnp.einsum(
            "gqsk,gskd->gqd", weights_low, v_chosen, preferred_element_type=jnp.float32
        ).astype(jnp.bfloat16)
        delta = jnp.sum(u_four.astype(jnp.float32) * attended.astype(jnp.float32), axis=-1)
        grad_weights = jnp.einsum(
            "gqd,gskd->gqsk", u_four, v_chosen, preferred_element_type=jnp.float32
        )
        grad_low = (weights * (grad_weights - delta[:, :, None, None]) * score_scale).astype(
            jnp.bfloat16
        )
        grad_query = jnp.einsum(
            "gqsk,gskd->gqd", grad_low, k_chosen, preferred_element_type=jnp.float32
        ).astype(jnp.bfloat16)
        key_products = jnp.einsum(
            "gqsk,gqd->gskd", grad_low, q_four, preferred_element_type=jnp.float32
        )
        value_products = jnp.einsum(
            "gqsk,gqd->gskd", weights_low, u_four, preferred_element_type=jnp.float32
        )
        return (carry, (attended, grad_query, key_products, value_products))

    step_index = jnp.arange(block_count // blocks_per_step, dtype=jnp.int32)
    unused, (attended, grad_query, key_products, value_products) = lax.scan(
        group_step, jnp.zeros((), jnp.float32), step_index
    )
    flat_lists = block_lists.reshape(-1)
    empty_grad = jnp.zeros((block_count, BLK, head_width), jnp.float32)
    grad_keys = empty_grad.at[flat_lists].add(key_products.reshape(-1, BLK, head_width))
    grad_values = empty_grad.at[flat_lists].add(value_products.reshape(-1, BLK, head_width))
    return (
        attended.reshape(length, head_width),
        grad_query.reshape(length, head_width),
        grad_keys.reshape(length, head_width).astype(jnp.bfloat16),
        grad_values.reshape(length, head_width).astype(jnp.bfloat16),
    )


def shards(query_raw, key_raw, value, upstream, query_gain, key_gain, key_blocks, live):
    device_list = lax.axis_size("seq")
    tokens = query_raw.shape[1]
    features = query_raw.shape[2]
    head_count = key_blocks.shape[1]
    per_device = head_count // device_list
    head_width = features // head_count
    q_unit, q_inverse, q_normed = norm_forward(query_raw[0], query_gain)
    k_unit, k_inverse, k_normed = norm_forward(key_raw[0], key_gain)
    head_loads = live[0]
    q_split = q_normed.reshape(tokens, head_count, head_width)
    k_split = k_normed.reshape(tokens, head_count, head_width)
    v_split = value[0].reshape(tokens, head_count, head_width)
    u_split = upstream[0].reshape(tokens, head_count, head_width)
    head_ids = jnp.arange(head_count, dtype=jnp.int32)
    q_heads, k_heads, v_heads, u_heads = (
        lax.all_to_all(q_split, "seq", split_axis=1, concat_axis=0, tiled=True),
        lax.all_to_all(k_split, "seq", split_axis=1, concat_axis=0, tiled=True),
        lax.all_to_all(v_split, "seq", split_axis=1, concat_axis=0, tiled=True),
        lax.all_to_all(u_split, "seq", split_axis=1, concat_axis=0, tiled=True),
    )
    owned = lax.dynamic_slice_in_dim(head_ids, lax.axis_index("seq") * per_device, per_device)
    owned_lists = key_blocks[0][owned]
    owned_counts = head_loads[owned]
    results = [
        head_pass(
            q_heads[:, member],
            k_heads[:, member],
            v_heads[:, member],
            u_heads[:, member],
            owned_lists[member],
            owned_counts[member],
        )
        for member in range(per_device)
    ]
    stacked = [jnp.stack([result[part] for result in results], axis=1) for part in range(4)]
    out_back, gq_back, gk_back, gv_back = in_one_piece(
        (stacked[0], stacked[1], stacked[2], stacked[3]), "seq", 0, 1, 2
    )
    attended = out_back.reshape(tokens, features)
    grad_value = gv_back.reshape(tokens, features)
    grad_query, q_gain_part = norm_backward(
        q_unit, q_inverse, query_gain, gq_back.reshape(tokens, features)
    )
    grad_key, k_gain_part = norm_backward(
        k_unit, k_inverse, key_gain, gk_back.reshape(tokens, features)
    )
    joined = jnp.concatenate([q_gain_part, k_gain_part])
    share = summed_on_arrival(joined, "seq", 0)
    share = lax.psum(share, "clip")
    whole = gather_directly(share, "seq", 0)
    q_gain_total = whole[:features]
    k_gain_total = whole[features:]
    return (
        attended[None],
        grad_query[None],
        grad_key[None],
        grad_value[None],
        q_gain_total,
        k_gain_total,
    )


def solution(mesh):
    placed = (
        P("clip", "seq", None),
        P("clip", "seq", None),
        P("clip", "seq", None),
        P("clip", "seq", None),
        P(),
        P(),
        P("clip", None, None, None),
        P("clip", None),
    )
    return jax.shard_map(
        shards,
        mesh=mesh,
        in_specs=placed,
        out_specs=(
            P("clip", "seq", None),
            P("clip", "seq", None),
            P("clip", "seq", None),
            P("clip", "seq", None),
            P(),
            P(),
        ),
        check_vma=False,
    )
```

profile of v0, /device:TPU:0, one launch (start us, length us, event | category | flops | bytes accessed | tf_op | source)
XLA Modules:
  0.0 379.1 jit_solution(4834525063319280687)
XLA Ops:
  2.9 2.8 multiply_convert_fusion
  5.6 8.0 %all-to-all-start.1 = ((bf16[128,32,128]{0,2,1:T(8,128)(2,1)}), bf16[128,32,128]{0,2,1:T(8,128)(2,1)S(1)}, u32[]{:S(2)}, u32[]{:S(2)}) async-start(bf16[128,32,128]{0,2,1:T(8,128)(2,1)} %get-tuple-element.442), calls=%async_computation.1 | async-start | bytes 2097152 | tf_op jit(solution)/shard_map/all_to_all | solution.py:152
  14.9 2.0 multiply_convert_fusion.1
  16.9 14.4 %all-to-all-done.1 = bf16[128,32,128]{0,2,1:T(8,128)(2,1)S(1)} async-done(((bf16[128,32,128]{0,2,1:T(8,128)(2,1)}), bf16[128,32,128]{0,2,1:T(8,128)(2,1)S(1)}, u32[]{:S(2)}, u32[]{:S(2)}) %all-to-all-start.1) | async-done | bytes 1048608 | tf_op jit(solution)/shard_map/all_to_all | solution.py:152
  31.3 3.7 all-to-all-start
  35.1 2.3 copy.227
  37.4 2.3 copy.228
  39.6 11.7 %all-to-all-done = bf16[128,32,128]{0,2,1:T(8,128)(2,1)S(1)} async-done(((bf16[128,32,128]{0,2,1:T(8,128)(2,1)}), bf16[128,32,128]{0,2,1:T(8,128)(2,1)S(1)}, u32[]{:S(2)}, u32[]{:S(2)}) %all-to-all-start) | async-done | bytes 1048608 | tf_op jit(solution)/shard_map/all_to_all | solution.py:151
  51.3 3.7 all-to-all-start.2
  56.3 2.3 copy.230
  61.8 9.5 %all-to-all-done.2 = bf16[128,32,128]{2,0,1:T(8,128)(2,1)S(1)} async-done(((bf16[128,32,128]{2,0,1:T(8,128)(2,1)}), bf16[128,32,128]{2,0,1:T(8,128)(2,1)S(1)}, u32[]{:S(2)}, u32[]{:S(2)}) %all-to-all-start.2) | async-done | bytes 1048608 | tf_op jit(solution)/shard_map/all_to_all | solution.py:153
  71.3 4.5 %all-to-all-start.3 = ((bf16[128,32,128]{0,2,1:T(8,128)(2,1)}), bf16[128,32,128]{0,2,1:T(8,128)(2,1)}, u32[]{:S(2)}, u32[]{:S(2)}) async-start(bf16[128,32,128]{0,2,1:T(8,128)(2,1)} %bitcast.287), calls=%async_computation.3 | async-start | bytes 2097152 | tf_op jit(solution)/shard_map/all_to_all | solution.py:154
  79.7 2.2 fusion.64
  82.8 8.8 %all-to-all-done.3 = bf16[128,32,128]{0,2,1:T(8,128)(2,1)} async-done(((bf16[128,32,128]{0,2,1:T(8,128)(2,1)}), bf16[128,32,128]{0,2,1:T(8,128)(2,1)}, u32[]{:S(2)}, u32[]{:S(2)}) %all-to-all-start.3) | async-done | bytes 1048608 | tf_op jit(solution)/shard_map/all_to_all | solution.py:154
  94.9 2.5 broadcast.215.clone.2
  97.3 2.5 broadcast.215.clone.3
  101.6 62.8 %while.34 = (s32[]{:T(128)}, bf16[4,4,128,128]{3,2,1,0:T(8,128)(2,1)}, bf16[4,4,128,128]{3,2,1,0:T(8,128)(2,1)}, f32[4,4,4,128,128]{4,3,2,1,0:T(8,128)}, f32[4,4...) while((s32[]{:T(128)}, ...), condition=%wide.region_6.7_spmd.clone, body=%wide.region_2.6_spmd.clone.sunk | while | flops 407502400 | bytes 17216512 | solution.py:120
  108.7 2.5 gather_fusion
  113.3 2.2 fusion.125
  124.4 2.5 gather_fusion
  129.0 2.2 fusion.125
  140.1 2.5 gather_fusion
  144.7 2.2 fusion.125
  155.8 2.5 gather_fusion
  160.4 2.2 fusion.125
  164.5 9.0 %scatter_fusion = f32[16,128,128]{2,1,0:T(8,128)S(1)} fusion(f32[16,128,128]{2,1,0:T(8,128)S(1)} %broadcast.220.clone.3, s32[64]{0:T(128)} %fusion.56, f32[64,128,128]{2,1,0:T(8,128)} %bitcast.275), kind=kCustom, calls=%fused_computation.6 | custom fusion | flops 1048576 | bytes 12583168 | tf_op jit(solution)/shard_map/scatter-add | solution.py:125
  174.5 8.8 %scatter_fusion.2 = f32[16,128,128]{2,1,0:T(8,128)S(1)} fusion(f32[16,128,128]{2,1,0:T(8,128)S(1)} %broadcast.220.clone.1, s32[64]{0:T(128)S(1)} %copy-done.25, f32[64,128,128]{2,1,0:T(8,128)} %bitcast.276), kind=kCustom, calls=%fused_computation.8 | custom fusion | flops 1048576 | bytes 12583168 | tf_op jit(solution)/shard_map/scatter-add | solution.py:126
  184.2 2.5 broadcast.215.clone
  186.7 2.5 broadcast.215.clone.1
  190.9 48.1 %while.35 = (s32[]{:T(128)}, bf16[4,4,128,128]{3,2,1,0:T(8,128)(2,1)}, bf16[4,4,128,128]{3,2,1,0:T(8,128)(2,1)}, f32[4,4,4,128,128]{4,3,2,1,0:T(8,128)}, f32[4,4...) while((s32[]{:T(128)}, ...), condition=%wide.region_11.12_spmd.clone, body=%wide.region_7.11_spmd.clone.sunk | while | flops 407502400 | bytes 15103075 | solution.py:120
  198.9 2.2 fusion.141
  210.9 2.2 fusion.141
  223.0 2.2 fusion.141
  235.0 2.2 fusion.141
  239.1 9.0 %scatter_fusion.1 = f32[16,128,128]{2,1,0:T(8,128)S(1)} fusion(f32[16,128,128]{2,1,0:T(8,128)S(1)} %broadcast.220.clone.2, s32[64]{0:T(128)} %fusion.57, f32[64,128,128]{2,1,0:T(8,128)} %bitcast.273), kind=kCustom, calls=%fused_computation.7 | custom fusion | flops 1048576 | bytes 12583168 | tf_op jit(solution)/shard_map/scatter-add | solution.py:125
  248.4 8.8 %scatter_fusion.3 = f32[16,128,128]{2,1,0:T(8,128)S(1)} fusion(f32[16,128,128]{2,1,0:T(8,128)S(1)} %broadcast.220.clone, s32[64]{0:T(128)S(1)} %copy-done.24, f32[64,128,128]{2,1,0:T(8,128)} %bitcast.274), kind=kCustom, calls=%fused_computation.9 | custom fusion | flops 1048576 | bytes 12583168 | tf_op jit(solution)/shard_map/scatter-add | solution.py:126
  257.3 2.6 maximum_maximum_fusion
  259.9 16.6 %copy.243 = bf16[2048,2,512]{2,1,0:T(2,128)(2,1)S(1)} copy(bf16[2048,2,512]{2,0,1:T(8,128)(2,1)S(1)} %maximum_maximum_fusion) | data formatting | bytes 8388608 | tf_op jit(solution)/shard_map/concatenate | solution.py:18
  276.5 52.5 %all_to_all.105 = bf16[2048,2,512]{2,1,0:T(2,128)(2,1)S(1)} all-to-all(bf16[2048,2,512]{2,1,0:T(2,128)(2,1)S(1)} %copy.243), channel_id=1, replica_groups=mesh['clip'=8,'seq'=16] {'seq'}, dimensions={0} | all-to-all | bytes 8388608 | tf_op jit(solution)/shard_map/all_to_all | solution.py:21
  330.1 2.4 fusion.60
  333.3 2.9 multiply_reduce_fusion.2
  338.0 2.6 multiply_reduce_fusion.3
  341.2 3.7 all-to-all-start.5
  344.9 2.6 fusion.52
  347.5 5.0 %all-to-all-done.5 = f32[16,1,512]{2,1,0:T(1,128)S(1)} async-done(((f32[16,1,512]{2,1,0:T(1,128)}), f32[16,1,512]{2,1,0:T(1,128)S(1)}, u32[]{:S(2)}, u32[]{:S(2)}) %all-to-all-start.5) | async-done | bytes 32800 | tf_op jit(solution)/shard_map/all_to_all | solution.py:35
  352.6 12.4 %psum.7 = f32[512]{0:T(512)S(1)} all-reduce(f32[512]{0:T(512)S(1)} %reduce_sum.105), channel_id=1, replica_groups=mesh['clip'=8,'seq'=16] {'clip'}, use_global_device_ids=true, to_apply=%region_21.22 | all-reduce | flops 512 | bytes 4096 | tf_op jit(solution)/shard_map/psum | solution.py:184
  365.6 3.5 all-to-all-start.6
  369.9 2.4 copy.252
  (295 shorter events, 112.0 us)
Async XLA Ops:
  0.6 55.0 %copy-start = (s32[1,32]{1,0:T(1,128)S(1)}, s32[1,32]{1,0:T(1,128)}, u32[]{:S(2)}) copy-start(s32[1,32]{1,0:T(1,128)} %param.19) | copy-start | bytes 388
  2.3 3.4 copy-start.4
  2.3 11.4 %copy-start.13 = (bf16[1,128,4096]{2,1,0:T(8,128)(2,1)S(1)}, bf16[1,128,4096]{2,1,0:T(8,128)(2,1)}, u32[]{:S(2)}) copy-start(bf16[1,128,4096]{2,1,0:T(8,128)(2,1)} %param.12) | copy-start | bytes 3145732
  2.9 2.8 copy-start.22
  2.9 12.1 %copy-start.15 = (f32[4096]{0:T(1024)S(1)}, f32[4096]{0:T(1024)}, u32[]{:S(2)}) copy-start(f32[4096]{0:T(1024)} %param.16) | copy-start | bytes 49156
  5.6 25.7 %all-to-all-start.1 = ((bf16[128,32,128]{0,2,1:T(8,128)(2,1)}), bf16[128,32,128]{0,2,1:T(8,128)(2,1)S(1)}, u32[]{:S(2)}, u32[]{:S(2)}) async-start(bf16[128,32,128]{0,2,1:T(8,128)(2,1)} %get-tuple-element.442), calls=%async_computation.1 | async-start | bytes 2097152 | tf_op jit(solution)/shard_map/all_to_all | solution.py:152
  14.3 23.0 %copy-start.2 = (bf16[1,128,4096]{1,2,0:T(8,128)(2,1)}, bf16[1,128,4096]{1,2,0:T(8,128)(2,1)S(1)}, u32[]{:S(2)}) copy-start(bf16[1,128,4096]{1,2,0:T(8,128)(2,1)S(1)} %copy.222) | copy-start | bytes 3145732
  14.3 20.7 %copy-start.19 = (s32[1,32,16,4]{1,3,2,0:T(4,128)S(1)}, s32[1,32,16,4]{1,3,2,0:T(4,128)}, u32[]{:S(2)}) copy-start(s32[1,32,16,4]{1,3,2,0:T(4,128)} %param.18) | copy-start | bytes 24580
  14.9 20.1 %copy-start.20 = (f32[128]{0:T(128)}, f32[128]{0:T(128)S(1)}, u32[]{:S(2)}) copy-start(f32[128]{0:T(128)S(1)} %add_rsqrt_fusion.1) | copy-start | bytes 1540
  31.3 20.0 %all-to-all-start = ((bf16[128,32,128]{0,2,1:T(8,128)(2,1)}), bf16[128,32,128]{0,2,1:T(8,128)(2,1)S(1)}, u32[]{:S(2)}, u32[]{:S(2)}) async-start(bf16[128,32,128]{0,2,1:T(8,128)(2,1)} %get-tuple-element.444), calls=%async_computation | async-start | bytes 2097152 | tf_op jit(solution)/shard_map/all_to_all | solution.py:151
  51.3 20.0 %all-to-all-start.2 = ((bf16[128,32,128]{2,0,1:T(8,128)(2,1)}), bf16[128,32,128]{2,0,1:T(8,128)(2,1)S(1)}, u32[]{:S(2)}, u32[]{:S(2)}) async-start(bf16[128,32,128]{2,0,1:T(8,128)(2,1)} %copy.228), calls=%async_computation.2 | async-start | bytes 2097152 | tf_op jit(solution)/shard_map/all_to_all | solution.py:153
  71.3 4.5 %copy-start.8 = (bf16[128,32,128]{2,0,1:T(8,128)(2,1)}, bf16[128,32,128]{2,0,1:T(8,128)(2,1)S(1)}, u32[]{:S(2)}) copy-start(bf16[128,32,128]{2,0,1:T(8,128)(2,1)S(1)} %all-to-all-done.2) | copy-start | bytes 3145732
  71.3 20.4 %all-to-all-start.3 = ((bf16[128,32,128]{0,2,1:T(8,128)(2,1)}), bf16[128,32,128]{0,2,1:T(8,128)(2,1)}, u32[]{:S(2)}, u32[]{:S(2)}) async-start(bf16[128,32,128]{0,2,1:T(8,128)(2,1)} %bitcast.287), calls=%async_computation.3 | async-start | bytes 2097152 | tf_op jit(solution)/shard_map/all_to_all | solution.py:154
  106.5 4.7 %copy-start.17 = (f32[4,128]{1,0:T(4,128)}, f32[4,128]{1,0:T(4,128)S(1)}, u32[]{:S(2)}) copy-start(f32[4,128]{1,0:T(4,128)S(1)} %fusion.122) | copy-start | bytes 6148 | tf_op jit(solution)/shard_map/while
  111.3 1.6 copy-start.6
  111.3 1.6 copy-start.18
  122.2 4.7 %copy-start.17 = (f32[4,128]{1,0:T(4,128)}, f32[4,128]{1,0:T(4,128)S(1)}, u32[]{:S(2)}) copy-start(f32[4,128]{1,0:T(4,128)S(1)} %fusion.122) | copy-start | bytes 6148 | tf_op jit(solution)/shard_map/while
  127.0 1.6 copy-start.6
  127.0 1.6 copy-start.18
  137.9 4.7 %copy-start.17 = (f32[4,128]{1,0:T(4,128)}, f32[4,128]{1,0:T(4,128)S(1)}, u32[]{:S(2)}) copy-start(f32[4,128]{1,0:T(4,128)S(1)} %fusion.122) | copy-start | bytes 6148 | tf_op jit(solution)/shard_map/while
  142.7 1.6 copy-start.6
  142.7 1.6 copy-start.18
  153.6 4.7 %copy-start.17 = (f32[4,128]{1,0:T(4,128)}, f32[4,128]{1,0:T(4,128)S(1)}, u32[]{:S(2)}) copy-start(f32[4,128]{1,0:T(4,128)S(1)} %fusion.122) | copy-start | bytes 6148 | tf_op jit(solution)/shard_map/while
  158.4 1.6 copy-start.6
  158.4 1.6 copy-start.18
  164.5 10.0 %copy-start.25 = (s32[64]{0:T(128)S(1)}, s32[64]{0:T(128)}, u32[]{:S(2)}) copy-start(s32[64]{0:T(128)} %fusion.56) | copy-start | bytes 772
  198.5 4.4 %copy-start.27 = (s32[4]{0:T(128)S(1)}, s32[4]{0:T(128)}, u32[]{:S(2)}) copy-start(s32[4]{0:T(128)} %copy-done.26) | copy-start | bytes 52 | tf_op jit(solution)/shard_map/while
  202.9 1.2 copy-start.26
  210.5 4.4 %copy-start.27 = (s32[4]{0:T(128)S(1)}, s32[4]{0:T(128)}, u32[]{:S(2)}) copy-start(s32[4]{0:T(128)} %copy-done.26) | copy-start | bytes 52 | tf_op jit(solution)/shard_map/while
  215.0 1.2 copy-start.26
  222.6 4.4 %copy-start.27 = (s32[4]{0:T(128)S(1)}, s32[4]{0:T(128)}, u32[]{:S(2)}) copy-start(s32[4]{0:T(128)} %copy-done.26) | copy-start | bytes 52 | tf_op jit(solution)/shard_map/while
  227.0 1.2 copy-start.26
  234.6 4.4 %copy-start.27 = (s32[4]{0:T(128)S(1)}, s32[4]{0:T(128)}, u32[]{:S(2)}) copy-start(s32[4]{0:T(128)} %copy-done.26) | copy-start | bytes 52 | tf_op jit(solution)/shard_map/while
  239.1 9.3 %copy-start.24 = (s32[64]{0:T(128)S(1)}, s32[64]{0:T(128)}, u32[]{:S(2)}) copy-start(s32[64]{0:T(128)} %fusion.57) | copy-start | bytes 772
  248.4 8.9 %copy-start.10 = (bf16[16,128,128]{2,1,0:T(8,128)(2,1)S(1)}, bf16[16,128,128]{2,1,0:T(8,128)(2,1)}, u32[]{:S(2)}) copy-start(bf16[16,128,128]{2,1,0:T(8,128)(2,1)} %convert_element_type.172) | copy-start | bytes 1572868
  248.4 8.9 %copy-start.11 = (bf16[16,128,128]{2,1,0:T(8,128)(2,1)S(1)}, bf16[16,128,128]{2,1,0:T(8,128)(2,1)}, u32[]{:S(2)}) copy-start(bf16[16,128,128]{2,1,0:T(8,128)(2,1)} %convert_element_type.176) | copy-start | bytes 1572868
  248.4 8.9 %copy-start.12 = (bf16[4,4,128,128]{3,2,1,0:T(8,128)(2,1)S(1)}, bf16[4,4,128,128]{3,2,1,0:T(8,128)(2,1)}, u32[]{:S(2)}) copy-start(bf16[4,4,128,128]{3,2,1,0:T(8,128)(2,1)} %get-tuple-element.137) | copy-start | bytes 1572868
  330.1 3.2 copy-start.14
  330.1 3.1 copy-start.23
  332.6 5.4 %copy-start.16 = (f32[4096]{0:T(1024)S(1)}, f32[4096]{0:T(1024)}, u32[]{:S(2)}) copy-start(f32[4096]{0:T(1024)} %param.16) | copy-start | bytes 49156
  332.6 5.4 %copy-start.21 = (f32[128]{0:T(128)S(1)}, f32[128]{0:T(128)}, u32[]{:S(2)}) copy-start(f32[128]{0:T(128)} %copy-done.20) | copy-start | bytes 1540
  333.3 3.0 copy-start.7
  333.3 11.7 %copy-start.5 = (bf16[1,128,4096]{1,2,0:T(8,128)(2,1)S(1)}, bf16[1,128,4096]{1,2,0:T(8,128)(2,1)}, u32[]{:S(2)}) copy-start(bf16[1,128,4096]{1,2,0:T(8,128)(2,1)} %copy-done.4) | copy-start | bytes 3145732
  336.3 32.9 %copy-start.3 = (bf16[1,128,4096]{1,2,0:T(8,128)(2,1)S(1)}, bf16[1,128,4096]{1,2,0:T(8,128)(2,1)}, u32[]{:S(2)}) copy-start(bf16[1,128,4096]{1,2,0:T(8,128)(2,1)} %copy-done.2) | copy-start | bytes 3145732
  341.2 11.3 %all-to-all-start.5 = ((f32[16,1,512]{2,1,0:T(1,128)}), f32[16,1,512]{2,1,0:T(1,128)S(1)}, u32[]{:S(2)}, u32[]{:S(2)}) async-start(f32[16,1,512]{2,1,0:T(1,128)} %all_to_all.95), calls=%async_computation.5 | async-start | bytes 65536 | tf_op jit(solution)/shard_map/all_to_all | solution.py:35
  365.6 12.8 %all-to-all-start.6 = ((f32[16,1,512]{2,1,0:T(1,128)}), f32[16,1,512]{2,1,0:T(1,128)S(1)}, u32[]{:S(2)}, u32[]{:S(2)}) async-start(f32[16,1,512]{2,1,0:T(1,128)} %broadcast_in_dim.84), calls=%async_computation.6 | async-start | bytes 65536 | tf_op jit(solution)/shard_map/all_to_all | solution.py:41
  369.9 6.6 %copy-start.9 = (bf16[128,32,128]{2,0,1:T(8,128)(2,1)S(1)}, bf16[128,32,128]{2,0,1:T(8,128)(2,1)}, u32[]{:S(2)}) copy-start(bf16[128,32,128]{2,0,1:T(8,128)(2,1)} %get-tuple-element.454) | copy-start | bytes 3145732
  373.5 5.5 %copy-start.1 = (s32[1,32]{1,0:T(1,128)S(1)}, s32[1,32]{1,0:T(1,128)}, u32[]{:S(2)}) copy-start(s32[1,32]{1,0:T(1,128)} %param.19) | copy-start | bytes 388
  (1 other events, 1.2 us)
where the time goes:
time: 383 us; the launch traced here: 379 us
  local copies, waits for them, and re-layouts  112 us (29%)
  blocking collectives  64.9 us (17%)
  other arithmetic  62.1 us (16%)
  matrix products  56.9 us (15%)
  waiting for transfers between devices  49.5 us (13%)
  starting transfers between devices  27 us (7%)
  loops' own time  5.87 us (2%)
    all_to_all x1, blocking collectives, in_one_piece(): lax.all_to_all(both, axis, split_axis=split_dim, concat_axis=concat_dim,...  52.5 us
    scatter-add x2, other arithmetic, head_pass(): empty_grad.at[flat_lists].add(key_products.reshape(-1, BLK, head_width))  18 us
    scatter-add x2, other arithmetic, head_pass(): empty_grad.at[flat_lists].add(value_products.reshape(-1, BLK, head_width))  17.6 us
    dot_general x8, matrix products, group_step(): jnp.einsum('gqsk,gqd->gskd', grad_low, q_four, preferred_element_type=jnp...  17.5 us
    concatenate x1, local copies, waits for them, and re-layouts, in_one_piece(): both = jnp.concatenate(arrays, axis=along)  16.6 us
    unnamed x57, local copies, waits for them, and re-layouts  15.7 us
    all_to_all x1, waiting for transfers between devices, shards(): lax.all_to_all(k_split, 'seq', split_axis=1, concat_axis=0, tiled=True)  14.4 us
    another operation x12, local copies, waits for them, and re-layouts  13.8 us
  transfers between devices with their start and end apart: 6, of which 5 were waited for; matrix products, arithmetic and copies ran while one was open for 9% of the time, Pallas kernels for 0%

commit v1 on v0

v1 whole, which is shorter than its diff:
```python
import jax
import jax.numpy as jnp
from jax import lax
from jax.experimental import pallas as pl
from jax.experimental.pallas import tpu as pltpu
from jax.sharding import PartitionSpec as P

BLK = 128
EPSILON = 1e-06
ROWS = 16
QUERY, KEY, VALUE, COTANGENT = range(4)
OUT, GRAD_Q, GRAD_K, GRAD_V = range(4)
LOG2E = 1.4426950408889634


def contract(a, b, dims):
    return lax.dot_general(a, b, (dims, ((), ())), preferred_element_type=jnp.float32)


def inverse_rms(x):
    return lax.rsqrt(jnp.mean(x * x, axis=-1, keepdims=True) + EPSILON)


def pack_kernel(q_ref, k_ref, v_ref, u_ref, qg_ref, kg_ref, out_ref):
    groups, _, heads, _, width = out_ref.shape

    def put(kind, rows):
        for group in range(groups):
            for head in range(heads):
                at = (group * heads + head) * width
                out_ref[group, kind, head] = rows[:, at : at + width]

    for kind, ref, gain_ref in ((QUERY, q_ref, qg_ref), (KEY, k_ref, kg_ref)):
        x = ref[...].astype(jnp.float32)
        put(kind, (x * inverse_rms(x) * gain_ref[...]).astype(jnp.bfloat16))
    put(VALUE, v_ref[...])
    put(COTANGENT, u_ref[...])


def pack(q, k, v, u, q_gain, k_gain, groups, heads):
    tokens, features = q.shape
    width = features // (groups * heads)
    rows = pl.BlockSpec((ROWS, features), lambda i: (i, 0))
    gain = pl.BlockSpec((1, features), lambda i: (0, 0))
    return pl.pallas_call(
        pack_kernel,
        grid=(tokens // ROWS,),
        in_specs=[rows] * 4 + [gain] * 2,
        out_specs=pl.BlockSpec((groups, 4, heads, ROWS, width), lambda i: (0, 0, 0, i, 0)),
        out_shape=jax.ShapeDtypeStruct((groups, 4, heads, tokens, width), jnp.bfloat16),
        name="pack",
    )(q, k, v, u, q_gain[None], k_gain[None])


def attention_kernel(lists_ref, live_ref, in_ref, out_ref, gains_ref, kt_ref, vt_ref, dk_ref, dv_ref):
    blocks, _, heads, _, width = in_ref.shape
    scale = width ** (-0.5)

    for head in range(heads):

        def prepare(j, carry):
            kt_ref[j] = in_ref[j, KEY, head].T
            vt_ref[j] = in_ref[j, VALUE, head].T
            dk_ref[j] = jnp.zeros((BLK, width), jnp.float32)
            dv_ref[j] = jnp.zeros((BLK, width), jnp.float32)
            return carry

        lax.fori_loop(0, blocks, prepare, 0)

        def one_block(b, slots):
            q = in_ref[b, QUERY, head]
            u = in_ref[b, COTANGENT, head]
            chosen = [lists_ref[head, b, s] for s in range(slots)]
            scores = [contract(in_ref[j, KEY, head], q, ((1,), (1,))) for j in chosen]
            grads = [contract(in_ref[j, VALUE, head], u, ((1,), (1,))) for j in chosen]
            top = scores[0]
            for s in scores[1:]:
                top = jnp.maximum(top, s)
            top = jnp.max(top, axis=0, keepdims=True) * (scale * LOG2E)
            raised = [jnp.exp2(s * (scale * LOG2E) - top) for s in scores]
            total = raised[0]
            for e in raised[1:]:
                total = total + e
            inverse = 1.0 / jnp.sum(total, axis=0, keepdims=True)
            probs = [e * inverse for e in raised]
            inner = probs[0] * grads[0]
            for p, g in zip(probs[1:], grads[1:]):
                inner = inner + p * g
            delta = jnp.sum(inner, axis=0, keepdims=True)
            low = [p.astype(jnp.bfloat16) for p in probs]
            ds = [(p * (g - delta) * scale).astype(jnp.bfloat16) for p, g in zip(probs, grads)]
            out_t = contract(vt_ref[chosen[0]], low[0], ((1,), (0,)))
            dq_t = contract(kt_ref[chosen[0]], ds[0], ((1,), (0,)))
            for j, p, d in zip(chosen[1:], low[1:], ds[1:]):
                out_t = out_t + contract(vt_ref[j], p, ((1,), (0,)))
                dq_t = dq_t + contract(kt_ref[j], d, ((1,), (0,)))
            out_ref[b, OUT, head] = out_t.T.astype(jnp.bfloat16)
            dq = dq_t.T.astype(jnp.bfloat16)
            out_ref[b, GRAD_Q, head] = dq
            for j, p, d in zip(chosen, low, ds):
                dv_ref[j] += contract(p, u, ((1,), (0,)))
                dk_ref[j] += contract(d, q, ((1,), (0,)))
            return jnp.sum(dq.astype(jnp.float32) * q.astype(jnp.float32), axis=0, keepdims=True)

        gains_ref[head : head + 1] = jnp.zeros((1, width), jnp.float32)
        for slots in (2, 3, 4):

            @pl.when(live_ref[head] == slots)
            def _():
                def step(b, gain):
                    return gain + one_block(b, slots)

                gains_ref[head : head + 1] = lax.fori_loop(
                    0, blocks, step, jnp.zeros((1, width), jnp.float32)
                )

        def finish(j, gain):
            dk = dk_ref[j].astype(jnp.bfloat16)
            out_ref[j, GRAD_K, head] = dk
            out_ref[j, GRAD_V, head] = dv_ref[j].astype(jnp.bfloat16)
            k = in_ref[j, KEY, head].astype(jnp.float32)
            return gain + jnp.sum(dk.astype(jnp.float32) * k, axis=0, keepdims=True)

        gains_ref[heads + head : heads + head + 1] = lax.fori_loop(
            0, blocks, finish, jnp.zeros((1, width), jnp.float32)
        )


def attention(lists, live, arrived):
    blocks, _, heads, _, width = arrived.shape
    vmem = pl.BlockSpec(memory_space=pltpu.VMEM)
    smem = pl.BlockSpec(memory_space=pltpu.SMEM)
    return pl.pallas_call(
        attention_kernel,
        in_specs=[smem, smem, vmem],
        out_specs=[vmem, vmem],
        out_shape=[
            jax.ShapeDtypeStruct(arrived.shape, jnp.bfloat16),
            jax.ShapeDtypeStruct((2 * heads, width), jnp.float32),
        ],
        scratch_shapes=[
            pltpu.VMEM((blocks, width, BLK), jnp.bfloat16),
            pltpu.VMEM((blocks, width, BLK), jnp.bfloat16),
            pltpu.VMEM((blocks, BLK, width), jnp.float32),
            pltpu.VMEM((blocks, BLK, width), jnp.float32),
        ],
        name="attention",
    )(lists, live, arrived)


def unpack_kernel(back_ref, q_ref, k_ref, qg_ref, kg_ref, out_ref, dq_ref, dk_ref, dv_ref):
    groups, _, heads, _, width = back_ref.shape

    def take(kind):
        return jnp.concatenate(
            [back_ref[g, kind, h] for g in range(groups) for h in range(heads)], axis=-1
        )

    out_ref[...] = take(OUT)
    dv_ref[...] = take(GRAD_V)
    for kind, raw_ref, gain_ref, ref in (
        (GRAD_Q, q_ref, qg_ref, dq_ref),
        (GRAD_K, k_ref, kg_ref, dk_ref),
    ):
        x = raw_ref[...].astype(jnp.float32)
        inverse = inverse_rms(x)
        unit = x * inverse
        g = take(kind).astype(jnp.float32) * gain_ref[...]
        mean = jnp.mean(g * unit, axis=-1, keepdims=True)
        ref[...] = (inverse * (g - unit * mean)).astype(jnp.bfloat16)


def unpack(back, q, k, q_gain, k_gain):
    groups, _, heads, tokens, width = back.shape
    features = q.shape[1]
    rows = pl.BlockSpec((ROWS, features), lambda i: (i, 0))
    gain = pl.BlockSpec((1, features), lambda i: (0, 0))
    return pl.pallas_call(
        unpack_kernel,
        grid=(tokens // ROWS,),
        in_specs=[
            pl.BlockSpec((groups, 4, heads, ROWS, width), lambda i: (0, 0, 0, i, 0)),
            rows,
            rows,
            gain,
            gain,
        ],
        out_specs=[rows] * 4,
        out_shape=[jax.ShapeDtypeStruct((tokens, features), jnp.bfloat16)] * 4,
        name="unpack",
    )(back, q, k, q_gain[None], k_gain[None])


def exchange_sum(x, axis):
    size = lax.axis_size(axis)
    step = 1
    while step < size:
        x = x + lax.ppermute(x, axis, [(i, i ^ step) for i in range(size)])
        step *= 2
    return x


def shards(query_raw, key_raw, value, upstream, query_gain, key_gain, key_blocks, live):
    groups = lax.axis_size("seq")
    features = query_raw.shape[2]
    heads = key_blocks.shape[1] // groups
    mine = lax.axis_index("seq")
    lists = lax.dynamic_slice_in_dim(key_blocks[0], mine * heads, heads)
    counts = lax.dynamic_slice_in_dim(live[0], mine * heads, heads)
    packed = pack(
        query_raw[0], key_raw[0], value[0], upstream[0], query_gain, key_gain, groups, heads
    )
    arrived = lax.all_to_all(packed, "seq", split_axis=0, concat_axis=0, tiled=True)
    results, gains = attention(lists, counts, arrived)
    back = lax.all_to_all(results, "seq", split_axis=0, concat_axis=0, tiled=True)
    gains = exchange_sum(gains.reshape(1, -1), "clip")
    gains = jnp.where(jnp.arange(groups)[:, None] == mine, gains, 0.0)
    gains = exchange_sum(gains, "seq").reshape(groups, 2, -1)
    attended, grad_query, grad_key, grad_value = unpack(
        back, query_raw[0], key_raw[0], query_gain, key_gain
    )
    return (
        attended[None],
        grad_query[None],
        grad_key[None],
        grad_value[None],
        gains[:, 0].reshape(features) / query_gain,
        gains[:, 1].reshape(features) / key_gain,
    )


def solution(mesh):
    tokens = P("clip", "seq", None)
    return jax.shard_map(
        shards,
        mesh=mesh,
        in_specs=(tokens,) * 4 + (P(), P(), P("clip", None, None, None), P("clip", None)),
        out_specs=(tokens,) * 4 + (P(), P()),
        check_vma=False,
    )
```

time: 383 us -> 200 us (0.52)
  local copies, waits for them, and re-layouts: 112 us -> 1.55 us
  waiting for transfers between devices: 49.5 us -> 128 us
  blocking collectives: 64.9 us -> 0 us
  other arithmetic: 62.1 us -> 1.49 us
  matrix products: 56.9 us -> 0 us
  Pallas kernels: 0 us -> 39.7 us
  loops' own time: 5.87 us -> 0 us
    ppermute x0 -> x7, waiting for transfers between devices: none -> 66.3 us  [exchange_sum(): x = x + lax.ppermute(x, axis, [(i, i ^ step) for i in range(size)])]
    dot_general x48 -> x0, matrix products: 56.9 us -> none  [the longest x8 17.5 us: group_step(): jnp.einsum('gqsk,gqd->gskd', grad_low, q_four, preferred_element_type=jnp...]
    all_to_all x1 -> x0, blocking collectives: 52.5 us -> none  [in_one_piece(): lax.all_to_all(both, axis, split_axis=split_dim, concat_axis=concat_dim,...]
    pallas_call x0 -> x3, Pallas kernels: none -> 39.7 us  [the longest x1 24.7 us: attention(): pl.pallas_call(attention_kernel, in_specs=[smem, smem, vmem], out_specs=[...]
    scatter-add x4 -> x0, other arithmetic: 35.6 us -> none  [the longest x2 18 us: head_pass(): empty_grad.at[flat_lists].add(key_products.reshape(-1, BLK, head_width))]
    gather x18 -> x0, local copies, waits for them, and re-layouts: 18.8 us -> none  [the longest x8 12.5 us: group_step(): v_chosen = v_blocks[row_lists]]
    concatenate x3 -> x0, local copies, waits for them, and re-layouts: 16.6 us -> none  [the longest x1 16.6 us: in_one_piece(): both = jnp.concatenate(arrays, axis=along)]
    another operation x15 -> x0, local copies, waits for them, and re-layouts: 16.3 us -> none
  transfers between devices with their start and end apart: 6 -> 9, of which waited for: 5 -> 8; matrix products, arithmetic and copies ran while one was open for 9% -> 2% of each run, Pallas kernels for 0% -> 0%
where the time goes in v1:
time: 200 us; the launch traced here: 197 us
  waiting for transfers between devices  128 us (64%)
  Pallas kernels  39.7 us (20%)
  starting transfers between devices  25.2 us (13%)
    ppermute x7, waiting for transfers between devices, exchange_sum(): x = x + lax.ppermute(x, axis, [(i, i ^ step) for i in range(size)])  66.3 us
    all_to_all x1, waiting for transfers between devices, shards(): lax.all_to_all(packed, 'seq', split_axis=0, concat_axis=0, tiled=True)  61.8 us
    pallas_call x1, Pallas kernels, attention(): pl.pallas_call(attention_kernel, in_specs=[smem, smem, vmem], out_specs=[...  24.7 us
    ppermute x7, starting transfers between devices, exchange_sum(): x = x + lax.ppermute(x, axis, [(i, i ^ step) for i in range(size)])  10.8 us
    all_to_all x1, starting transfers between devices, shards(): lax.all_to_all(packed, 'seq', split_axis=0, concat_axis=0, tiled=True)  8.17 us
    pallas_call x1, Pallas kernels, unpack(): pl.pallas_call(unpack_kernel, grid=(tokens // ROWS,), in_specs=[pl.BlockS...  7.55 us
    pallas_call x1, Pallas kernels, pack(): pl.pallas_call(pack_kernel, grid=(tokens // ROWS,), in_specs=[rows] * 4 +...  7.38 us
    all_to_all x1, starting transfers between devices, shards(): lax.all_to_all(results, 'seq', split_axis=0, concat_axis=0, tiled=True)  6.27 us
  transfers between devices with their start and end apart: 9, of which 8 were waited for; matrix products, arithmetic and copies ran while one was open for 2% of the time, Pallas kernels for 0%

profile of v1, /device:TPU:0, one launch (start us, length us, event | category | flops | bytes accessed | tf_op | source)
XLA Modules:
  0.0 196.7 jit_solution(10808133925554368260)
XLA Ops:
  0.6 0.0 copy-start
  0.6 7.4 %pack.1 = bf16[16,4,2,128,128]{4,3,2,1,0:T(8,128)(2,1)} custom-call(bf16[128,4096]{1,0:T(8,128)(2,1)} %bitcast.18, bf16[128,4096]{1,0:T(8,128)(2,1)} %bitcast.20, bf16[128,4096]{1,0:T(8,128)(2,1)} %bitcast.22, bf16[128,4096]{1,0:T(8,128)(2,1)} %bitcast.23, f32[1,4096]{1,0:T(1,128)} %bitcast.24, f32[1,4096]{1,0:T(1,128)} %bitcast.26), custom_call_target="tpu_custom_call" | custom-call | tf_op jit(solution)/shard_map/pack/pallas_call | solution.py:45
  8.0 0.0 copy-start.4
  8.0 8.2 %all-to-all-start = ((bf16[16,4,2,128,128]{4,3,2,1,0:T(8,128)(2,1)}), bf16[16,4,2,128,128]{4,3,2,1,0:T(8,128)(2,1)}, u32[]{:S(2)}, u32[]{:S(2)}) async-start(bf16[16,4,2,128,128]{4,3,2,1,0:T(8,128)(2,1)} %pack.1), calls=%async_computation | async-start | bytes 8388608 | tf_op jit(solution)/shard_map/all_to_all | solution.py:213
  16.2 0.0 copy-done
  16.2 0.1 dynamic-slice_bitcast_fusion
  16.3 0.8 copy.15.lists_ref
  17.1 0.0 copy-done.4
  17.1 0.6 dynamic-slice_bitcast_fusion.1.live_ref
  17.7 61.8 %all-to-all-done.in_ref = bf16[16,4,2,128,128]{4,3,2,1,0:T(8,128)(2,1)} async-done(((bf16[16,4,2,128,128]{4,3,2,1,0:T(8,128)(2,1)}), bf16[16,4,2,128,128]{4,3,2,1,0:T(8,128)(2,1)}, u32[]{:S(2)}, u32[]{:S(2)}) %all-to-all-start) | async-done | bytes 4194336 | tf_op jit(solution)/shard_map/all_to_all | solution.py:213
  79.5 24.7 %attention.1 = (bf16[16,4,2,128,128]{4,3,2,1,0:T(8,128)(2,1)}, f32[4,128]{1,0:T(4,128)}) custom-call(s32[2,16,4]{2,1,0:T(8,128)} %copy.15.lists_ref, s32[2]{0:T(128)} %dynamic-slice_bitcast_fusion.1.live_ref, bf16[16,4,2,128,128]{4,3,2,1,0:T(8,128)(2,1)} %all-to-all-done.in_ref), custom_call_target="tpu_custom_call" | custom-call | tf_op jit(solution)/shard_map/attention/pallas_call | solution.py:133
  104.2 0.0 copy-start.3
  104.2 0.0 copy-start.2
  104.2 0.0 copy-start.1
  104.2 6.3 %all-to-all-start.1 = ((bf16[16,4,2,128,128]{4,3,2,1,0:T(8,128)(2,1)}), bf16[16,4,2,128,128]{4,3,2,1,0:T(8,128)(2,1)}, u32[]{:S(2)}, u32[]{:S(2)}) async-start(bf16[16,4,2,128,128]{4,3,2,1,0:T(8,128)(2,1)} %get-tuple-element.12), calls=%async_computation.1 | async-start | bytes 8388608 | tf_op jit(solution)/shard_map/all_to_all | solution.py:215
  110.5 0.0 copy-done.3
  110.5 0.1 collective-permute-start
  110.6 1.1 collective-permute-done
  111.8 2.9 %collective-permute-start.1 = (f32[1,512]{1,0:T(1,128)S(1)}, f32[1,512]{1,0:T(1,128)S(1)}, u32[]{:S(2)}, u32[]{:S(2)}) collective-permute-start(f32[1,512]{1,0:T(1,128)S(1)} %add.26), channel_id=1, source_target_pairs={{0,32},{16,48},{32,0},{48,16},{64,96},{80,112},{96,64},{112,80},{1... | collective-permute-start | bytes 6152 | tf_op jit(solution)/shard_map/ppermute | solution.py:198
  114.7 1.6 collective-permute-done.1
  116.2 2.2 %collective-permute-start.2 = (f32[1,512]{1,0:T(1,128)S(1)}, f32[1,512]{1,0:T(1,128)S(1)}, u32[]{:S(2)}, u32[]{:S(2)}) collective-permute-start(f32[1,512]{1,0:T(1,128)S(1)} %add.27), channel_id=1, source_target_pairs={{0,64},{16,80},{32,96},{48,112},{64,0},{80,16},{96,32},{112,48},{1... | collective-permute-start | bytes 6152 | tf_op jit(solution)/shard_map/ppermute | solution.py:198
  118.4 2.9 %collective-permute-done.2 = f32[1,512]{1,0:T(1,128)S(1)} collective-permute-done((f32[1,512]{1,0:T(1,128)S(1)}, f32[1,512]{1,0:T(1,128)S(1)}, u32[]{:S(2)}, u32[]{:S(2)}) %collective-permute-start.2) | collective-permute-done | bytes 2080 | tf_op jit(solution)/shard_map/ppermute | solution.py:198
  121.3 0.1 broadcast_select_fusion
  121.4 1.9 collective-permute-start.3
  123.3 49.6 %collective-permute-done.3 = f32[16,512]{1,0:T(8,128)S(1)} collective-permute-done((f32[16,512]{1,0:T(8,128)S(1)}, f32[16,512]{1,0:T(8,128)S(1)}, u32[]{:S(2)}, u32[]{:S(2)}) %collective-permute-start.3) | collective-permute-done | bytes 32800 | tf_op jit(solution)/shard_map/ppermute | solution.py:198
  172.9 0.1 fusion
  173.0 0.2 collective-permute-start.4
  173.2 5.2 %collective-permute-done.4 = f32[16,512]{1,0:T(8,128)S(1)} collective-permute-done((f32[16,512]{1,0:T(8,128)S(1)}, f32[16,512]{1,0:T(8,128)S(1)}, u32[]{:S(2)}, u32[]{:S(2)}) %collective-permute-start.4) | collective-permute-done | bytes 32800 | tf_op jit(solution)/shard_map/ppermute | solution.py:198
  178.4 0.1 fusion.2
  178.5 0.5 collective-permute-start.5
  179.0 3.5 %collective-permute-done.5 = f32[16,512]{1,0:T(8,128)S(1)} collective-permute-done((f32[16,512]{1,0:T(8,128)S(1)}, f32[16,512]{1,0:T(8,128)S(1)}, u32[]{:S(2)}, u32[]{:S(2)}) %collective-permute-start.5) | collective-permute-done | bytes 32800 | tf_op jit(solution)/shard_map/ppermute | solution.py:198
  182.4 3.0 %collective-permute-start.6 = (f32[16,512]{1,0:T(8,128)S(1)}, f32[16,512]{1,0:T(8,128)S(1)}, u32[]{:S(2)}, u32[]{:S(2)}) collective-permute-start(f32[16,512]{1,0:T(8,128)S(1)} %add.31), channel_id=1, source_target_pairs={{0,8},{1,9},{2,10},{3,11},{4,12},{5,13},{6,14},{7,15},{8,0},{9,1},... | collective-permute-start | bytes 98312 | tf_op jit(solution)/shard_map/ppermute | solution.py:198
  185.5 2.4 %collective-permute-done.6 = f32[16,512]{1,0:T(8,128)S(1)} collective-permute-done((f32[16,512]{1,0:T(8,128)S(1)}, f32[16,512]{1,0:T(8,128)S(1)}, u32[]{:S(2)}, u32[]{:S(2)}) %collective-permute-start.6) | collective-permute-done | bytes 32800 | tf_op jit(solution)/shard_map/ppermute | solution.py:198
  187.9 0.0 copy-done.2
  187.9 0.6 div.7
  188.6 0.0 copy-done.1
  188.6 0.6 div.6
  189.2 0.0 all-to-all-done.1.back_ref
  189.2 7.6 %unpack.1 = (bf16[128,4096]{1,0:T(8,128)(2,1)}, bf16[128,4096]{1,0:T(8,128)(2,1)}, bf16[128,4096]{1,0:T(8,128)(2,1)}, bf16[128,4096]{1,0:T(8,128)(2,1)}) custom-call(bf16[16,4,2,128,128]{4,3,2,1,0:T(8,128)(2,1)} %all-to-all-done.1.back_ref, bf16[128,4096]{1,0:T(8,128)(2,1)} %bitcast.19, bf16[128,4096]{1,0:T(8,128)(2,1)} %bitcast.21, f32[1,4096]{1,0:T(1,128)} %bitcast.25, ...), custom_call_target="tpu_custom_call" | custom-call | tf_op jit(solution)/shard_map/unpack/pallas_call | solution.py:178
  (8 shorter events, 0.1 us)
Async XLA Ops:
  0.6 15.6 %copy-start = (s32[1,32,16,4]{1,3,2,0:T(4,128)S(1)}, s32[1,32,16,4]{1,3,2,0:T(4,128)}, u32[]{:S(2)}) copy-start(s32[1,32,16,4]{1,3,2,0:T(4,128)} %param.14) | copy-start | bytes 24580
  8.0 9.1 %copy-start.4 = (s32[1,32]{1,0:T(1,128)S(1)}, s32[1,32]{1,0:T(1,128)}, u32[]{:S(2)}) copy-start(s32[1,32]{1,0:T(1,128)} %param.15) | copy-start | bytes 388
  8.0 71.5 %all-to-all-start = ((bf16[16,4,2,128,128]{4,3,2,1,0:T(8,128)(2,1)}), bf16[16,4,2,128,128]{4,3,2,1,0:T(8,128)(2,1)}, u32[]{:S(2)}, u32[]{:S(2)}) async-start(bf16[16,4,2,128,128]{4,3,2,1,0:T(8,128)(2,1)} %pack.1), calls=%async_computation | async-start | bytes 8388608 | tf_op jit(solution)/shard_map/all_to_all | solution.py:213
  104.2 6.3 %copy-start.3 = (f32[4,128]{1,0:T(4,128)S(1)}, f32[4,128]{1,0:T(4,128)}, u32[]{:S(2)}) copy-start(f32[4,128]{1,0:T(4,128)} %get-tuple-element.17) | copy-start | bytes 6148
  104.2 83.7 %copy-start.2 = (f32[4096]{0:T(1024)S(1)}, f32[4096]{0:T(1024)}, u32[]{:S(2)}) copy-start(f32[4096]{0:T(1024)} %param.13) | copy-start | bytes 49156
  104.2 84.3 %copy-start.1 = (f32[4096]{0:T(1024)S(1)}, f32[4096]{0:T(1024)}, u32[]{:S(2)}) copy-start(f32[4096]{0:T(1024)} %param.12) | copy-start | bytes 49156
  104.2 84.9 %all-to-all-start.1 = ((bf16[16,4,2,128,128]{4,3,2,1,0:T(8,128)(2,1)}), bf16[16,4,2,128,128]{4,3,2,1,0:T(8,128)(2,1)}, u32[]{:S(2)}, u32[]{:S(2)}) async-start(bf16[16,4,2,128,128]{4,3,2,1,0:T(8,128)(2,1)} %get-tuple-element.12), calls=%async_computation.1 | async-start | bytes 8388608 | tf_op jit(solution)/shard_map/all_to_all | solution.py:215
  110.5 1.2 collective-permute-start
  111.8 4.5 %collective-permute-start.1 = (f32[1,512]{1,0:T(1,128)S(1)}, f32[1,512]{1,0:T(1,128)S(1)}, u32[]{:S(2)}, u32[]{:S(2)}) collective-permute-start(f32[1,512]{1,0:T(1,128)S(1)} %add.26), channel_id=1, source_target_pairs={{0,32},{16,48},{32,0},{48,16},{64,96},{80,112},{96,64},{112,80},{1... | collective-permute-start | bytes 6152 | tf_op jit(solution)/shard_map/ppermute | solution.py:198
  116.2 5.1 %collective-permute-start.2 = (f32[1,512]{1,0:T(1,128)S(1)}, f32[1,512]{1,0:T(1,128)S(1)}, u32[]{:S(2)}, u32[]{:S(2)}) collective-permute-start(f32[1,512]{1,0:T(1,128)S(1)} %add.27), channel_id=1, source_target_pairs={{0,64},{16,80},{32,96},{48,112},{64,0},{80,16},{96,32},{112,48},{1... | collective-permute-start | bytes 6152 | tf_op jit(solution)/shard_map/ppermute | solution.py:198
  121.4 51.5 %collective-permute-start.3 = (f32[16,512]{1,0:T(8,128)S(1)}, f32[16,512]{1,0:T(8,128)S(1)}, u32[]{:S(2)}, u32[]{:S(2)}) collective-permute-start(f32[16,512]{1,0:T(8,128)S(1)} %broadcast_select_fusion), channel_id=1, source_target_pairs={{0,1},{1,0},{2,3},{3,2},{4,5},{5,4},{6,7},{7,6},{8,9},{9,8},{10,11... | collective-permute-start | bytes 98312 | tf_op jit(solution)/shard_map/ppermute | solution.py:198
  173.0 5.4 %collective-permute-start.4 = (f32[16,512]{1,0:T(8,128)S(1)}, f32[16,512]{1,0:T(8,128)S(1)}, u32[]{:S(2)}, u32[]{:S(2)}) collective-permute-start(f32[16,512]{1,0:T(8,128)S(1)} %fusion), channel_id=1, source_target_pairs={{0,2},{1,3},{2,0},{3,1},{4,6},{5,7},{6,4},{7,5},{8,10},{9,11},{10,... | collective-permute-start | bytes 98312 | tf_op jit(solution)/shard_map/ppermute | solution.py:198
  178.5 3.9 %collective-permute-start.5 = (f32[16,512]{1,0:T(8,128)S(1)}, f32[16,512]{1,0:T(8,128)S(1)}, u32[]{:S(2)}, u32[]{:S(2)}) collective-permute-start(f32[16,512]{1,0:T(8,128)S(1)} %fusion.2), channel_id=1, source_target_pairs={{0,4},{1,5},{2,6},{3,7},{4,0},{5,1},{6,2},{7,3},{8,12},{9,13},{10,... | collective-permute-start | bytes 98312 | tf_op jit(solution)/shard_map/ppermute | solution.py:198
  182.4 5.4 %collective-permute-start.6 = (f32[16,512]{1,0:T(8,128)S(1)}, f32[16,512]{1,0:T(8,128)S(1)}, u32[]{:S(2)}, u32[]{:S(2)}) collective-permute-start(f32[16,512]{1,0:T(8,128)S(1)} %add.31), channel_id=1, source_target_pairs={{0,8},{1,9},{2,10},{3,11},{4,12},{5,13},{6,14},{7,15},{8,0},{9,1},... | collective-permute-start | bytes 98312 | tf_op jit(solution)/shard_map/ppermute | solution.py:198

commit v2 on v1

v2 whole, which is shorter than its diff:
```python
import jax
import jax.numpy as jnp
from jax import lax
from jax.experimental import pallas as pl
from jax.experimental.pallas import tpu as pltpu
from jax.sharding import PartitionSpec as P

BLK = 128
EPSILON = 1e-06
ROWS = 16
CHUNKS = 4
PARTS = 3
SPARE = 8
QUERY, COTANGENT, KEY, VALUE = range(4)
GRAD_Q, OUT, GRAD_K, GRAD_V = range(4)
LOG2E = 1.4426950408889634


def contract(a, b, dims):
    return lax.dot_general(a, b, (dims, ((), ())), preferred_element_type=jnp.float32)


def inverse_rms(x):
    return lax.rsqrt(jnp.mean(x * x, axis=-1, keepdims=True) + EPSILON)


def pack_kernel(
    q_hbm, k_hbm, v_hbm, u_hbm, qg_hbm, kg_hbm, out_ref, raw_ref, gain_ref, raw_sems, gain_sems, copy_sems
):
    groups, span, both = out_ref.shape
    width = both // 2
    tokens = raw_ref.shape[1]
    heads = span // (2 * tokens)
    step = tokens // CHUNKS

    loads = [
        [
            pltpu.make_async_copy(
                hbm.at[pl.ds(c * step, step)],
                raw_ref.at[n, pl.ds(c * step, step)],
                raw_sems.at[n, c],
            )
            for c in range(CHUNKS)
        ]
        for n, hbm in enumerate((q_hbm, k_hbm))
    ]
    gain_loads = [
        pltpu.make_async_copy(hbm, gain_ref.at[n], gain_sems.at[n])
        for n, hbm in enumerate((qg_hbm, kg_hbm))
    ]
    for n in range(2):
        gain_loads[n].start()
        loads[n][0].start()
    for c in range(1, CHUNKS):
        for n in range(2):
            loads[n][c].start()
    moves = []
    for group in range(groups):
        for head in range(heads):
            at = (group * heads + head) * width
            for n, (hbm, pair) in enumerate(((u_hbm, 0), (v_hbm, 1))):
                first = (pair * heads + head) * tokens
                moves.append(
                    pltpu.make_async_copy(
                        hbm.at[:, pl.ds(at, width)],
                        out_ref.at[group, pl.ds(first, tokens), pl.ds(width, width)],
                        copy_sems.at[group * heads + head, n],
                    )
                )
    for move in moves:
        move.start()
    for c in range(CHUNKS):
        for n in range(2):
            if c == 0:
                gain_loads[n].wait()
            loads[n][c].wait()

            def some_rows(i, carry):
                row = pl.multiple_of(c * step + i * ROWS, ROWS)
                x = raw_ref[n, pl.ds(row, ROWS)].astype(jnp.float32)
                y = (x * inverse_rms(x) * gain_ref[n]).astype(jnp.bfloat16)
                for group in range(groups):
                    for head in range(heads):
                        at = (group * heads + head) * width
                        first = (n * heads + head) * tokens
                        out_ref[group, pl.ds(first + row, ROWS), :width] = y[:, at : at + width]
                return carry

            lax.fori_loop(0, step // ROWS, some_rows, 0)
    for move in moves:
        move.wait()


def in_hbm(x):
    return pltpu.with_memory_space_constraint(x, pltpu.HBM)


def pack(q, k, v, u, q_gain, k_gain, groups, heads):
    tokens, features = q.shape
    width = features // (groups * heads)
    hbm = pl.BlockSpec(memory_space=pltpu.HBM)
    vmem = pl.BlockSpec(memory_space=pltpu.VMEM)
    return pl.pallas_call(
        pack_kernel,
        in_specs=[hbm] * 6,
        out_specs=vmem,
        out_shape=jax.ShapeDtypeStruct((groups, 2 * heads * tokens, 2 * width), jnp.bfloat16),
        scratch_shapes=[
            pltpu.VMEM((2, tokens, features), jnp.bfloat16),
            pltpu.VMEM((2, 1, features), jnp.float32),
            pltpu.SemaphoreType.DMA((2, CHUNKS)),
            pltpu.SemaphoreType.DMA((2,)),
            pltpu.SemaphoreType.DMA((groups * heads, 2)),
        ],
        compiler_params=pltpu.CompilerParams(vmem_limit_bytes=12 << 20),
        name="pack",
    )(*(in_hbm(x) for x in (q, k, v, u, q_gain[None], k_gain[None])))


def attention_kernel(first_ref, lists_ref, live_ref, in_ref, out_ref, *scratch):
    blocks, span, both = in_ref.shape
    heads = len(scratch) // 2
    width = both // 2
    scale = width ** (-0.5)
    turned, sums, gains_ref = scratch[:heads], scratch[heads:-1], scratch[-1]
    first_head = first_ref[0]
    live = [live_ref[0, first_head + head] for head in range(heads)]

    def place(pair, head):
        return pl.ds((pair * heads + head) * BLK, BLK)

    def parts(row):
        pieces = []
        for _ in range(PARTS):
            pieces.append(row.astype(jnp.bfloat16))
            row = row - pieces[-1].astype(jnp.float32)
        return pieces

    def prepare(j, carry):
        for head in range(heads):
            turned[head][j] = in_ref[j, place(1, head)].T
            sums[head][j] = jnp.zeros((BLK, both), jnp.float32)
        return carry

    lax.fori_loop(0, blocks, prepare, 0)

    def start(b, head, slots):
        q = in_ref[b, place(0, head), :width]
        u = in_ref[b, place(0, head), width:]
        diagonal = (q, u)
        chosen = [lists_ref[b, s, first_head + head] for s in range(slots)]
        rows = jnp.concatenate([in_ref[j, place(1, head)] for j in chosen], axis=0)
        scores = contract(rows[:, :width], q, ((1,), (1,)))
        grads = contract(rows[:, width:], u, ((1,), (1,)))
        products = ([scores[s * BLK : (s + 1) * BLK] for s in range(slots)], [grads[s * BLK : (s + 1) * BLK] for s in range(slots)])
        return q, diagonal, chosen, products

    def softmax(head, products):
        scores, grads = products
        factor = scale * LOG2E
        bias = [jnp.where(s < live[head], 0.0, -jnp.inf) for s in range(len(scores))]
        tops = [jnp.max(s, axis=0, keepdims=True) * factor + x for s, x in zip(scores, bias)]
        top = tops[0]
        for t in tops[1:]:
            top = jnp.maximum(top, t)
        raised = [jnp.exp2(s * factor + (x - top)) for s, x in zip(scores, bias)]
        total = raised[0]
        inner = raised[0] * grads[0]
        for e, g in zip(raised[1:], grads[1:]):
            total = total + e
            inner = inner + e * g
        inverse = 1.0 / jnp.sum(total, axis=0, keepdims=True)
        delta = jnp.sum(inner, axis=0, keepdims=True) * inverse
        probs = [e * inverse for e in raised]
        low = [p.astype(jnp.bfloat16) for p in probs]
        ds = [(p * ((g - delta) * scale)).astype(jnp.bfloat16) for p, g in zip(probs, grads)]
        return low, ds

    def finish_block(b, head, q, diagonal, chosen, low, ds):
        keys = jnp.concatenate([turned[head][j, :width] for j in chosen], axis=1)
        values = jnp.concatenate([turned[head][j, width:] for j in chosen], axis=1)
        out_t = contract(values, jnp.concatenate(low, axis=0), ((1,), (0,)))
        dq_t = contract(keys, jnp.concatenate(ds, axis=0), ((1,), (0,)))
        q, u = diagonal
        more_k = contract(jnp.concatenate(ds, axis=0), q, ((1,), (0,)))
        more_v = contract(jnp.concatenate(low, axis=0), u, ((1,), (0,)))
        old = [sums[head][j] for j in chosen]
        for s, (j, o) in enumerate(zip(chosen, old)):
            sums[head][j, :, :width] = o[:, :width] + more_k[s * BLK : (s + 1) * BLK]
            sums[head][j, :, width:] = o[:, width:] + more_v[s * BLK : (s + 1) * BLK]
        dq = dq_t.T.astype(jnp.bfloat16)
        out_ref[b, place(0, head), :width] = dq
        out_ref[b, place(0, head), width:] = out_t.T.astype(jnp.bfloat16)
        return jnp.sum(dq.astype(jnp.float32) * q.astype(jnp.float32), axis=0, keepdims=True)

    most = live[0]
    for head in range(1, heads):
        most = jnp.maximum(most, live[head])
    for slots in (2, 3, 4):

        @pl.when(most == slots)
        def _():
            def step(b, gain):
                begun = [start(b, h, slots) for h in range(heads)]
                done = []
                for h, (q, diagonal, chosen, products) in enumerate(begun):
                    low, ds = softmax(h, products)
                    done.append(gain[h] + finish_block(b, h, q, diagonal, chosen, low, ds))
                return tuple(done)

            gain = lax.fori_loop(
                0, blocks, step, (jnp.zeros((1, width), jnp.float32),) * heads
            )
            for h in range(heads):
                gains_ref[h : h + 1] = gain[h]

    def finish(j, gain):
        totals = []
        for head in range(heads):
            grads = sums[head][j].astype(jnp.bfloat16)
            out_ref[j, place(1, head)] = grads
            k = in_ref[j, place(1, head), :width].astype(jnp.float32)
            dk = grads[:, :width].astype(jnp.float32)
            totals.append(gain[head] + jnp.sum(dk * k, axis=0, keepdims=True))
        return tuple(totals)

    gain = lax.fori_loop(0, blocks, finish, (jnp.zeros((1, width), jnp.float32),) * heads)
    for h in range(heads):
        gains_ref[heads + h : heads + h + 1] = gain[h]
    extra = []
    for piece in parts(gains_ref[...]):
        for n in range(2):
            rows = [piece[n * heads + h : n * heads + h + 1] for h in range(heads)]
            extra.append(jnp.concatenate(rows, axis=1))
    extra.append(jnp.zeros((SPARE - 2 * PARTS, both), jnp.bfloat16))
    extra = jnp.concatenate(extra, axis=0)

    def spread(j, carry):
        out_ref[j, span:] = extra
        return carry

    lax.fori_loop(0, blocks, spread, 0)


def attention(first, lists, live, arrived, heads):
    blocks, span, both = arrived.shape
    vmem = pl.BlockSpec(memory_space=pltpu.VMEM)
    smem = pl.BlockSpec(memory_space=pltpu.SMEM)
    return pl.pallas_call(
        attention_kernel,
        in_specs=[smem, smem, smem, vmem],
        out_specs=vmem,
        out_shape=jax.ShapeDtypeStruct((blocks, span + SPARE, both), jnp.bfloat16),
        scratch_shapes=[pltpu.VMEM((blocks, both, BLK), jnp.bfloat16)] * heads
        + [pltpu.VMEM((blocks, BLK, both), jnp.float32)] * heads
        + [pltpu.VMEM((2 * heads, both // 2), jnp.float32)],
        compiler_params=pltpu.CompilerParams(vmem_limit_bytes=24 << 20),
        name="attention",
    )(first, lists, live, arrived)


def unpack_kernel(
    back_ref, q_ref, k_ref, qg_ref, kg_ref, out_hbm, dq_hbm, dk_hbm, dv_hbm, done_ref, sems, copy_sems
):
    groups, _, both = back_ref.shape
    width = both // 2
    tokens, features = q_ref.shape
    heads = features // (groups * width)
    step = tokens // CHUNKS
    moves = []
    for group in range(groups):
        for head in range(heads):
            at = (group * heads + head) * width
            for n, hbm in enumerate((out_hbm, dv_hbm)):
                first = (n * heads + head) * tokens
                moves.append(
                    pltpu.make_async_copy(
                        back_ref.at[group, pl.ds(first, tokens), pl.ds(width, width)],
                        hbm.at[:, pl.ds(at, width)],
                        copy_sems.at[group * heads + head, n],
                    )
                )
    for move in moves:
        move.start()
    for c in range(CHUNKS):
        for n, (raw_ref, gain_ref, hbm) in enumerate(
            ((q_ref, qg_ref, dq_hbm), (k_ref, kg_ref, dk_hbm))
        ):

            def some_rows(i, carry):
                row = pl.multiple_of(c * step + i * ROWS, ROWS)
                x = raw_ref[pl.ds(row, ROWS)].astype(jnp.float32)
                inverse = inverse_rms(x)
                unit = x * inverse
                grads = jnp.concatenate(
                    [
                        back_ref[g, pl.ds((n * heads + h) * tokens + row, ROWS), :width]
                        for g in range(groups)
                        for h in range(heads)
                    ],
                    axis=-1,
                )
                g = grads.astype(jnp.float32) * gain_ref[...]
                mean = jnp.mean(g * unit, axis=-1, keepdims=True)
                done_ref[n, pl.ds(row, ROWS)] = (inverse * (g - unit * mean)).astype(jnp.bfloat16)
                return carry

            lax.fori_loop(0, step // ROWS, some_rows, 0)
            move = pltpu.make_async_copy(
                done_ref.at[n, pl.ds(c * step, step)], hbm.at[pl.ds(c * step, step)], sems.at[n, c]
            )
            move.start()
            moves.append(move)
    for move in moves:
        move.wait()


def unpack(back, q, k, q_gain, k_gain):
    groups, _, both = back.shape
    tokens, features = q.shape
    hbm = pl.BlockSpec(memory_space=pltpu.HBM)
    vmem = pl.BlockSpec(memory_space=pltpu.VMEM)
    return pl.pallas_call(
        unpack_kernel,
        in_specs=[vmem] * 5,
        out_specs=[hbm] * 4,
        out_shape=[jax.ShapeDtypeStruct((tokens, features), jnp.bfloat16)] * 4,
        scratch_shapes=[
            pltpu.VMEM((2, tokens, features), jnp.bfloat16),
            pltpu.SemaphoreType.DMA((2, CHUNKS)),
            pltpu.SemaphoreType.DMA((2 * features // both, 2)),
        ],
        compiler_params=pltpu.CompilerParams(vmem_limit_bytes=12 << 20),
        name="unpack",
    )(back, q, k, q_gain[None], k_gain[None])


def gains_kernel(back_ref, out_ref):
    groups, rows, both = back_ref.shape
    span = rows - SPARE
    for group in range(groups):
        extra = back_ref[group, span:].astype(jnp.float32)
        total = extra[0:2]
        for n in range(1, PARTS):
            total = total + extra[2 * n : 2 * n + 2]
        out_ref[:, group * both : (group + 1) * both] = total


def add_kernel(a_ref, b_ref, out_ref):
    out_ref[...] = a_ref[...] + b_ref[...]


def last_kernel(a_ref, b_ref, qg_ref, kg_ref, q_ref, k_ref):
    total = a_ref[...] + b_ref[...]
    q_ref[...] = total[0:1] / qg_ref[...]
    k_ref[...] = total[1:2] / kg_ref[...]


def small_call(kernel, shapes, name, *args):
    return pl.pallas_call(
        kernel,
        in_specs=[pl.BlockSpec(memory_space=pltpu.VMEM)] * len(args),
        out_specs=[pl.BlockSpec(memory_space=pltpu.VMEM)] * len(shapes),
        out_shape=[jax.ShapeDtypeStruct(shape, jnp.float32) for shape in shapes],
        compiler_params=pltpu.CompilerParams(vmem_limit_bytes=2 << 20),
        name=name,
    )(*args)


def clip_gains(back, q_gain, k_gain):
    features = q_gain.shape[0]
    (total,) = small_call(gains_kernel, [(2, features)], "gains", back)
    size = lax.axis_size("clip")
    flips = [1, 2, 6]
    for n, flip in enumerate(flips):
        other = lax.ppermute(total, "clip", [(i, i ^ flip) for i in range(size)])
        if n < len(flips) - 1:
            (total,) = small_call(add_kernel, [(2, features)], "add", total, other)
    q, k = small_call(
        last_kernel, [(1, features)] * 2, "last", total, other, q_gain[None], k_gain[None]
    )
    return q[0], k[0]


def shards(query_raw, key_raw, value, upstream, query_gain, key_gain, key_blocks, live):
    groups = lax.axis_size("seq")
    heads = key_blocks.shape[1] // groups
    first = (lax.axis_index("seq") * heads).reshape(1)
    lists = jnp.transpose(key_blocks[0], (1, 2, 0))
    packed = pack(
        query_raw[0], key_raw[0], value[0], upstream[0], query_gain, key_gain, groups, heads
    )
    packed, first = lax.optimization_barrier((packed, first))
    arrived = lax.all_to_all(packed, "seq", split_axis=0, concat_axis=0, tiled=True)
    results = attention(first, lists, live, arrived, heads)
    back = lax.all_to_all(results, "seq", split_axis=0, concat_axis=0, tiled=True)
    attended, grad_query, grad_key, grad_value = unpack(
        back, query_raw[0], key_raw[0], query_gain, key_gain
    )
    q_total, k_total = clip_gains(back, query_gain, key_gain)
    return (
        attended[None],
        grad_query[None],
        grad_key[None],
        grad_value[None],
        q_total,
        k_total,
    )


def solution(mesh):
    tokens = P("clip", "seq", None)
    return jax.shard_map(
        shards,
        mesh=mesh,
        in_specs=(tokens,) * 4 + (P(), P(), P("clip", None, None, None), P("clip", None)),
        out_specs=(tokens,) * 4 + (P(), P()),
        check_vma=False,
    )
```

time: 200 us -> 149 us (0.74); the launches traced: 197 us -> 149 us
  waiting for transfers between devices: 128 us -> 3.09 us
  blocking collectives: 0 us -> 114 us
  starting transfers between devices: 25.2 us -> 4.24 us
  Pallas kernels: 39.7 us -> 26.8 us
    all_to_all x0 -> x2, blocking collectives: none -> 114 us  [the longest x1 58.6 us: shards(): lax.all_to_all(packed, 'seq', split_axis=0, concat_axis=0, tiled=True)]
    ppermute x7 -> x3, waiting for transfers between devices: 66.3 us -> 3.09 us  [clip_gains(): other = lax.ppermute(total, 'clip', [(i, i ^ flip) for i in range(size)])]
    all_to_all x2 -> x0, waiting for transfers between devices: 61.8 us -> none  [the longest x1 61.8 us: shards(): lax.all_to_all(packed, 'seq', split_axis=0, concat_axis=0, tiled=True)]
    all_to_all x2 -> x0, starting transfers between devices: 14.4 us -> none  [the longest x1 8.17 us: shards(): lax.all_to_all(packed, 'seq', split_axis=0, concat_axis=0, tiled=True)]
    pallas_call x3 -> x7, Pallas kernels: 39.7 us -> 26.8 us  [the longest x1 15.3 us: attention(): pl.pallas_call(attention_kernel, in_specs=[smem, smem, smem, vmem], out_s...]
    ppermute x7 -> x3, starting transfers between devices: 10.8 us -> 4.24 us  [clip_gains(): other = lax.ppermute(total, 'clip', [(i, i ^ flip) for i in range(size)])]
  transfers between devices with their start and end apart: 9 -> 3, of which waited for: 8 -> 2; matrix products, arithmetic and copies ran while one was open for 2% -> 0% of each run, Pallas kernels for 0% -> 4%
where the time goes in v2:
time: 149 us
  blocking collectives  114 us (77%)
  Pallas kernels  26.8 us (18%)
  starting transfers between devices  4.24 us (3%)
  waiting for transfers between devices  3.09 us (2%)
    all_to_all x1, blocking collectives, shards(): lax.all_to_all(packed, 'seq', split_axis=0, concat_axis=0, tiled=True)  58.6 us
    all_to_all x1, blocking collectives, shards(): lax.all_to_all(results, 'seq', split_axis=0, concat_axis=0, tiled=True)  55.7 us
    pallas_call x1, Pallas kernels, attention(): pl.pallas_call(attention_kernel, in_specs=[smem, smem, smem, vmem], out_s...  15.3 us
    pallas_call x1, Pallas kernels, unpack(): pl.pallas_call(unpack_kernel, in_specs=[vmem] * 5, out_specs=[hbm] * 4, o...  5.71 us
    pallas_call x1, Pallas kernels, pack(): pl.pallas_call(pack_kernel, in_specs=[hbm] * 6, out_specs=vmem, out_shape...  5.14 us
    ppermute x3, starting transfers between devices, clip_gains(): other = lax.ppermute(total, 'clip', [(i, i ^ flip) for i in range(size)])  4.24 us
    ppermute x3, waiting for transfers between devices, clip_gains(): other = lax.ppermute(total, 'clip', [(i, i ^ flip) for i in range(size)])  3.09 us
  transfers between devices with their start and end apart: 3, of which 2 were waited for; matrix products, arithmetic and copies ran while one was open for 0% of the time, Pallas kernels for 4%

profile of v2, /device:TPU:0, one launch (start us, length us, event | category | flops | bytes accessed | tf_op | source)
XLA Modules:
  0.0 149.2 jit_solution(13416046481193151405)
XLA Ops:
  0.6 5.1 %pack.1 = bf16[16,512,256]{2,1,0:T(8,128)(2,1)S(1)} custom-call(bf16[128,4096]{1,0:T(8,128)(2,1)} %bitcast.16, bf16[128,4096]{1,0:T(8,128)(2,1)} %bitcast.18, bf16[128,4096]{1,0:T(8,128)(2,1)} %bitcast.27, bf16[128,4096]{1,0:T(8,128)(2,1)} %bitcast.28, f32[1,4096]{1,0:T(1,128)} %bitcast.20, f32[1,4096]{1,0:T(1,128)} %bitcast.23), custom_call_target="tpu_custom_call" | custom-call | tf_op jit(solution)/shard_map/pack/pallas_call | solution.py:103
  5.8 0.0 copy-start.4
  5.8 0.0 copy-start.5
  5.8 58.6 %all_to_all.10.in_ref = bf16[16,512,256]{2,1,0:T(8,128)(2,1)S(1)} all-to-all(bf16[16,512,256]{2,1,0:T(8,128)(2,1)S(1)} %pack.1), channel_id=1, replica_groups=mesh['clip'=8,'seq'=16] {'seq'}, dimensions={0} | all-to-all | bytes 8388608 | tf_op jit(solution)/shard_map/all_to_all | solution.py:394
  64.5 0.0 copy-done.4
  64.5 0.0 copy-done.5
  64.5 15.3 %attention.1 = bf16[16,520,256]{2,1,0:T(8,128)(2,1)S(1)} custom-call(s32[1]{0:T(128)} %bitcast.6.first_ref, s32[16,4,32]{2,1,0:T(4,128)S(1)} %bitcast.26, s32[1,32]{1,0:T(1,128)S(1)} %copy-done.5, bf16[16,512,256]{2,1,0:T(8,128)(2,1)S(1)} %all_to_all.10.in_ref), custom_call_target="tpu_custom_call" | custom-call | tf_op jit(solution)/shard_map/attention/pallas_call | solution.py:249
  79.7 55.7 %all_to_all.11.back_ref = bf16[16,520,256]{2,1,0:T(8,128)(2,1)S(1)} all-to-all(bf16[16,520,256]{2,1,0:T(8,128)(2,1)S(1)} %attention.1), channel_id=1, replica_groups=mesh['clip'=8,'seq'=16] {'seq'}, dimensions={0} | all-to-all | bytes 8519680 | tf_op jit(solution)/shard_map/all_to_all | solution.py:396
  135.4 0.0 copy-start
  135.4 0.0 copy-start.1
  135.4 0.0 copy-start.2
  135.4 0.0 copy-start.3
  135.4 0.1 collective-permute-start
  135.5 1.2 collective-permute-done.b_ref
  136.7 2.0 %collective-permute-start.1 = (f32[2,4096]{1,0:T(2,128)S(1)}, f32[2,4096]{1,0:T(2,128)S(1)}, u32[]{:S(2)}, u32[]{:S(2)}) collective-permute-start(f32[2,4096]{1,0:T(2,128)S(1)} %add.2.a_ref), channel_id=1, source_target_pairs={{0,32},{16,48},{32,0},{48,16},{64,96},{80,112},{96,64},{112,80},{1... | collective-permute-start | bytes 98312 | tf_op jit(solution)/shard_map/ppermute | solution.py:376
  138.8 1.9 %collective-permute-done.1.b_ref = f32[2,4096]{1,0:T(2,128)S(1)} collective-permute-done((f32[2,4096]{1,0:T(2,128)S(1)}, f32[2,4096]{1,0:T(2,128)S(1)}, u32[]{:S(2)}, u32[]{:S(2)}) %collective-permute-start.1) | collective-permute-done | bytes 32800 | tf_op jit(solution)/shard_map/ppermute | solution.py:376
  140.7 2.1 %collective-permute-start.2 = (f32[2,4096]{1,0:T(2,128)S(1)}, f32[2,4096]{1,0:T(2,128)S(1)}, u32[]{:S(2)}, u32[]{:S(2)}) collective-permute-start(f32[2,4096]{1,0:T(2,128)S(1)} %add.3.a_ref), channel_id=1, source_target_pairs={{0,96},{16,112},{32,64},{48,80},{64,32},{80,48},{96,0},{112,16},{1... | collective-permute-start | bytes 98312 | tf_op jit(solution)/shard_map/ppermute | solution.py:376
  142.8 0.0 copy-done
  142.8 0.0 copy-done.1
  142.8 0.0 copy-done.2
  142.8 0.0 copy-done.3
  142.8 5.7 %unpack.1 = (bf16[128,4096]{1,0:T(8,128)(2,1)}, bf16[128,4096]{1,0:T(8,128)(2,1)}, bf16[128,4096]{1,0:T(8,128)(2,1)}, bf16[128,4096]{1,0:T(8,128)(2,1)}) custom-call(bf16[16,520,256]{2,1,0:T(8,128)(2,1)S(1)} %all_to_all.11.back_ref, bf16[128,4096]{1,0:T(8,128)(2,1)S(1)} %bitcast.17, bf16[128,4096]{1,0:T(8,128)(2,1)S(1)} %bitcast.19, f32[1,4096]{1,0:T(1,128)S(1)} %bitcast.21, ...), custom_call_target="tpu_custom_call" | custom-call | tf_op jit(solution)/shard_map/unpack/pallas_call | solution.py:323
  148.5 0.0 collective-permute-done.2.b_ref
  148.5 0.6 last.1
  (3 shorter events, 0.0 us)
Async XLA Ops:
  5.8 58.7 %copy-start.4 = (s32[1,32,16,4]{1,3,2,0:T(4,128)S(1)}, s32[1,32,16,4]{1,3,2,0:T(4,128)}, u32[]{:S(2)}) copy-start(s32[1,32,16,4]{1,3,2,0:T(4,128)} %param.14) | copy-start | bytes 24580
  5.8 58.7 %copy-start.5 = (s32[1,32]{1,0:T(1,128)S(1)}, s32[1,32]{1,0:T(1,128)}, u32[]{:S(2)}) copy-start(s32[1,32]{1,0:T(1,128)} %live_ref.1) | copy-start | bytes 388
  135.4 7.4 %copy-start = (bf16[1,128,4096]{2,1,0:T(8,128)(2,1)S(1)}, bf16[1,128,4096]{2,1,0:T(8,128)(2,1)}, u32[]{:S(2)}) copy-start(bf16[1,128,4096]{2,1,0:T(8,128)(2,1)} %param.8) | copy-start | bytes 3145732
  135.4 7.4 %copy-start.1 = (bf16[1,128,4096]{2,1,0:T(8,128)(2,1)S(1)}, bf16[1,128,4096]{2,1,0:T(8,128)(2,1)}, u32[]{:S(2)}) copy-start(bf16[1,128,4096]{2,1,0:T(8,128)(2,1)} %param.9) | copy-start | bytes 3145732
  135.4 7.4 %copy-start.2 = (f32[4096]{0:T(1024)S(1)}, f32[4096]{0:T(1024)}, u32[]{:S(2)}) copy-start(f32[4096]{0:T(1024)} %param.12) | copy-start | bytes 49156
  135.4 7.4 %copy-start.3 = (f32[4096]{0:T(1024)S(1)}, f32[4096]{0:T(1024)}, u32[]{:S(2)}) copy-start(f32[4096]{0:T(1024)} %param.13) | copy-start | bytes 49156
  135.4 1.3 collective-permute-start
  136.7 3.9 %collective-permute-start.1 = (f32[2,4096]{1,0:T(2,128)S(1)}, f32[2,4096]{1,0:T(2,128)S(1)}, u32[]{:S(2)}, u32[]{:S(2)}) collective-permute-start(f32[2,4096]{1,0:T(2,128)S(1)} %add.2.a_ref), channel_id=1, source_target_pairs={{0,32},{16,48},{32,0},{48,16},{64,96},{80,112},{96,64},{112,80},{1... | collective-permute-start | bytes 98312 | tf_op jit(solution)/shard_map/ppermute | solution.py:376
  140.7 7.9 %collective-permute-start.2 = (f32[2,4096]{1,0:T(2,128)S(1)}, f32[2,4096]{1,0:T(2,128)S(1)}, u32[]{:S(2)}, u32[]{:S(2)}) collective-permute-start(f32[2,4096]{1,0:T(2,128)S(1)} %add.3.a_ref), channel_id=1, source_target_pairs={{0,96},{16,112},{32,64},{48,80},{64,32},{80,48},{96,0},{112,16},{1... | collective-permute-start | bytes 98312 | tf_op jit(solution)/shard_map/ppermute | solution.py:376

commit v3 on v2

--- a/solution.py
+++ b/solution.py
@@ -119,10 +119,10 @@
 
 def attention_kernel(first_ref, lists_ref, live_ref, in_ref, out_ref, *scratch):
     blocks, span, both = in_ref.shape
-    heads = len(scratch) // 2
+    heads = len(scratch) // 3
     width = both // 2
     scale = width ** (-0.5)
-    turned, sums, gains_ref = scratch[:heads], scratch[heads:-1], scratch[-1]
+    turned, sums, ahead, gains_ref = scratch[:heads], scratch[heads : 2 * heads], scratch[2 * heads : -1], scratch[-1]
     first_head = first_ref[0]
     live = [live_ref[0, first_head + head] for head in range(heads)]
 
@@ -200,13 +200,26 @@
 
         @pl.when(most == slots)
         def _():
+            def keep(h, products):
+                for s in range(slots):
+                    for n in range(2):
+                        ahead[h][n, s] = products[n][s]
+
             def step(b, gain):
-                begun = [start(b, h, slots) for h in range(heads)]
                 done = []
-                for h, (q, diagonal, chosen, products) in enumerate(begun):
+                for h in range(heads):
+                    products = [[ahead[h][n, s] for s in range(slots)] for n in range(2)]
+                    after = h + 1 if h + 1 < heads else 0
+                    at = b if h + 1 < heads else jnp.minimum(b + 1, blocks - 1)
+                    keep(after, start(at, after, slots)[3])
                     low, ds = softmax(h, products)
-                    done.append(gain[h] + finish_block(b, h, q, diagonal, chosen, low, ds))
+                    q = in_ref[b, place(0, h), :width]
+                    u = in_ref[b, place(0, h), width:]
+                    chosen = [lists_ref[b, s, first_head + h] for s in range(slots)]
+                    done.append(gain[h] + finish_block(b, h, q, (q, u), chosen, low, ds))
                 return tuple(done)
+
+            keep(0, start(0, 0, slots)[3])
 
             gain = lax.fori_loop(
                 0, blocks, step, (jnp.zeros((1, width), jnp.float32),) * heads
@@ -214,32 +227,17 @@
             for h in range(heads):
                 gains_ref[h : h + 1] = gain[h]
 
-    def finish(j, gain):
-        totals = []
+    extra = parts(jnp.concatenate([gains_ref[h : h + 1] for h in range(heads)], axis=1))
+    extra.append(jnp.zeros((SPARE - PARTS, both), jnp.bfloat16))
+    extra = jnp.concatenate(extra, axis=0)
+
+    def finish(j, carry):
         for head in range(heads):
-            grads = sums[head][j].astype(jnp.bfloat16)
-            out_ref[j, place(1, head)] = grads
-            k = in_ref[j, place(1, head), :width].astype(jnp.float32)
-            dk = grads[:, :width].astype(jnp.float32)
-            totals.append(gain[head] + jnp.sum(dk * k, axis=0, keepdims=True))
-        return tuple(totals)
-
-    gain = lax.fori_loop(0, blocks, finish, (jnp.zeros((1, width), jnp.float32),) * heads)
-    for h in range(heads):
-        gains_ref[heads + h : heads + h + 1] = gain[h]
-    extra = []
-    for piece in parts(gains_ref[...]):
-        for n in range(2):
-            rows = [piece[n * heads + h : n * heads + h + 1] for h in range(heads)]
-            extra.append(jnp.concatenate(rows, axis=1))
-    extra.append(jnp.zeros((SPARE - 2 * PARTS, both), jnp.bfloat16))
-    extra = jnp.concatenate(extra, axis=0)
-
-    def spread(j, carry):
+            out_ref[j, place(1, head)] = sums[head][j].astype(jnp.bfloat16)
         out_ref[j, span:] = extra
         return carry
 
-    lax.fori_loop(0, blocks, spread, 0)
+    lax.fori_loop(0, blocks, finish, 0)
 
 
 def attention(first, lists, live, arrived, heads):
@@ -253,7 +251,8 @@
         out_shape=jax.ShapeDtypeStruct((blocks, span + SPARE, both), jnp.bfloat16),
         scratch_shapes=[pltpu.VMEM((blocks, both, BLK), jnp.bfloat16)] * heads
         + [pltpu.VMEM((blocks, BLK, both), jnp.float32)] * heads
-        + [pltpu.VMEM((2 * heads, both // 2), jnp.float32)],
+        + [pltpu.VMEM((2, lists.shape[1], BLK, BLK), jnp.float32)] * heads
+        + [pltpu.VMEM((heads, both // 2), jnp.float32)],
         compiler_params=pltpu.CompilerParams(vmem_limit_bytes=24 << 20),
         name="attention",
     )(first, lists, live, arrived)
@@ -337,13 +336,16 @@
 
 def gains_kernel(back_ref, out_ref):
     groups, rows, both = back_ref.shape
-    span = rows - SPARE
+    lanes = out_ref.shape[1]
     for group in range(groups):
-        extra = back_ref[group, span:].astype(jnp.float32)
-        total = extra[0:2]
+        extra = back_ref[group, rows - SPARE :].astype(jnp.float32)
+        total = extra[0:1]
         for n in range(1, PARTS):
-            total = total + extra[2 * n : 2 * n + 2]
-        out_ref[:, group * both : (group + 1) * both] = total
+            total = total + extra[n : n + 1]
+        for n in range(both // lanes):
+            row = total[:, n * lanes : (n + 1) * lanes]
+            at = group * (both // lanes) + n
+            out_ref[at : at + 1] = row
 
 
 def add_kernel(a_ref, b_ref, out_ref):
@@ -352,8 +354,8 @@
 
 def last_kernel(a_ref, b_ref, qg_ref, kg_ref, q_ref, k_ref):
     total = a_ref[...] + b_ref[...]
-    q_ref[...] = total[0:1] / qg_ref[...]
-    k_ref[...] = total[1:2] / kg_ref[...]
+    q_ref[...] = total / qg_ref[...]
+    k_ref[...] = total / kg_ref[...]
 
 
 def small_call(kernel, shapes, name, *args):
@@ -368,18 +370,24 @@
 
 
 def clip_gains(back, q_gain, k_gain):
-    features = q_gain.shape[0]
-    (total,) = small_call(gains_kernel, [(2, features)], "gains", back)
     size = lax.axis_size("clip")
+    rows = q_gain.shape[0] // BLK
+    (total,) = small_call(gains_kernel, [(rows, BLK)], "gains", back)
     flips = [1, 2, 6]
     for n, flip in enumerate(flips):
         other = lax.ppermute(total, "clip", [(i, i ^ flip) for i in range(size)])
         if n < len(flips) - 1:
-            (total,) = small_call(add_kernel, [(2, features)], "add", total, other)
+            (total,) = small_call(add_kernel, [(rows, BLK)], "add", total, other)
     q, k = small_call(
-        last_kernel, [(1, features)] * 2, "last", total, other, q_gain[None], k_gain[None]
+        last_kernel,
+        [(rows, BLK)] * 2,
+        "last",
+        total,
+        other,
+        q_gain.reshape(rows, BLK),
+        k_gain.reshape(rows, BLK),
     )
-    return q[0], k[0]
+    return q.reshape(-1), k.reshape(-1)
 
 
 def shards(query_raw, key_raw, value, upstream, query_gain, key_gain, key_blocks, live):

time: 149 us -> 148 us (level)
  Pallas kernels: 26.8 us -> 23.5 us
  blocking collectives: 114 us -> 116 us
    pallas_call x1, Pallas kernels: 15.3 us -> 12 us  [attention(): pl.pallas_call(attention_kernel, in_specs=[smem, smem, smem, vmem], out_s...]
    all_to_all x1, blocking collectives: 55.7 us -> 57.2 us  [shards(): lax.all_to_all(results, 'seq', split_axis=0, concat_axis=0, tiled=True)]
where the time goes in v3:
time: 148 us; the launch traced here: 147 us
  blocking collectives  116 us (78%)
  Pallas kernels  23.5 us (16%)
  waiting for transfers between devices  3.87 us (3%)
  starting transfers between devices  3.26 us (2%)
    all_to_all x1, blocking collectives, shards(): lax.all_to_all(packed, 'seq', split_axis=0, concat_axis=0, tiled=True)  58.6 us
    all_to_all x1, blocking collectives, shards(): lax.all_to_all(results, 'seq', split_axis=0, concat_axis=0, tiled=True)  57.2 us
    pallas_call x1, Pallas kernels, attention(): pl.pallas_call(attention_kernel, in_specs=[smem, smem, smem, vmem], out_s...  12 us
    pallas_call x1, Pallas kernels, unpack(): pl.pallas_call(unpack_kernel, in_specs=[vmem] * 5, out_specs=[hbm] * 4, o...  5.71 us
    pallas_call x1, Pallas kernels, pack(): pl.pallas_call(pack_kernel, in_specs=[hbm] * 6, out_specs=vmem, out_shape...  5.14 us
    ppermute x3, waiting for transfers between devices, clip_gains(): other = lax.ppermute(total, 'clip', [(i, i ^ flip) for i in range(size)])  3.87 us
    ppermute x3, starting transfers between devices, clip_gains(): other = lax.ppermute(total, 'clip', [(i, i ^ flip) for i in range(size)])  3.26 us
  transfers between devices with their start and end apart: 3, of which 2 were waited for; matrix products, arithmetic and copies ran while one was open for 0% of the time, Pallas kernels for 4%

profile of v3, /device:TPU:0, one launch (start us, length us, event | category | flops | bytes accessed | tf_op | source)
XLA Modules:
  0.0 147.3 jit_solution(11237434336062592383)
XLA Ops:
  0.6 5.1 %pack.1 = bf16[16,512,256]{2,1,0:T(8,128)(2,1)S(1)} custom-call(bf16[128,4096]{1,0:T(8,128)(2,1)} %bitcast.18, bf16[128,4096]{1,0:T(8,128)(2,1)} %bitcast.20, bf16[128,4096]{1,0:T(8,128)(2,1)} %bitcast.29, bf16[128,4096]{1,0:T(8,128)(2,1)} %bitcast.30, f32[1,4096]{1,0:T(1,128)} %bitcast.22, f32[1,4096]{1,0:T(1,128)} %bitcast.25), custom_call_target="tpu_custom_call" | custom-call | tf_op jit(solution)/shard_map/pack/pallas_call | solution.py:103
  5.8 0.0 copy-start.4
  5.8 0.0 copy-start.5
  5.8 58.6 %all_to_all.10.in_ref = bf16[16,512,256]{2,1,0:T(8,128)(2,1)S(1)} all-to-all(bf16[16,512,256]{2,1,0:T(8,128)(2,1)S(1)} %pack.1), channel_id=1, replica_groups=mesh['clip'=8,'seq'=16] {'seq'}, dimensions={0} | all-to-all | bytes 8388608 | tf_op jit(solution)/shard_map/all_to_all | solution.py:402
  64.5 0.0 copy-done.4
  64.5 0.0 copy-done.5
  64.5 12.0 %attention.1 = bf16[16,520,256]{2,1,0:T(8,128)(2,1)S(1)} custom-call(s32[1]{0:T(128)} %bitcast.6.first_ref, s32[16,4,32]{2,1,0:T(4,128)S(1)} %bitcast.28, s32[1,32]{1,0:T(1,128)S(1)} %copy-done.5, bf16[16,512,256]{2,1,0:T(8,128)(2,1)S(1)} %all_to_all.10.in_ref), custom_call_target="tpu_custom_call" | custom-call | tf_op jit(solution)/shard_map/attention/pallas_call | solution.py:247
  76.5 57.2 %all_to_all.11.back_ref = bf16[16,520,256]{2,1,0:T(8,128)(2,1)S(1)} all-to-all(bf16[16,520,256]{2,1,0:T(8,128)(2,1)S(1)} %attention.1), channel_id=1, replica_groups=mesh['clip'=8,'seq'=16] {'seq'}, dimensions={0} | all-to-all | bytes 8519680 | tf_op jit(solution)/shard_map/all_to_all | solution.py:404
  133.7 0.0 copy-start
  133.7 0.0 copy-start.1
  133.7 0.0 copy-start.2
  133.7 0.0 copy-start.3
  133.8 0.1 collective-permute-start
  133.9 1.2 collective-permute-done.b_ref
  135.0 1.0 collective-permute-start.1
  136.1 2.7 %collective-permute-done.1.b_ref = f32[32,128]{1,0:T(8,128)S(1)} collective-permute-done((f32[32,128]{1,0:T(8,128)S(1)}, f32[32,128]{1,0:T(8,128)S(1)}, u32[]{:S(2)}, u32[]{:S(2)}) %collective-permute-start.1) | collective-permute-done | bytes 16416 | tf_op jit(solution)/shard_map/ppermute | solution.py:378
  138.8 2.1 %collective-permute-start.2 = (f32[32,128]{1,0:T(8,128)S(1)}, f32[32,128]{1,0:T(8,128)S(1)}, u32[]{:S(2)}, u32[]{:S(2)}) collective-permute-start(f32[32,128]{1,0:T(8,128)S(1)} %add.3.a_ref), channel_id=1, source_target_pairs={{0,96},{16,112},{32,64},{48,80},{64,32},{80,48},{96,0},{112,16},{1... | collective-permute-start | bytes 49160 | tf_op jit(solution)/shard_map/ppermute | solution.py:378
  140.9 0.0 copy-done
  140.9 0.0 copy-done.1
  140.9 0.0 copy-done.2
  140.9 0.0 copy-done.3
  140.9 5.7 %unpack.1 = (bf16[128,4096]{1,0:T(8,128)(2,1)}, bf16[128,4096]{1,0:T(8,128)(2,1)}, bf16[128,4096]{1,0:T(8,128)(2,1)}, bf16[128,4096]{1,0:T(8,128)(2,1)}) custom-call(bf16[16,520,256]{2,1,0:T(8,128)(2,1)S(1)} %all_to_all.11.back_ref, bf16[128,4096]{1,0:T(8,128)(2,1)S(1)} %bitcast.19, bf16[128,4096]{1,0:T(8,128)(2,1)S(1)} %bitcast.21, f32[1,4096]{1,0:T(1,128)S(1)} %bitcast.23, ...), custom_call_target="tpu_custom_call" | custom-call | tf_op jit(solution)/shard_map/unpack/pallas_call | solution.py:322
  146.6 0.0 collective-permute-done.2.b_ref
  146.6 0.6 last.1
  (3 shorter events, 0.0 us)
Async XLA Ops:
  5.8 58.7 %copy-start.4 = (s32[1,32,16,4]{1,3,2,0:T(4,128)S(1)}, s32[1,32,16,4]{1,3,2,0:T(4,128)}, u32[]{:S(2)}) copy-start(s32[1,32,16,4]{1,3,2,0:T(4,128)} %param.14) | copy-start | bytes 24580
  5.8 58.7 %copy-start.5 = (s32[1,32]{1,0:T(1,128)S(1)}, s32[1,32]{1,0:T(1,128)}, u32[]{:S(2)}) copy-start(s32[1,32]{1,0:T(1,128)} %live_ref.1) | copy-start | bytes 388
  133.7 7.2 %copy-start = (bf16[1,128,4096]{2,1,0:T(8,128)(2,1)S(1)}, bf16[1,128,4096]{2,1,0:T(8,128)(2,1)}, u32[]{:S(2)}) copy-start(bf16[1,128,4096]{2,1,0:T(8,128)(2,1)} %param.8) | copy-start | bytes 3145732
  133.7 7.2 %copy-start.1 = (bf16[1,128,4096]{2,1,0:T(8,128)(2,1)S(1)}, bf16[1,128,4096]{2,1,0:T(8,128)(2,1)}, u32[]{:S(2)}) copy-start(bf16[1,128,4096]{2,1,0:T(8,128)(2,1)} %param.9) | copy-start | bytes 3145732
  133.7 7.2 %copy-start.2 = (f32[4096]{0:T(1024)S(1)}, f32[4096]{0:T(1024)}, u32[]{:S(2)}) copy-start(f32[4096]{0:T(1024)} %param.12) | copy-start | bytes 49156
  133.7 7.2 %copy-start.3 = (f32[4096]{0:T(1024)S(1)}, f32[4096]{0:T(1024)}, u32[]{:S(2)}) copy-start(f32[4096]{0:T(1024)} %param.13) | copy-start | bytes 49156
  133.8 1.3 collective-permute-start
  135.0 3.7 %collective-permute-start.1 = (f32[32,128]{1,0:T(8,128)S(1)}, f32[32,128]{1,0:T(8,128)S(1)}, u32[]{:S(2)}, u32[]{:S(2)}) collective-permute-start(f32[32,128]{1,0:T(8,128)S(1)} %add.2.a_ref), channel_id=1, source_target_pairs={{0,32},{16,48},{32,0},{48,16},{64,96},{80,112},{96,64},{112,80},{1... | collective-permute-start | bytes 49160 | tf_op jit(solution)/shard_map/ppermute | solution.py:378
  138.8 7.9 %collective-permute-start.2 = (f32[32,128]{1,0:T(8,128)S(1)}, f32[32,128]{1,0:T(8,128)S(1)}, u32[]{:S(2)}, u32[]{:S(2)}) collective-permute-start(f32[32,128]{1,0:T(8,128)S(1)} %add.3.a_ref), channel_id=1, source_target_pairs={{0,96},{16,112},{32,64},{48,80},{64,32},{80,48},{96,0},{112,16},{1... | collective-permute-start | bytes 49160 | tf_op jit(solution)/shard_map/ppermute | solution.py:378

commit v4 on v3

v4 whole, which is shorter than its diff:
```python
import jax
import jax.numpy as jnp
from jax import lax
from jax.experimental import pallas as pl
from jax.experimental.pallas import tpu as pltpu
from jax.sharding import PartitionSpec as P

BLK = 128
EPSILON = 1e-06
ROWS = 16
CHUNKS = 4
PARTS = 3
SPARE = 8
QUERY, COTANGENT, KEY, VALUE = range(4)
GRAD_Q, OUT, GRAD_K, GRAD_V = range(4)
LOG2E = 1.4426950408889634


def contract(a, b, dims):
    return lax.dot_general(a, b, (dims, ((), ())), preferred_element_type=jnp.float32)


def inverse_rms(x):
    return lax.rsqrt(jnp.mean(x * x, axis=-1, keepdims=True) + EPSILON)


def rank_heads(live_ref, place_ref, order_ref):
    count = place_ref.shape[0]
    most = lax.fori_loop(0, count, lambda h, n: n + (live_ref[0, h] >= 4).astype(jnp.int32), 0)
    some = lax.fori_loop(0, count, lambda h, n: n + (live_ref[0, h] >= 3).astype(jnp.int32), 0)

    def put(h, counts):
        four, three, two = counts
        is_four = live_ref[0, h] >= 4
        is_three = jnp.logical_and(live_ref[0, h] >= 3, jnp.logical_not(is_four))
        rank = jnp.where(is_four, four, jnp.where(is_three, three, two))
        place_ref[h] = rank
        order_ref[rank] = h
        step = jnp.logical_not(jnp.logical_or(is_four, is_three))
        return (
            four + is_four.astype(jnp.int32),
            three + is_three.astype(jnp.int32),
            two + step.astype(jnp.int32),
        )

    lax.fori_loop(0, count, put, (jnp.int32(0), most, some))


def group_and_slot(rank, groups):
    second = rank >= groups
    return jnp.where(second, 2 * groups - 1 - rank, rank), second.astype(jnp.int32)


def rank_scratch(heads):
    return [pltpu.SMEM((heads,), jnp.int32)] * 2


def pack_kernel(
    live_hbm,
    q_hbm,
    k_hbm,
    v_hbm,
    u_hbm,
    qg_hbm,
    kg_hbm,
    out_ref,
    raw_ref,
    gain_ref,
    live_ref,
    place_ref,
    order_ref,
    raw_sems,
    gain_sems,
    copy_sems,
    live_sem,
):
    groups, span, both = out_ref.shape
    width = both // 2
    tokens = raw_ref.shape[1]
    heads = span // (2 * tokens)
    step = tokens // CHUNKS

    loads = [
        [
            pltpu.make_async_copy(
                hbm.at[pl.ds(c * step, step)],
                raw_ref.at[n, pl.ds(c * step, step)],
                raw_sems.at[n, c],
            )
            for c in range(CHUNKS)
        ]
        for n, hbm in enumerate((q_hbm, k_hbm))
    ]
    gain_loads = [
        pltpu.make_async_copy(hbm, gain_ref.at[n], gain_sems.at[n])
        for n, hbm in enumerate((qg_hbm, kg_hbm))
    ]
    live_load = pltpu.make_async_copy(live_hbm, live_ref, live_sem)
    live_load.start()
    for n in range(2):
        gain_loads[n].start()
        loads[n][0].start()
    for c in range(1, CHUNKS):
        for n in range(2):
            loads[n][c].start()
    live_load.wait()
    rank_heads(live_ref, place_ref, order_ref)
    moves, spots = [], []
    for head in range(groups * heads):
        group, slot = group_and_slot(place_ref[head], groups)
        spots.append((group, slot))
        for n, (hbm, pair) in enumerate(((u_hbm, 0), (v_hbm, 1))):
            first = pl.multiple_of((pair * heads + slot) * tokens, tokens)
            moves.append(
                pltpu.make_async_copy(
                    hbm.at[:, pl.ds(head * width, width)],
                    out_ref.at[group, pl.ds(first, tokens), pl.ds(width, width)],
                    copy_sems.at[head, n],
                )
            )
    for move in moves:
        move.start()
    for c in range(CHUNKS):
        for n in range(2):
            if c == 0:
                gain_loads[n].wait()
            loads[n][c].wait()

            def some_rows(i, carry):
                row = pl.multiple_of(c * step + i * ROWS, ROWS)
                x = raw_ref[n, pl.ds(row, ROWS)].astype(jnp.float32)
                y = (x * inverse_rms(x) * gain_ref[n]).astype(jnp.bfloat16)
                for head, (group, slot) in enumerate(spots):
                    first = pl.multiple_of((n * heads + slot) * tokens + row, ROWS)
                    at = head * width
                    out_ref[group, pl.ds(first, ROWS), :width] = y[:, at : at + width]
                return carry

            lax.fori_loop(0, step // ROWS, some_rows, 0)
    for move in moves:
        move.wait()


def in_hbm(x):
    return pltpu.with_memory_space_constraint(x, pltpu.HBM)


def pack(live, q, k, v, u, q_gain, k_gain, groups, heads):
    tokens, features = q.shape
    width = features // (groups * heads)
    hbm = pl.BlockSpec(memory_space=pltpu.HBM)
    vmem = pl.BlockSpec(memory_space=pltpu.VMEM)
    return pl.pallas_call(
        pack_kernel,
        in_specs=[hbm] * 7,
        out_specs=vmem,
        out_shape=jax.ShapeDtypeStruct((groups, 2 * heads * tokens, 2 * width), jnp.bfloat16),
        scratch_shapes=[
            pltpu.VMEM((2, tokens, features), jnp.bfloat16),
            pltpu.VMEM((2, 1, features), jnp.float32),
            pltpu.SMEM(live.shape, jnp.int32),
            *rank_scratch(groups * heads),
            pltpu.SemaphoreType.DMA((2, CHUNKS)),
            pltpu.SemaphoreType.DMA((2,)),
            pltpu.SemaphoreType.DMA((groups * heads, 2)),
            pltpu.SemaphoreType.DMA(()),
        ],
        compiler_params=pltpu.CompilerParams(vmem_limit_bytes=12 << 20),
        name="pack",
    )(*(in_hbm(x) for x in (live, q, k, v, u, q_gain[None], k_gain[None])))


def attention_kernel(mine_ref, lists_ref, live_ref, in_ref, out_ref, *scratch):
    place_ref, order_ref, *scratch = scratch
    blocks, span, both = in_ref.shape
    heads = len(scratch) // 3
    width = both // 2
    scale = width ** (-0.5)
    turned, sums, ahead, gains_ref = scratch[:heads], scratch[heads : 2 * heads], scratch[2 * heads : -1], scratch[-1]
    rank_heads(live_ref, place_ref, order_ref)
    mine = mine_ref[0]
    owned = [order_ref[mine], order_ref[2 * blocks - 1 - mine]]
    live = [live_ref[0, h] for h in owned]

    def place(pair, head):
        return pl.ds((pair * heads + head) * BLK, BLK)

    def parts(row):
        pieces = []
        for _ in range(PARTS):
            pieces.append(row.astype(jnp.bfloat16))
            row = row - pieces[-1].astype(jnp.float32)
        return pieces

    def prepare(j, carry):
        for head in range(heads):
            turned[head][j] = in_ref[j, place(1, head)].T
            sums[head][j] = jnp.zeros((BLK, both), jnp.float32)
        return carry

    lax.fori_loop(0, blocks, prepare, 0, unroll=4)

    def start(b, head, slots):
        q = in_ref[b, place(0, head), :width]
        u = in_ref[b, place(0, head), width:]
        diagonal = (q, u)
        chosen = [lists_ref[b, s, owned[head]] for s in range(slots)]
        rows = jnp.concatenate([in_ref[j, place(1, head)] for j in chosen], axis=0)
        scores = contract(rows[:, :width], q, ((1,), (1,)))
        grads = contract(rows[:, width:], u, ((1,), (1,)))
        products = ([scores[s * BLK : (s + 1) * BLK] for s in range(slots)], [grads[s * BLK : (s + 1) * BLK] for s in range(slots)])
        return q, diagonal, chosen, products

    def softmax(products):
        scores, grads = products
        factor = scale * LOG2E
        tops = [jnp.max(s, axis=0, keepdims=True) * factor for s in scores]
        top = tops[0]
        for t in tops[1:]:
            top = jnp.maximum(top, t)
        raised = [jnp.exp2(s * factor - top) for s in scores]
        total = raised[0]
        inner = raised[0] * grads[0]
        for e, g in zip(raised[1:], grads[1:]):
            total = total + e
            inner = inner + e * g
        inverse = 1.0 / jnp.sum(total, axis=0, keepdims=True)
        delta = jnp.sum(inner, axis=0, keepdims=True) * inverse
        probs = [e * inverse for e in raised]
        low = [p.astype(jnp.bfloat16) for p in probs]
        ds = [(p * ((g - delta) * scale)).astype(jnp.bfloat16) for p, g in zip(probs, grads)]
        return low, ds

    def finish_block(b, head, q, diagonal, chosen, low, ds):
        keys = jnp.concatenate([turned[head][j, :width] for j in chosen], axis=1)
        values = jnp.concatenate([turned[head][j, width:] for j in chosen], axis=1)
        out_t = contract(values, jnp.concatenate(low, axis=0), ((1,), (0,)))
        dq_t = contract(keys, jnp.concatenate(ds, axis=0), ((1,), (0,)))
        q, u = diagonal
        more_k = contract(jnp.concatenate(ds, axis=0), q, ((1,), (0,)))
        more_v = contract(jnp.concatenate(low, axis=0), u, ((1,), (0,)))
        old = [sums[head][j] for j in chosen]
        for s, (j, o) in enumerate(zip(chosen, old)):
            sums[head][j, :, :width] = o[:, :width] + more_k[s * BLK : (s + 1) * BLK]
            sums[head][j, :, width:] = o[:, width:] + more_v[s * BLK : (s + 1) * BLK]
        dq = dq_t.astype(jnp.bfloat16).T
        out_ref[b, place(0, head), :width] = dq
        out_ref[b, place(0, head), width:] = out_t.astype(jnp.bfloat16).T
        return jnp.sum(dq.astype(jnp.float32) * q.astype(jnp.float32), axis=0, keepdims=True)

    for slots in ((2, 2), (3, 2), (3, 3), (4, 2), (4, 3), (4, 4)):

        @pl.when(jnp.logical_and(live[0] == slots[0], live[1] == slots[1]))
        def _():
            def keep(h, products):
                for s in range(slots[h]):
                    for n in range(2):
                        ahead[h][n, s] = products[n][s]

            def step(b, gain):
                done = []
                for h in range(heads):
                    products = [[ahead[h][n, s] for s in range(slots[h])] for n in range(2)]
                    after = h + 1 if h + 1 < heads else 0
                    at = b if h + 1 < heads else jnp.minimum(b + 1, blocks - 1)
                    keep(after, start(at, after, slots[after])[3])
                    low, ds = softmax(products)
                    q = in_ref[b, place(0, h), :width]
                    u = in_ref[b, place(0, h), width:]
                    chosen = [lists_ref[b, s, owned[h]] for s in range(slots[h])]
                    done.append(gain[h] + finish_block(b, h, q, (q, u), chosen, low, ds))
                return tuple(done)

            keep(0, start(0, 0, slots[0])[3])

            gain = lax.fori_loop(
                0, blocks, step, (jnp.zeros((1, width), jnp.float32),) * heads, unroll=4
            )
            for h in range(heads):
                gains_ref[h : h + 1] = gain[h]

    extra = parts(jnp.concatenate([gains_ref[h : h + 1] for h in range(heads)], axis=1))
    extra.append(jnp.zeros((SPARE - PARTS, both), jnp.bfloat16))
    extra = jnp.concatenate(extra, axis=0)

    def finish(j, carry):
        for head in range(heads):
            out_ref[j, place(1, head)] = sums[head][j].astype(jnp.bfloat16)
        out_ref[j, span:] = extra
        return carry

    lax.fori_loop(0, blocks, finish, 0, unroll=4)


def attention(mine, lists, live, arrived, heads):
    blocks, span, both = arrived.shape
    vmem = pl.BlockSpec(memory_space=pltpu.VMEM)
    smem = pl.BlockSpec(memory_space=pltpu.SMEM)
    return pl.pallas_call(
        attention_kernel,
        in_specs=[smem, smem, smem, vmem],
        out_specs=vmem,
        out_shape=jax.ShapeDtypeStruct((blocks, span + SPARE, both), jnp.bfloat16),
        scratch_shapes=rank_scratch(live.shape[1])
        + [pltpu.VMEM((blocks, both, BLK), jnp.bfloat16)] * heads
        + [pltpu.VMEM((blocks, BLK, both), jnp.float32)] * heads
        + [pltpu.VMEM((2, lists.shape[1], BLK, BLK), jnp.float32)] * heads
        + [pltpu.VMEM((heads, both // 2), jnp.float32)],
        compiler_params=pltpu.CompilerParams(vmem_limit_bytes=24 << 20),
        name="attention",
    )(mine, lists, live, arrived)


def unpack_kernel(
    live_ref,
    back_ref,
    q_ref,
    k_ref,
    qg_ref,
    kg_ref,
    out_hbm,
    dq_hbm,
    dk_hbm,
    dv_hbm,
    place_ref,
    order_ref,
    done_ref,
    sems,
    copy_sems,
):
    groups, _, both = back_ref.shape
    width = both // 2
    tokens, features = q_ref.shape
    heads = features // (groups * width)
    step = tokens // CHUNKS
    rank_heads(live_ref, place_ref, order_ref)
    moves, spots = [], []
    for head in range(groups * heads):
        group, slot = group_and_slot(place_ref[head], groups)
        spots.append((group, slot))
        for n, hbm in enumerate((out_hbm, dv_hbm)):
            first = pl.multiple_of((n * heads + slot) * tokens, tokens)
            moves.append(
                pltpu.make_async_copy(
                    back_ref.at[group, pl.ds(first, tokens), pl.ds(width, width)],
                    hbm.at[:, pl.ds(head * width, width)],
                    copy_sems.at[head, n],
                )
            )
    for move in moves:
        move.start()
    for c in range(CHUNKS):
        for n, (raw_ref, gain_ref, hbm) in enumerate(
            ((q_ref, qg_ref, dq_hbm), (k_ref, kg_ref, dk_hbm))
        ):

            def some_rows(i, carry):
                row = pl.multiple_of(c * step + i * ROWS, ROWS)
                x = raw_ref[pl.ds(row, ROWS)].astype(jnp.float32)
                inverse = inverse_rms(x)
                unit = x * inverse
                pieces = []
                for group, slot in spots:
                    first = pl.multiple_of((n * heads + slot) * tokens + row, ROWS)
                    pieces.append(back_ref[group, pl.ds(first, ROWS), :width])
                grads = jnp.concatenate(pieces, axis=-1)
                g = grads.astype(jnp.float32) * gain_ref[...]
                mean = jnp.mean(g * unit, axis=-1, keepdims=True)
                done_ref[n, pl.ds(row, ROWS)] = (inverse * (g - unit * mean)).astype(jnp.bfloat16)
                return carry

            lax.fori_loop(0, step // ROWS, some_rows, 0)
            move = pltpu.make_async_copy(
                done_ref.at[n, pl.ds(c * step, step)], hbm.at[pl.ds(c * step, step)], sems.at[n, c]
            )
            move.start()
            moves.append(move)
    for move in moves:
        move.wait()


def unpack(live, back, q, k, q_gain, k_gain):
    groups, _, both = back.shape
    tokens, features = q.shape
    hbm = pl.BlockSpec(memory_space=pltpu.HBM)
    vmem = pl.BlockSpec(memory_space=pltpu.VMEM)
    return pl.pallas_call(
        unpack_kernel,
        in_specs=[pl.BlockSpec(memory_space=pltpu.SMEM)] + [vmem] * 5,
        out_specs=[hbm] * 4,
        out_shape=[jax.ShapeDtypeStruct((tokens, features), jnp.bfloat16)] * 4,
        scratch_shapes=[
            *rank_scratch(live.shape[1]),
            pltpu.VMEM((2, tokens, features), jnp.bfloat16),
            pltpu.SemaphoreType.DMA((2, CHUNKS)),
            pltpu.SemaphoreType.DMA((2 * features // both, 2)),
        ],
        compiler_params=pltpu.CompilerParams(vmem_limit_bytes=12 << 20),
        name="unpack",
    )(live, back, q, k, q_gain[None], k_gain[None])


def gains_kernel(live_ref, back_ref, out_ref, place_ref, order_ref):
    groups, rows, _ = back_ref.shape
    heads, width = out_ref.shape
    rank_heads(live_ref, place_ref, order_ref)
    for head in range(heads):
        group, slot = group_and_slot(place_ref[head], groups)
        extra = back_ref[group, rows - SPARE :].astype(jnp.float32)
        total = extra[0:1]
        for n in range(1, PARTS):
            total = total + extra[n : n + 1]
        out_ref[head : head + 1] = jnp.where(slot == 0, total[:, :width], total[:, width:])


def add_kernel(a_ref, b_ref, out_ref):
    out_ref[...] = a_ref[...] + b_ref[...]


def last_kernel(a_ref, b_ref, qg_ref, kg_ref, q_ref, k_ref):
    total = a_ref[...] + b_ref[...]
    q_ref[...] = total / qg_ref[...]
    k_ref[...] = total / kg_ref[...]


def small_call(kernel, shapes, name, *args):
    return pl.pallas_call(
        kernel,
        in_specs=[pl.BlockSpec(memory_space=pltpu.VMEM)] * len(args),
        out_specs=[pl.BlockSpec(memory_space=pltpu.VMEM)] * len(shapes),
        out_shape=[jax.ShapeDtypeStruct(shape, jnp.float32) for shape in shapes],
        compiler_params=pltpu.CompilerParams(vmem_limit_bytes=2 << 20),
        name=name,
    )(*args)


def clip_gains(live, back, q_gain, k_gain):
    size = lax.axis_size("clip")
    rows = q_gain.shape[0] // BLK
    total = pl.pallas_call(
        gains_kernel,
        in_specs=[pl.BlockSpec(memory_space=pltpu.SMEM), pl.BlockSpec(memory_space=pltpu.VMEM)],
        out_specs=pl.BlockSpec(memory_space=pltpu.VMEM),
        out_shape=jax.ShapeDtypeStruct((rows, BLK), jnp.float32),
        scratch_shapes=rank_scratch(rows),
        compiler_params=pltpu.CompilerParams(vmem_limit_bytes=2 << 20),
        name="gains",
    )(live, back)
    flips = [1, 2, 6]
    for n, flip in enumerate(flips):
        other = lax.ppermute(total, "clip", [(i, i ^ flip) for i in range(size)])
        if n < len(flips) - 1:
            (total,) = small_call(add_kernel, [(rows, BLK)], "add", total, other)
    q, k = small_call(
        last_kernel,
        [(rows, BLK)] * 2,
        "last",
        total,
        other,
        q_gain.reshape(rows, BLK),
        k_gain.reshape(rows, BLK),
    )
    return q.reshape(-1), k.reshape(-1)


def shards(query_raw, key_raw, value, upstream, query_gain, key_gain, key_blocks, live):
    groups = lax.axis_size("seq")
    heads = key_blocks.shape[1] // groups
    mine = lax.axis_index("seq").reshape(1)
    lists = jnp.transpose(key_blocks[0], (1, 2, 0))
    packed = pack(
        live, query_raw[0], key_raw[0], value[0], upstream[0], query_gain, key_gain, groups, heads
    )
    packed, mine = lax.optimization_barrier((packed, mine))
    arrived = lax.all_to_all(packed, "seq", split_axis=0, concat_axis=0, tiled=True)
    results = attention(mine, lists, live, arrived, heads)
    back = lax.all_to_all(results, "seq", split_axis=0, concat_axis=0, tiled=True)
    attended, grad_query, grad_key, grad_value = unpack(
        live, back, query_raw[0], key_raw[0], query_gain, key_gain
    )
    q_total, k_total = clip_gains(live, back, query_gain, key_gain)
    return (
        attended[None],
        grad_query[None],
        grad_key[None],
        grad_value[None],
        q_total,
        k_total,
    )


def solution(mesh):
    tokens = P("clip", "seq", None)
    return jax.shard_map(
        shards,
        mesh=mesh,
        in_specs=(tokens,) * 4 + (P(), P(), P("clip", None, None, None), P("clip", None)),
        out_specs=(tokens,) * 4 + (P(), P()),
        check_vma=False,
    )
```

time: 148 us -> 148 us (level)
  Pallas kernels: 23.5 us -> 26.7 us
  blocking collectives: 116 us -> 113 us
    all_to_all x1, blocking collectives: 57.2 us -> 53.9 us  [shards(): lax.all_to_all(results, 'seq', split_axis=0, concat_axis=0, tiled=True)]
    pallas_call x2 -> x3, Pallas kernels: 10.8 us -> 14.1 us  [the longest x1 7.33 us: unpack(): pl.pallas_call(unpack_kernel, in_specs=[pl.BlockSpec(memory_space=pltpu.S...]
  transfers between devices with their start and end apart: 3 -> 3, of which waited for: 2 -> 2; matrix products, arithmetic and copies ran while one was open for 0% -> 0% of each run, Pallas kernels for 4% -> 5%
where the time goes in v4:
time: 148 us
  blocking collectives  113 us (76%)
  Pallas kernels  26.7 us (18%)
  starting transfers between devices  4.39 us (3%)
  waiting for transfers between devices  3.31 us (2%)
    all_to_all x1, blocking collectives, shards(): lax.all_to_all(packed, 'seq', split_axis=0, concat_axis=0, tiled=True)  58.6 us
    all_to_all x1, blocking collectives, shards(): lax.all_to_all(results, 'seq', split_axis=0, concat_axis=0, tiled=True)  53.9 us
    pallas_call x1, Pallas kernels, attention(): pl.pallas_call(attention_kernel, in_specs=[smem, smem, smem, vmem], out_s...  12 us
    pallas_call x1, Pallas kernels, unpack(): pl.pallas_call(unpack_kernel, in_specs=[pl.BlockSpec(memory_space=pltpu.S...  7.33 us
    pallas_call x1, Pallas kernels, pack(): pl.pallas_call(pack_kernel, in_specs=[hbm] * 7, out_specs=vmem, out_shape...  5.21 us
    ppermute x3, starting transfers between devices, clip_gains(): other = lax.ppermute(total, 'clip', [(i, i ^ flip) for i in range(size)])  4.39 us
    ppermute x3, waiting for transfers between devices, clip_gains(): other = lax.ppermute(total, 'clip', [(i, i ^ flip) for i in range(size)])  3.31 us
  transfers between devices with their start and end apart: 3, of which 2 were waited for; matrix products, arithmetic and copies ran while one was open for 0% of the time, Pallas kernels for 5%

profile of v4, /device:TPU:0, one launch (start us, length us, event | category | flops | bytes accessed | tf_op | source)
XLA Modules:
  0.0 147.7 jit_solution(1183272017475471988)
XLA Ops:
  0.6 5.2 %pack.1 = bf16[16,512,256]{2,1,0:T(8,128)(2,1)S(1)} custom-call(s32[1,32]{1,0:T(1,128)} %live_ref.5, bf16[128,4096]{1,0:T(8,128)(2,1)} %bitcast.18, bf16[128,4096]{1,0:T(8,128)(2,1)} %bitcast.20, bf16[128,4096]{1,0:T(8,128)(2,1)} %bitcast.29, bf16[128,4096]{1,0:T(8,128)(2,1)} %bitcast.30, f32[1,4096]{1,0:T(1,128)} %bitcast.22, f32[1,4096]{1,0:T(1,128)} %bitcast.25), custom_call_target="tpu_custom_call" | custom-call | tf_op jit(solution)/shard_map/pack/pallas_call | solution.py:153
  5.9 0.0 copy-start.4
  5.9 0.0 copy-start.5
  5.9 58.6 %all_to_all.10.in_ref = bf16[16,512,256]{2,1,0:T(8,128)(2,1)S(1)} all-to-all(bf16[16,512,256]{2,1,0:T(8,128)(2,1)S(1)} %pack.1), channel_id=1, replica_groups=mesh['clip'=8,'seq'=16] {'seq'}, dimensions={0} | all-to-all | bytes 8388608 | tf_op jit(solution)/shard_map/all_to_all | solution.py:475
  64.5 0.0 copy-done.4
  64.5 0.0 copy-done.5
  64.5 12.0 %attention.1 = bf16[16,520,256]{2,1,0:T(8,128)(2,1)S(1)} custom-call(s32[1]{0:T(128)} %bitcast.6.mine_ref, s32[16,4,32]{2,1,0:T(4,128)S(1)} %bitcast.28, s32[1,32]{1,0:T(1,128)S(1)} %copy-done.5, bf16[16,512,256]{2,1,0:T(8,128)(2,1)S(1)} %all_to_all.10.in_ref), custom_call_target="tpu_custom_call" | custom-call | tf_op jit(solution)/shard_map/attention/pallas_call | solution.py:299
  76.5 53.9 %all_to_all.11.back_ref = bf16[16,520,256]{2,1,0:T(8,128)(2,1)S(1)} all-to-all(bf16[16,520,256]{2,1,0:T(8,128)(2,1)S(1)} %attention.1), channel_id=1, replica_groups=mesh['clip'=8,'seq'=16] {'seq'}, dimensions={0} | all-to-all | bytes 8519680 | tf_op jit(solution)/shard_map/all_to_all | solution.py:477
  130.5 0.0 copy-start
  130.5 0.0 copy-start.1
  130.5 0.0 copy-start.2
  130.5 0.0 copy-start.3
  130.5 1.5 %gains.1.a_ref = f32[32,128]{1,0:T(8,128)S(1)} custom-call(s32[1,32]{1,0:T(1,128)S(1)} %copy-done.5, bf16[16,520,256]{2,1,0:T(8,128)(2,1)S(1)} %all_to_all.11.back_ref), custom_call_target="tpu_custom_call" | custom-call | tf_op jit(solution)/shard_map/gains/pallas_call | solution.py:440
  132.1 0.1 collective-permute-start
  132.1 1.2 collective-permute-done.b_ref
  133.3 1.6 %collective-permute-start.1 = (f32[32,128]{1,0:T(8,128)S(1)}, f32[32,128]{1,0:T(8,128)S(1)}, u32[]{:S(2)}, u32[]{:S(2)}) collective-permute-start(f32[32,128]{1,0:T(8,128)S(1)} %add.2.a_ref), channel_id=1, source_target_pairs={{0,32},{16,48},{32,0},{48,16},{64,96},{80,112},{96,64},{112,80},{1... | collective-permute-start | bytes 49160 | tf_op jit(solution)/shard_map/ppermute | solution.py:451
  134.9 2.1 %collective-permute-done.1.b_ref = f32[32,128]{1,0:T(8,128)S(1)} collective-permute-done((f32[32,128]{1,0:T(8,128)S(1)}, f32[32,128]{1,0:T(8,128)S(1)}, u32[]{:S(2)}, u32[]{:S(2)}) %collective-permute-start.1) | collective-permute-done | bytes 16416 | tf_op jit(solution)/shard_map/ppermute | solution.py:451
  137.1 2.7 %collective-permute-start.2 = (f32[32,128]{1,0:T(8,128)S(1)}, f32[32,128]{1,0:T(8,128)S(1)}, u32[]{:S(2)}, u32[]{:S(2)}) collective-permute-start(f32[32,128]{1,0:T(8,128)S(1)} %add.3.a_ref), channel_id=1, source_target_pairs={{0,96},{16,112},{32,64},{48,80},{64,32},{80,48},{96,0},{112,16},{1... | collective-permute-start | bytes 49160 | tf_op jit(solution)/shard_map/ppermute | solution.py:451
  139.8 0.0 copy-done
  139.8 0.0 copy-done.1
  139.8 0.0 copy-done.2
  139.8 0.0 copy-done.3
  139.8 7.3 %unpack.1 = (bf16[128,4096]{1,0:T(8,128)(2,1)}, bf16[128,4096]{1,0:T(8,128)(2,1)}, bf16[128,4096]{1,0:T(8,128)(2,1)}, bf16[128,4096]{1,0:T(8,128)(2,1)}) custom-call(s32[1,32]{1,0:T(1,128)S(1)} %copy-done.5, bf16[16,520,256]{2,1,0:T(8,128)(2,1)S(1)} %all_to_all.11.back_ref, bf16[128,4096]{1,0:T(8,128)(2,1)S(1)} %bitcast.19, bf16[128,4096]{1,0:T(8,128)(2,1)S(1)} %bitcast.21, ...), custom_call_target="tpu_custom_call" | custom-call | tf_op jit(solution)/shard_map/unpack/pallas_call | solution.py:387
  147.1 0.0 collective-permute-done.2.b_ref
  147.1 0.6 last.1
  (2 shorter events, 0.0 us)
Async XLA Ops:
  5.9 58.7 %copy-start.4 = (s32[1,32,16,4]{1,3,2,0:T(4,128)S(1)}, s32[1,32,16,4]{1,3,2,0:T(4,128)}, u32[]{:S(2)}) copy-start(s32[1,32,16,4]{1,3,2,0:T(4,128)} %param.14) | copy-start | bytes 24580
  5.9 58.7 %copy-start.5 = (s32[1,32]{1,0:T(1,128)S(1)}, s32[1,32]{1,0:T(1,128)}, u32[]{:S(2)}) copy-start(s32[1,32]{1,0:T(1,128)} %live_ref.5) | copy-start | bytes 388
  130.5 9.3 %copy-start = (bf16[1,128,4096]{2,1,0:T(8,128)(2,1)S(1)}, bf16[1,128,4096]{2,1,0:T(8,128)(2,1)}, u32[]{:S(2)}) copy-start(bf16[1,128,4096]{2,1,0:T(8,128)(2,1)} %param.8) | copy-start | bytes 3145732
  130.5 9.3 %copy-start.1 = (bf16[1,128,4096]{2,1,0:T(8,128)(2,1)S(1)}, bf16[1,128,4096]{2,1,0:T(8,128)(2,1)}, u32[]{:S(2)}) copy-start(bf16[1,128,4096]{2,1,0:T(8,128)(2,1)} %param.9) | copy-start | bytes 3145732
  130.5 9.3 %copy-start.2 = (f32[4096]{0:T(1024)S(1)}, f32[4096]{0:T(1024)}, u32[]{:S(2)}) copy-start(f32[4096]{0:T(1024)} %param.12) | copy-start | bytes 49156
  130.5 9.3 %copy-start.3 = (f32[4096]{0:T(1024)S(1)}, f32[4096]{0:T(1024)}, u32[]{:S(2)}) copy-start(f32[4096]{0:T(1024)} %param.13) | copy-start | bytes 49156
  132.1 1.3 collective-permute-start
  133.3 3.7 %collective-permute-start.1 = (f32[32,128]{1,0:T(8,128)S(1)}, f32[32,128]{1,0:T(8,128)S(1)}, u32[]{:S(2)}, u32[]{:S(2)}) collective-permute-start(f32[32,128]{1,0:T(8,128)S(1)} %add.2.a_ref), channel_id=1, source_target_pairs={{0,32},{16,48},{32,0},{48,16},{64,96},{80,112},{96,64},{112,80},{1... | collective-permute-start | bytes 49160 | tf_op jit(solution)/shard_map/ppermute | solution.py:451
  137.1 10.0 %collective-permute-start.2 = (f32[32,128]{1,0:T(8,128)S(1)}, f32[32,128]{1,0:T(8,128)S(1)}, u32[]{:S(2)}, u32[]{:S(2)}) collective-permute-start(f32[32,128]{1,0:T(8,128)S(1)} %add.3.a_ref), channel_id=1, source_target_pairs={{0,96},{16,112},{32,64},{48,80},{64,32},{80,48},{96,0},{112,16},{1... | collective-permute-start | bytes 49160 | tf_op jit(solution)/shard_map/ppermute | solution.py:451

commit v5 on v4

--- a/solution.py
+++ b/solution.py
@@ -7,10 +7,11 @@
 
 BLK = 128
 EPSILON = 1e-06
-ROWS = 16
-CHUNKS = 4
+ROWS = 64
+CHUNKS = 2
 PARTS = 3
 SPARE = 8
+PLACE, ORDER = range(2)
 QUERY, COTANGENT, KEY, VALUE = range(4)
 GRAD_Q, OUT, GRAD_K, GRAD_V = range(4)
 LOG2E = 1.4426950408889634
@@ -24,8 +25,8 @@
     return lax.rsqrt(jnp.mean(x * x, axis=-1, keepdims=True) + EPSILON)
 
 
-def rank_heads(live_ref, place_ref, order_ref):
-    count = place_ref.shape[0]
+def rank_heads(live_ref, table_ref):
+    count = table_ref.shape[1]
     most = lax.fori_loop(0, count, lambda h, n: n + (live_ref[0, h] >= 4).astype(jnp.int32), 0)
     some = lax.fori_loop(0, count, lambda h, n: n + (live_ref[0, h] >= 3).astype(jnp.int32), 0)
 
@@ -34,8 +35,8 @@
         is_four = live_ref[0, h] >= 4
         is_three = jnp.logical_and(live_ref[0, h] >= 3, jnp.logical_not(is_four))
         rank = jnp.where(is_four, four, jnp.where(is_three, three, two))
-        place_ref[h] = rank
-        order_ref[rank] = h
+        table_ref[PLACE, h] = rank
+        table_ref[ORDER, rank] = h
         step = jnp.logical_not(jnp.logical_or(is_four, is_three))
         return (
             four + is_four.astype(jnp.int32),
@@ -49,10 +50,6 @@
 def group_and_slot(rank, groups):
     second = rank >= groups
     return jnp.where(second, 2 * groups - 1 - rank, rank), second.astype(jnp.int32)
-
-
-def rank_scratch(heads):
-    return [pltpu.SMEM((heads,), jnp.int32)] * 2
 
 
 def pack_kernel(
@@ -64,11 +61,10 @@
     qg_hbm,
     kg_hbm,
     out_ref,
+    table_ref,
     raw_ref,
     gain_ref,
     live_ref,
-    place_ref,
-    order_ref,
     raw_sems,
     gain_sems,
     copy_sems,
@@ -104,10 +100,10 @@
         for n in range(2):
             loads[n][c].start()
     live_load.wait()
-    rank_heads(live_ref, place_ref, order_ref)
+    rank_heads(live_ref, table_ref)
     moves, spots = [], []
     for head in range(groups * heads):
-        group, slot = group_and_slot(place_ref[head], groups)
+        group, slot = group_and_slot(table_ref[PLACE, head], groups)
         spots.append((group, slot))
         for n, (hbm, pair) in enumerate(((u_hbm, 0), (v_hbm, 1))):
             first = pl.multiple_of((pair * heads + slot) * tokens, tokens)
@@ -153,13 +149,15 @@
     return pl.pallas_call(
         pack_kernel,
         in_specs=[hbm] * 7,
-        out_specs=vmem,
-        out_shape=jax.ShapeDtypeStruct((groups, 2 * heads * tokens, 2 * width), jnp.bfloat16),
+        out_specs=[vmem, pl.BlockSpec(memory_space=pltpu.SMEM)],
+        out_shape=[
+            jax.ShapeDtypeStruct((groups, 2 * heads * tokens, 2 * width), jnp.bfloat16),
+            jax.ShapeDtypeStruct((2, groups * heads), jnp.int32),
+        ],
         scratch_shapes=[
             pltpu.VMEM((2, tokens, features), jnp.bfloat16),
             pltpu.VMEM((2, 1, features), jnp.float32),
             pltpu.SMEM(live.shape, jnp.int32),
-            *rank_scratch(groups * heads),
             pltpu.SemaphoreType.DMA((2, CHUNKS)),
             pltpu.SemaphoreType.DMA((2,)),
             pltpu.SemaphoreType.DMA((groups * heads, 2)),
@@ -170,16 +168,14 @@
     )(*(in_hbm(x) for x in (live, q, k, v, u, q_gain[None], k_gain[None])))
 
 
-def attention_kernel(mine_ref, lists_ref, live_ref, in_ref, out_ref, *scratch):
-    place_ref, order_ref, *scratch = scratch
+def attention_kernel(mine_ref, table_ref, lists_ref, live_ref, in_ref, out_ref, *scratch):
     blocks, span, both = in_ref.shape
     heads = len(scratch) // 3
     width = both // 2
     scale = width ** (-0.5)
     turned, sums, ahead, gains_ref = scratch[:heads], scratch[heads : 2 * heads], scratch[2 * heads : -1], scratch[-1]
-    rank_heads(live_ref, place_ref, order_ref)
     mine = mine_ref[0]
-    owned = [order_ref[mine], order_ref[2 * blocks - 1 - mine]]
+    owned = [table_ref[ORDER, rank] for rank in (mine, 2 * blocks - 1 - mine)]
     live = [live_ref[0, h] for h in owned]
 
     def place(pair, head):
@@ -292,27 +288,26 @@
     lax.fori_loop(0, blocks, finish, 0, unroll=4)
 
 
-def attention(mine, lists, live, arrived, heads):
+def attention(mine, table, lists, live, arrived, heads):
     blocks, span, both = arrived.shape
     vmem = pl.BlockSpec(memory_space=pltpu.VMEM)
     smem = pl.BlockSpec(memory_space=pltpu.SMEM)
     return pl.pallas_call(
         attention_kernel,
-        in_specs=[smem, smem, smem, vmem],
+        in_specs=[smem, smem, smem, smem, vmem],
         out_specs=vmem,
         out_shape=jax.ShapeDtypeStruct((blocks, span + SPARE, both), jnp.bfloat16),
-        scratch_shapes=rank_scratch(live.shape[1])
-        + [pltpu.VMEM((blocks, both, BLK), jnp.bfloat16)] * heads
+        scratch_shapes=[pltpu.VMEM((blocks, both, BLK), jnp.bfloat16)] * heads
         + [pltpu.VMEM((blocks, BLK, both), jnp.float32)] * heads
         + [pltpu.VMEM((2, lists.shape[1], BLK, BLK), jnp.float32)] * heads
         + [pltpu.VMEM((heads, both // 2), jnp.float32)],
         compiler_params=pltpu.CompilerParams(vmem_limit_bytes=24 << 20),
         name="attention",
-    )(mine, lists, live, arrived)
+    )(mine, table, lists, live, arrived)
 
 
 def unpack_kernel(
-    live_ref,
+    table_ref,
     back_ref,
     q_ref,
     k_ref,
@@ -322,8 +317,6 @@
     dq_hbm,
     dk_hbm,
     dv_hbm,
-    place_ref,
-    order_ref,
     done_ref,
     sems,
     copy_sems,
@@ -333,10 +326,9 @@
     tokens, features = q_ref.shape
     heads = features // (groups * width)
     step = tokens // CHUNKS
-    rank_heads(live_ref, place_ref, order_ref)
     moves, spots = [], []
     for head in range(groups * heads):
-        group, slot = group_and_slot(place_ref[head], groups)
+        group, slot = group_and_slot(table_ref[PLACE, head], groups)
         spots.append((group, slot))
         for n, hbm in enumerate((out_hbm, dv_hbm)):
             first = pl.multiple_of((n * heads + slot) * tokens, tokens)
@@ -379,7 +371,7 @@
         move.wait()
 
 
-def unpack(live, back, q, k, q_gain, k_gain):
+def unpack(table, back, q, k, q_gain, k_gain):
     groups, _, both = back.shape
     tokens, features = q.shape
     hbm = pl.BlockSpec(memory_space=pltpu.HBM)
@@ -390,22 +382,20 @@
         out_specs=[hbm] * 4,
         out_shape=[jax.ShapeDtypeStruct((tokens, features), jnp.bfloat16)] * 4,
         scratch_shapes=[
-            *rank_scratch(live.shape[1]),
             pltpu.VMEM((2, tokens, features), jnp.bfloat16),
             pltpu.SemaphoreType.DMA((2, CHUNKS)),
             pltpu.SemaphoreType.DMA((2 * features // both, 2)),
         ],
         compiler_params=pltpu.CompilerParams(vmem_limit_bytes=12 << 20),
         name="unpack",
-    )(live, back, q, k, q_gain[None], k_gain[None])
-
-
-def gains_kernel(live_ref, back_ref, out_ref, place_ref, order_ref):
+    )(table, back, q, k, q_gain[None], k_gain[None])
+
+
+def gains_kernel(table_ref, back_ref, out_ref):
     groups, rows, _ = back_ref.shape
     heads, width = out_ref.shape
-    rank_heads(live_ref, place_ref, order_ref)
     for head in range(heads):
-        group, slot = group_and_slot(place_ref[head], groups)
+        group, slot = group_and_slot(table_ref[PLACE, head], groups)
         extra = back_ref[group, rows - SPARE :].astype(jnp.float32)
         total = extra[0:1]
         for n in range(1, PARTS):
@@ -434,7 +424,7 @@
     )(*args)
 
 
-def clip_gains(live, back, q_gain, k_gain):
+def clip_gains(table, back, q_gain, k_gain):
     size = lax.axis_size("clip")
     rows = q_gain.shape[0] // BLK
     total = pl.pallas_call(
@@ -442,10 +432,9 @@
         in_specs=[pl.BlockSpec(memory_space=pltpu.SMEM), pl.BlockSpec(memory_space=pltpu.VMEM)],
         out_specs=pl.BlockSpec(memory_space=pltpu.VMEM),
         out_shape=jax.ShapeDtypeStruct((rows, BLK), jnp.float32),
-        scratch_shapes=rank_scratch(rows),
         compiler_params=pltpu.CompilerParams(vmem_limit_bytes=2 << 20),
         name="gains",
-    )(live, back)
+    )(table, back)
     flips = [1, 2, 6]
     for n, flip in enumerate(flips):
         other = lax.ppermute(total, "clip", [(i, i ^ flip) for i in range(size)])
@@ -468,17 +457,17 @@
     heads = key_blocks.shape[1] // groups
     mine = lax.axis_index("seq").reshape(1)
     lists = jnp.transpose(key_blocks[0], (1, 2, 0))
-    packed = pack(
+    packed, table = pack(
         live, query_raw[0], key_raw[0], value[0], upstream[0], query_gain, key_gain, groups, heads
     )
     packed, mine = lax.optimization_barrier((packed, mine))
     arrived = lax.all_to_all(packed, "seq", split_axis=0, concat_axis=0, tiled=True)
-    results = attention(mine, lists, live, arrived, heads)
+    results = attention(mine, table, lists, live, arrived, heads)
     back = lax.all_to_all(results, "seq", split_axis=0, concat_axis=0, tiled=True)
     attended, grad_query, grad_key, grad_value = unpack(
-        live, back, query_raw[0], key_raw[0], query_gain, key_gain
+        table, back, query_raw[0], key_raw[0], query_gain, key_gain
     )
-    q_total, k_total = clip_gains(live, back, query_gain, key_gain)
+    q_total, k_total = clip_gains(table, back, query_gain, key_gain)
     return (
         attended[None],
         grad_query[None],

time: 148 us -> 143 us (0.966)
  Pallas kernels: 26.7 us -> 21.6 us
    pallas_call x1, Pallas kernels: 7.33 us -> 4.68 us  [unpack(): pl.pallas_call(unpack_kernel, in_specs=[pl.BlockSpec(memory_space=pltpu.S...]
    pallas_call x2, Pallas kernels: 17.2 us -> 15.6 us  [the longest x1 11 us: attention(): pl.pallas_call(attention_kernel, in_specs=[smem, smem, smem, smem, vmem],...]
  transfers between devices with their start and end apart: 3 -> 3, of which waited for: 2 -> 2; matrix products, arithmetic and copies ran while one was open for 0% -> 0% of each run, Pallas kernels for 5% -> 3%
where the time goes in v5:
time: 143 us
  blocking collectives  113 us (79%)
  Pallas kernels  21.6 us (15%)
  starting transfers between devices  4.43 us (3%)
  waiting for transfers between devices  3.45 us (2%)
    all_to_all x1, blocking collectives, shards(): lax.all_to_all(packed, 'seq', split_axis=0, concat_axis=0, tiled=True)  58.6 us
    all_to_all x1, blocking collectives, shards(): lax.all_to_all(results, 'seq', split_axis=0, concat_axis=0, tiled=True)  54 us
    pallas_call x1, Pallas kernels, attention(): pl.pallas_call(attention_kernel, in_specs=[smem, smem, smem, smem, vmem],...  11 us
    pallas_call x1, Pallas kernels, unpack(): pl.pallas_call(unpack_kernel, in_specs=[pl.BlockSpec(memory_space=pltpu.S...  4.68 us
    pallas_call x1, Pallas kernels, pack(): pl.pallas_call(pack_kernel, in_specs=[hbm] * 7, out_specs=[vmem, pl.Block...  4.62 us
    ppermute x3, starting transfers between devices, clip_gains(): other = lax.ppermute(total, 'clip', [(i, i ^ flip) for i in range(size)])  4.43 us
    ppermute x3, waiting for transfers between devices, clip_gains(): other = lax.ppermute(total, 'clip', [(i, i ^ flip) for i in range(size)])  3.45 us
  transfers between devices with their start and end apart: 3, of which 2 were waited for; matrix products, arithmetic and copies ran while one was open for 0% of the time, Pallas kernels for 3%

profile of v5, /device:TPU:0, one launch (start us, length us, event | category | flops | bytes accessed | tf_op | source)
XLA Modules:
  0.0 142.8 jit_solution(5698068124862232373)
XLA Ops:
  0.6 4.6 %pack.1 = (bf16[16,512,256]{2,1,0:T(8,128)(2,1)S(1)}, s32[2,32]{1,0:T(2,128)S(1)}) custom-call(s32[1,32]{1,0:T(1,128)} %live_ref.1, bf16[128,4096]{1,0:T(8,128)(2,1)} %bitcast.18, bf16[128,4096]{1,0:T(8,128)(2,1)} %bitcast.20, bf16[128,4096]{1,0:T(8,128)(2,1)} %bitcast.29, bf16[128,4096]{1,0:T(8,128)(2,1)} %bitcast.30, f32[1,4096]{1,0:T(1,128)} %bitcast.22, ...), custom_call_target="tpu_custom_call" | custom-call | tf_op jit(solution)/shard_map/pack/pallas_call | solution.py:149
  5.3 0.0 copy-start.4
  5.3 0.0 copy-start.5
  5.3 58.6 %all_to_all.10.in_ref = bf16[16,512,256]{2,1,0:T(8,128)(2,1)S(1)} all-to-all(bf16[16,512,256]{2,1,0:T(8,128)(2,1)S(1)} %get-tuple-element.19), channel_id=1, replica_groups=mesh['clip'=8,'seq'=16] {'seq'}, dimensions={0} | all-to-all | bytes 8388608 | tf_op jit(solution)/shard_map/all_to_all | solution.py:464
  63.9 0.0 copy-done.4
  63.9 0.0 copy-done.5
  63.9 11.0 %attention.1 = bf16[16,520,256]{2,1,0:T(8,128)(2,1)S(1)} custom-call(s32[1]{0:T(128)} %bitcast.6.mine_ref, s32[2,32]{1,0:T(2,128)S(1)} %get-tuple-element.16.table_ref, s32[16,4,32]{2,1,0:T(4,128)S(1)} %bitcast.28, s32[1,32]{1,0:T(1,128)S(1)} %copy-done.5, bf16[16,512,256]{2,1,0:T(8,128)(2,1)S(1)} %all_to_all.10.in_ref), custom_call_target="tpu_custom_call" | custom-call | tf_op jit(solution)/shard_map/attention/pallas_call | solution.py:295
  75.0 54.0 %all_to_all.11.back_ref = bf16[16,520,256]{2,1,0:T(8,128)(2,1)S(1)} all-to-all(bf16[16,520,256]{2,1,0:T(8,128)(2,1)S(1)} %attention.1), channel_id=1, replica_groups=mesh['clip'=8,'seq'=16] {'seq'}, dimensions={0} | all-to-all | bytes 8519680 | tf_op jit(solution)/shard_map/all_to_all | solution.py:466
  128.9 0.0 copy-start
  128.9 0.0 copy-start.1
  128.9 0.0 copy-start.2
  128.9 0.0 copy-start.3
  128.9 0.7 gains.1.a_ref
  129.6 0.1 collective-permute-start
  129.7 1.2 collective-permute-done.b_ref
  130.9 1.5 %collective-permute-start.1 = (f32[32,128]{1,0:T(8,128)S(1)}, f32[32,128]{1,0:T(8,128)S(1)}, u32[]{:S(2)}, u32[]{:S(2)}) collective-permute-start(f32[32,128]{1,0:T(8,128)S(1)} %add.2.a_ref), channel_id=1, source_target_pairs={{0,32},{16,48},{32,0},{48,16},{64,96},{80,112},{96,64},{112,80},{1... | collective-permute-start | bytes 49160 | tf_op jit(solution)/shard_map/ppermute | solution.py:440
  132.3 2.3 %collective-permute-done.1.b_ref = f32[32,128]{1,0:T(8,128)S(1)} collective-permute-done((f32[32,128]{1,0:T(8,128)S(1)}, f32[32,128]{1,0:T(8,128)S(1)}, u32[]{:S(2)}, u32[]{:S(2)}) %collective-permute-start.1) | collective-permute-done | bytes 16416 | tf_op jit(solution)/shard_map/ppermute | solution.py:440
  134.6 2.9 %collective-permute-start.2 = (f32[32,128]{1,0:T(8,128)S(1)}, f32[32,128]{1,0:T(8,128)S(1)}, u32[]{:S(2)}, u32[]{:S(2)}) collective-permute-start(f32[32,128]{1,0:T(8,128)S(1)} %add.3.a_ref), channel_id=1, source_target_pairs={{0,96},{16,112},{32,64},{48,80},{64,32},{80,48},{96,0},{112,16},{1... | collective-permute-start | bytes 49160 | tf_op jit(solution)/shard_map/ppermute | solution.py:440
  137.5 0.0 copy-done
  137.5 0.0 copy-done.1
  137.5 0.0 copy-done.2
  137.5 0.0 copy-done.3
  137.5 4.7 %unpack.1 = (bf16[128,4096]{1,0:T(8,128)(2,1)}, bf16[128,4096]{1,0:T(8,128)(2,1)}, bf16[128,4096]{1,0:T(8,128)(2,1)}, bf16[128,4096]{1,0:T(8,128)(2,1)}) custom-call(s32[2,32]{1,0:T(2,128)S(1)} %get-tuple-element.16.table_ref, bf16[16,520,256]{2,1,0:T(8,128)(2,1)S(1)} %all_to_all.11.back_ref, bf16[128,4096]{1,0:T(8,128)(2,1)S(1)} %bitcast.19, ...), custom_call_target="tpu_custom_call" | custom-call | tf_op jit(solution)/shard_map/unpack/pallas_call | solution.py:379
  142.2 0.0 collective-permute-done.2.b_ref
  142.2 0.6 last.1
  (2 shorter events, 0.0 us)
Async XLA Ops:
  5.3 58.7 %copy-start.4 = (s32[1,32,16,4]{1,3,2,0:T(4,128)S(1)}, s32[1,32,16,4]{1,3,2,0:T(4,128)}, u32[]{:S(2)}) copy-start(s32[1,32,16,4]{1,3,2,0:T(4,128)} %param.14) | copy-start | bytes 24580
  5.3 58.7 %copy-start.5 = (s32[1,32]{1,0:T(1,128)S(1)}, s32[1,32]{1,0:T(1,128)}, u32[]{:S(2)}) copy-start(s32[1,32]{1,0:T(1,128)} %live_ref.1) | copy-start | bytes 388
  128.9 8.6 %copy-start = (bf16[1,128,4096]{2,1,0:T(8,128)(2,1)S(1)}, bf16[1,128,4096]{2,1,0:T(8,128)(2,1)}, u32[]{:S(2)}) copy-start(bf16[1,128,4096]{2,1,0:T(8,128)(2,1)} %param.8) | copy-start | bytes 3145732
  128.9 8.6 %copy-start.1 = (bf16[1,128,4096]{2,1,0:T(8,128)(2,1)S(1)}, bf16[1,128,4096]{2,1,0:T(8,128)(2,1)}, u32[]{:S(2)}) copy-start(bf16[1,128,4096]{2,1,0:T(8,128)(2,1)} %param.9) | copy-start | bytes 3145732
  128.9 8.6 %copy-start.2 = (f32[4096]{0:T(1024)S(1)}, f32[4096]{0:T(1024)}, u32[]{:S(2)}) copy-start(f32[4096]{0:T(1024)} %param.12) | copy-start | bytes 49156
  128.9 8.6 %copy-start.3 = (f32[4096]{0:T(1024)S(1)}, f32[4096]{0:T(1024)}, u32[]{:S(2)}) copy-start(f32[4096]{0:T(1024)} %param.13) | copy-start | bytes 49156
  129.6 1.3 collective-permute-start
  130.9 3.7 %collective-permute-start.1 = (f32[32,128]{1,0:T(8,128)S(1)}, f32[32,128]{1,0:T(8,128)S(1)}, u32[]{:S(2)}, u32[]{:S(2)}) collective-permute-start(f32[32,128]{1,0:T(8,128)S(1)} %add.2.a_ref), channel_id=1, source_target_pairs={{0,32},{16,48},{32,0},{48,16},{64,96},{80,112},{96,64},{112,80},{1... | collective-permute-start | bytes 49160 | tf_op jit(solution)/shard_map/ppermute | solution.py:440
  134.6 7.6 %collective-permute-start.2 = (f32[32,128]{1,0:T(8,128)S(1)}, f32[32,128]{1,0:T(8,128)S(1)}, u32[]{:S(2)}, u32[]{:S(2)}) collective-permute-start(f32[32,128]{1,0:T(8,128)S(1)} %add.3.a_ref), channel_id=1, source_target_pairs={{0,96},{16,112},{32,64},{48,80},{64,32},{80,48},{96,0},{112,16},{1... | collective-permute-start | bytes 49160 | tf_op jit(solution)/shard_map/ppermute | solution.py:440

commit v6 on v2

v6 whole, which is shorter than its diff:
```python
import jax
import jax.numpy as jnp
from jax import lax
from jax.experimental import pallas as pl
from jax.experimental.pallas import tpu as pltpu
from jax.sharding import PartitionSpec as P

BLK = 128
EPSILON = 1e-06
ROWS = 64
CHUNKS = 2
PARTS = 3
SPARE = 8
UNROLL = 4
QUERY, COTANGENT, KEY, VALUE = range(4)
GRAD_Q, OUT, GRAD_K, GRAD_V = range(4)
LOG2E = 1.4426950408889634


def contract(a, b, dims):
    return lax.dot_general(a, b, (dims, ((), ())), preferred_element_type=jnp.float32)


def inverse_rms(x):
    return lax.rsqrt(jnp.mean(x * x, axis=-1, keepdims=True) + EPSILON)


def pack_kernel(
    q_hbm, k_hbm, v_hbm, u_hbm, qg_hbm, kg_hbm, out_ref, raw_ref, gain_ref, raw_sems, gain_sems, copy_sems
):
    groups, span, both = out_ref.shape
    width = both // 2
    tokens = raw_ref.shape[1]
    heads = span // (2 * tokens)
    step = tokens // CHUNKS

    loads = [
        [
            pltpu.make_async_copy(
                hbm.at[pl.ds(c * step, step)],
                raw_ref.at[n, pl.ds(c * step, step)],
                raw_sems.at[n, c],
            )
            for c in range(CHUNKS)
        ]
        for n, hbm in enumerate((q_hbm, k_hbm))
    ]
    gain_loads = [
        pltpu.make_async_copy(hbm, gain_ref.at[n], gain_sems.at[n])
        for n, hbm in enumerate((qg_hbm, kg_hbm))
    ]
    for n in range(2):
        gain_loads[n].start()
        loads[n][0].start()
    for c in range(1, CHUNKS):
        for n in range(2):
            loads[n][c].start()
    moves = []
    for group in range(groups):
        for head in range(heads):
            at = (group * heads + head) * width
            for n, (hbm, pair) in enumerate(((u_hbm, 0), (v_hbm, 1))):
                first = (pair * heads + head) * tokens
                moves.append(
                    pltpu.make_async_copy(
                        hbm.at[:, pl.ds(at, width)],
                        out_ref.at[group, pl.ds(first, tokens), pl.ds(width, width)],
                        copy_sems.at[group * heads + head, n],
                    )
                )
    for move in moves:
        move.start()
    for c in range(CHUNKS):
        for n in range(2):
            if c == 0:
                gain_loads[n].wait()
            loads[n][c].wait()

            def some_rows(i, carry):
                row = pl.multiple_of(c * step + i * ROWS, ROWS)
                x = raw_ref[n, pl.ds(row, ROWS)].astype(jnp.float32)
                y = (x * inverse_rms(x) * gain_ref[n]).astype(jnp.bfloat16)
                for group in range(groups):
                    for head in range(heads):
                        at = (group * heads + head) * width
                        first = (n * heads + head) * tokens
                        out_ref[group, pl.ds(first + row, ROWS), :width] = y[:, at : at + width]
                return carry

            lax.fori_loop(0, step // ROWS, some_rows, 0)
    for move in moves:
        move.wait()


def in_hbm(x):
    return pltpu.with_memory_space_constraint(x, pltpu.HBM)


def pack(q, k, v, u, q_gain, k_gain, groups, heads):
    tokens, features = q.shape
    width = features // (groups * heads)
    hbm = pl.BlockSpec(memory_space=pltpu.HBM)
    vmem = pl.BlockSpec(memory_space=pltpu.VMEM)
    return pl.pallas_call(
        pack_kernel,
        in_specs=[hbm] * 6,
        out_specs=vmem,
        out_shape=jax.ShapeDtypeStruct((groups, 2 * heads * tokens, 2 * width), jnp.bfloat16),
        scratch_shapes=[
            pltpu.VMEM((2, tokens, features), jnp.bfloat16),
            pltpu.VMEM((2, 1, features), jnp.float32),
            pltpu.SemaphoreType.DMA((2, CHUNKS)),
            pltpu.SemaphoreType.DMA((2,)),
            pltpu.SemaphoreType.DMA((groups * heads, 2)),
        ],
        compiler_params=pltpu.CompilerParams(vmem_limit_bytes=12 << 20),
        name="pack",
    )(*(in_hbm(x) for x in (q, k, v, u, q_gain[None], k_gain[None])))


def head_pass(owner, lists_ref, live_ref, source, put_query, put_key, scratch, after_step, after_keys):
    turned_ref, sums_ref, ahead_ref, sum_ref = scratch
    blocks, both, _ = turned_ref.shape
    width = both // 2
    scale = width ** (-0.5)
    query_rows, key_rows = source

    def prepare(j, carry):
        turned_ref[j] = key_rows(j).T
        sums_ref[j] = jnp.zeros((BLK, both), jnp.float32)
        return carry

    lax.fori_loop(0, blocks, prepare, 0, unroll=4)

    def softmax(scores, grads):
        factor = scale * LOG2E
        top = scores[0]
        for s in scores[1:]:
            top = jnp.maximum(top, s)
        top = jnp.max(top, axis=0, keepdims=True) * factor
        raised = [jnp.exp2(s * factor - top) for s in scores]
        total = raised[0]
        inner = raised[0] * grads[0]
        for e, g in zip(raised[1:], grads[1:]):
            total = total + e
            inner = inner + e * g
        inverse = 1.0 / jnp.sum(total, axis=0, keepdims=True)
        delta = jnp.sum(inner, axis=0, keepdims=True) * inverse
        probs = [e * inverse for e in raised]
        low = [p.astype(jnp.bfloat16) for p in probs]
        ds = [(p * ((g - delta) * scale)).astype(jnp.bfloat16) for p, g in zip(probs, grads)]
        return low, ds

    def finish_block(b, slots, low, ds):
        rows = query_rows(b)
        q, u = rows[:, :width], rows[:, width:]
        chosen = [lists_ref[b, s, owner] for s in range(slots)]
        keys = jnp.concatenate([turned_ref[j, :width] for j in chosen], axis=1)
        values = jnp.concatenate([turned_ref[j, width:] for j in chosen], axis=1)
        ds_all = jnp.concatenate(ds, axis=0)
        low_all = jnp.concatenate(low, axis=0)
        out_t = contract(values, low_all, ((1,), (0,)))
        dq_t = contract(keys, ds_all, ((1,), (0,)))
        more_k = contract(ds_all, q, ((1,), (0,)))
        more_v = contract(low_all, u, ((1,), (0,)))
        old = [sums_ref[j] for j in chosen]
        for s, (j, o) in enumerate(zip(chosen, old)):
            sums_ref[j, :, :width] = o[:, :width] + more_k[s * BLK : (s + 1) * BLK]
            sums_ref[j, :, width:] = o[:, width:] + more_v[s * BLK : (s + 1) * BLK]
        dq = dq_t.astype(jnp.bfloat16).T
        put_query(b, dq, out_t.astype(jnp.bfloat16).T)
        return jnp.sum(dq.astype(jnp.float32) * q.astype(jnp.float32), axis=0, keepdims=True)

    for slots in (2, 3, 4):

        @pl.when(live_ref[0, owner] == slots)
        def _():
            def step(i, gain):
                for k in range(UNROLL):
                    b = UNROLL * i + k
                    scores, grads = [
                        [ahead_ref[k % 2, n, s] for s in range(slots)] for n in range(2)
                    ]
                    start_at(b + 1, (k + 1) % 2, slots)
                    low, ds = softmax(scores, grads)
                    gain = gain + finish_block(b, slots, low, ds)
                after_step(i)
                return gain

            def start_at(b, side, slots):
                b = jnp.minimum(b, blocks - 1)
                rows = query_rows(b)
                keys = jnp.concatenate(
                    [key_rows(lists_ref[b, s, owner]) for s in range(slots)], axis=0
                )
                scores = contract(keys[:, :width], rows[:, :width], ((1,), (1,)))
                grads = contract(keys[:, width:], rows[:, width:], ((1,), (1,)))
                for s in range(slots):
                    ahead_ref[side, 0, s] = scores[s * BLK : (s + 1) * BLK]
                    ahead_ref[side, 1, s] = grads[s * BLK : (s + 1) * BLK]

            start_at(0, 0, slots)
            sum_ref[...] = lax.fori_loop(
                0, blocks // UNROLL, step, jnp.zeros((1, width), jnp.float32)
            )

    def finish(i, carry):
        for k in range(UNROLL):
            j = UNROLL * i + k
            put_key(j, sums_ref[j].astype(jnp.bfloat16))
        after_keys(i)
        return carry

    lax.fori_loop(0, blocks // UNROLL, finish, 0)


def first_head_kernel(
    mine_ref, lists_ref, live_ref, in_ref, out_hbm, rest_hbm, keys_hbm, sum_ref, *scratch
):
    *scratch, out_ref, keys_ref, sems, out_sems, keys_sems = scratch
    moves = [
        pltpu.make_async_copy(
            in_ref.at[:, pl.ds(source * BLK, BLK)], rest_hbm.at[:, pl.ds(n * BLK, BLK)], sems.at[n]
        )
        for n, source in enumerate((1, 3))
    ]
    for move in moves:
        move.start()

    def put_query(b, dq, out):
        width = dq.shape[1]
        out_ref[b, :, :width] = dq
        out_ref[b, :, width:] = out

    def put_key(j, grads):
        keys_ref[j] = grads

    def store(i, ref, hbm, sems):
        at = pl.multiple_of(i * UNROLL, UNROLL)
        return pltpu.make_async_copy(ref.at[pl.ds(at, UNROLL)], hbm.at[pl.ds(at, UNROLL)], sems.at[i])

    source = (lambda b: in_ref[b, :BLK], lambda j: in_ref[j, 2 * BLK : 3 * BLK])
    head_pass(
        2 * mine_ref[0],
        lists_ref,
        live_ref,
        source,
        put_query,
        put_key,
        (*scratch, sum_ref),
        lambda i: store(i, out_ref, out_hbm, out_sems).start(),
        lambda i: store(i, keys_ref, keys_hbm, keys_sems).start(),
    )
    for i in range(in_ref.shape[0] // UNROLL):
        store(i, out_ref, out_hbm, out_sems).wait()
        store(i, keys_ref, keys_hbm, keys_sems).wait()
    for move in moves:
        move.wait()


def second_head_kernel(
    mine_ref, lists_ref, live_ref, in_ref, keys_hbm, before_ref, out_ref, sums_ref, *scratch
):
    *scratch, sum_ref, sems = scratch
    move = pltpu.make_async_copy(keys_hbm, out_ref.at[:, pl.ds(0, BLK)], sems.at[0])
    move.start()

    def put_query(b, dq, out):
        width = dq.shape[1]
        out_ref[b, BLK : 2 * BLK, :width] = dq
        out_ref[b, BLK : 2 * BLK, width:] = out

    def put_key(j, grads):
        out_ref[j, 2 * BLK : 3 * BLK] = grads

    source = (lambda b: in_ref[b, :BLK], lambda j: in_ref[j, BLK : 2 * BLK])
    head_pass(
        2 * mine_ref[0] + 1,
        lists_ref,
        live_ref,
        source,
        put_query,
        put_key,
        (*scratch, sum_ref),
        lambda i: None,
        lambda i: None,
    )
    sums_ref[0:1] = before_ref[...]
    sums_ref[1:2] = sum_ref[...]
    move.wait()


def head_scratch(blocks, both, slots):
    return [
        pltpu.VMEM((blocks, both, BLK), jnp.bfloat16),
        pltpu.VMEM((blocks, BLK, both), jnp.float32),
        pltpu.VMEM((2, 2, slots, BLK, BLK), jnp.float32),
    ]


def first_head(mine, lists, live, arrived):
    blocks, _, both = arrived.shape
    vmem = pl.BlockSpec(memory_space=pltpu.VMEM)
    smem = pl.BlockSpec(memory_space=pltpu.SMEM)
    hbm = pl.BlockSpec(memory_space=pltpu.HBM)
    return pl.pallas_call(
        first_head_kernel,
        in_specs=[smem, smem, smem, vmem],
        out_specs=[hbm, hbm, hbm, vmem],
        out_shape=[
            pltpu.HBM((blocks, BLK, both), jnp.bfloat16),
            pltpu.HBM((blocks, 2 * BLK, both), jnp.bfloat16),
            pltpu.HBM((blocks, BLK, both), jnp.bfloat16),
            jax.ShapeDtypeStruct((1, both // 2), jnp.float32),
        ],
        scratch_shapes=head_scratch(blocks, both, lists.shape[1])
        + [
            pltpu.VMEM((blocks, BLK, both), jnp.bfloat16),
            pltpu.VMEM((blocks, BLK, both), jnp.bfloat16),
            pltpu.SemaphoreType.DMA((2,)),
            pltpu.SemaphoreType.DMA((blocks // UNROLL,)),
            pltpu.SemaphoreType.DMA((blocks // UNROLL,)),
        ],
        compiler_params=pltpu.CompilerParams(vmem_limit_bytes=20 << 20),
        name="first_head",
    )(mine, lists, live, arrived)


def second_head(mine, lists, live, rest, keys, before):
    blocks, _, both = rest.shape
    vmem = pl.BlockSpec(memory_space=pltpu.VMEM)
    smem = pl.BlockSpec(memory_space=pltpu.SMEM)
    return pl.pallas_call(
        second_head_kernel,
        in_specs=[smem, smem, smem, vmem, pl.BlockSpec(memory_space=pltpu.HBM), vmem],
        out_specs=[vmem] * 2,
        out_shape=[
            jax.ShapeDtypeStruct((blocks, 3 * BLK + SPARE, both), jnp.bfloat16),
            jax.ShapeDtypeStruct((2, both // 2), jnp.float32),
        ],
        scratch_shapes=head_scratch(blocks, both, lists.shape[1])
        + [pltpu.VMEM((1, both // 2), jnp.float32), pltpu.SemaphoreType.DMA((1,))],
        compiler_params=pltpu.CompilerParams(vmem_limit_bytes=20 << 20),
        name="second_head",
    )(mine, lists, live, rest, in_hbm(keys), before)


def add_kernel(a_ref, b_ref, out_ref):
    out_ref[...] = a_ref[...] + b_ref[...]


def add(a, b):
    vmem = pl.BlockSpec(memory_space=pltpu.VMEM)
    return pl.pallas_call(
        add_kernel,
        in_specs=[vmem] * 2,
        out_specs=vmem,
        out_shape=jax.ShapeDtypeStruct(a.shape, a.dtype),
        compiler_params=pltpu.CompilerParams(vmem_limit_bytes=1 << 20),
        name="add",
    )(a, b)


def attach_kernel(a_ref, b_ref, given_ref, out_ref, extra_ref, sems):
    del given_ref
    total = a_ref[...] + b_ref[...]
    row = jnp.concatenate([total[n : n + 1] for n in range(total.shape[0])], axis=1)
    pieces = []
    for _ in range(PARTS):
        pieces.append(row.astype(jnp.bfloat16))
        row = row - pieces[-1].astype(jnp.float32)
    pieces.append(jnp.zeros((SPARE - PARTS, row.shape[1]), jnp.bfloat16))
    extra_ref[...] = jnp.concatenate(pieces, axis=0)
    moves = [
        pltpu.make_async_copy(extra_ref, out_ref.at[j, pl.ds(3 * BLK, SPARE)], sems.at[j])
        for j in range(out_ref.shape[0])
    ]
    for move in moves:
        move.start()
    for move in moves:
        move.wait()


def attach(a, b, results):
    vmem = pl.BlockSpec(memory_space=pltpu.VMEM)
    anywhere = pl.BlockSpec(memory_space=pl.ANY)
    return pl.pallas_call(
        attach_kernel,
        in_specs=[vmem, vmem, anywhere],
        out_specs=anywhere,
        out_shape=jax.ShapeDtypeStruct(results.shape, results.dtype),
        scratch_shapes=[
            pltpu.VMEM((SPARE, results.shape[2]), results.dtype),
            pltpu.SemaphoreType.DMA((results.shape[0],)),
        ],
        input_output_aliases={2: 0},
        compiler_params=pltpu.CompilerParams(vmem_limit_bytes=1 << 20),
        name="attach",
    )(a, b, results)


def unpack_kernel(
    first_ref,
    back_ref,
    q_ref,
    k_ref,
    qg_ref,
    kg_ref,
    qr_ref,
    kr_ref,
    out_hbm,
    dq_hbm,
    dk_hbm,
    dv_hbm,
    q_total_ref,
    k_total_ref,
    done_ref,
    sems,
    copy_sems,
):
    groups, _, both = back_ref.shape
    width = both // 2
    tokens, features = q_ref.shape
    step = tokens // CHUNKS
    places = (((first_ref, 0), (back_ref, tokens)), ((back_ref, 0), (back_ref, 2 * tokens)))
    moves = []
    for group in range(groups):
        for head in range(2):
            at = (2 * group + head) * width
            for n, hbm in enumerate((out_hbm, dv_hbm)):
                ref, row = places[n][head]
                moves.append(
                    pltpu.make_async_copy(
                        ref.at[group, pl.ds(row, tokens), pl.ds(width, width)],
                        hbm.at[:, pl.ds(at, width)],
                        copy_sems.at[2 * group + head, n],
                    )
                )
    for move in moves:
        move.start()
    for c in range(CHUNKS):
        for n, (raw_ref, gain_ref, hbm) in enumerate(
            ((q_ref, qg_ref, dq_hbm), (k_ref, kg_ref, dk_hbm))
        ):

            def some_rows(i, carry):
                row = pl.multiple_of(c * step + i * ROWS, ROWS)
                x = raw_ref[pl.ds(row, ROWS)].astype(jnp.float32)
                inverse = inverse_rms(x)
                unit = x * inverse
                pieces = []
                for group in range(groups):
                    for ref, first in places[n]:
                        pieces.append(ref[group, pl.ds(first + row, ROWS), :width])
                g = jnp.concatenate(pieces, axis=-1).astype(jnp.float32) * gain_ref[...]
                mean = jnp.mean(g * unit, axis=-1, keepdims=True)
                done_ref[n, pl.ds(row, ROWS)] = (inverse * (g - unit * mean)).astype(jnp.bfloat16)
                return carry

            lax.fori_loop(0, step // ROWS, some_rows, 0)
            move = pltpu.make_async_copy(
                done_ref.at[n, pl.ds(c * step, step)], hbm.at[pl.ds(c * step, step)], sems.at[n, c]
            )
            move.start()
            moves.append(move)
    rows = []
    for group in range(groups):
        extra = back_ref[group, 3 * tokens :].astype(jnp.float32)
        total = extra[0:1]
        for n in range(1, PARTS):
            total = total + extra[n : n + 1]
        rows += [total[:, :width], total[:, width:]]
    total = jnp.concatenate(rows, axis=0)
    q_total_ref[...] = total / qr_ref[...]
    k_total_ref[...] = total / kr_ref[...]
    for move in moves:
        move.wait()


def unpack(first, back, q, k, q_gain, k_gain):
    tokens, features = q.shape
    hbm = pl.BlockSpec(memory_space=pltpu.HBM)
    vmem = pl.BlockSpec(memory_space=pltpu.VMEM)
    rows = features // BLK
    results = pl.pallas_call(
        unpack_kernel,
        in_specs=[vmem] * 8,
        out_specs=[hbm] * 4 + [vmem] * 2,
        out_shape=[jax.ShapeDtypeStruct((tokens, features), jnp.bfloat16)] * 4
        + [jax.ShapeDtypeStruct((rows, BLK), jnp.float32)] * 2,
        scratch_shapes=[
            pltpu.VMEM((2, tokens, features), jnp.bfloat16),
            pltpu.SemaphoreType.DMA((2, CHUNKS)),
            pltpu.SemaphoreType.DMA((rows, 2)),
        ],
        compiler_params=pltpu.CompilerParams(vmem_limit_bytes=14 << 20),
        name="unpack",
    )(
        first,
        back,
        q,
        k,
        q_gain[None],
        k_gain[None],
        q_gain.reshape(rows, BLK),
        k_gain.reshape(rows, BLK),
    )
    return (*results[:4], results[4].reshape(-1), results[5].reshape(-1))


def shards(query_raw, key_raw, value, upstream, query_gain, key_gain, key_blocks, live):
    groups = lax.axis_size("seq")
    clips = lax.axis_size("clip")
    heads = key_blocks.shape[1] // groups
    mine = lax.axis_index("seq").reshape(1)
    lists = jnp.transpose(key_blocks[0], (1, 2, 0))
    packed = pack(
        query_raw[0], key_raw[0], value[0], upstream[0], query_gain, key_gain, groups, heads
    )
    packed, mine = lax.optimization_barrier((packed, mine))
    arrived = lax.all_to_all(packed, "seq", split_axis=0, concat_axis=0, tiled=True)
    first, rest, keys, before = first_head(mine, lists, live, arrived)
    first_back = lax.all_to_all(first, "seq", split_axis=0, concat_axis=0, tiled=True)
    results, total = second_head(mine, lists, live, rest, keys, before)
    flips = [1, 2, 6]
    for n, flip in enumerate(flips):
        other = lax.ppermute(total, "clip", [(i, i ^ flip) for i in range(clips)])
        if n < len(flips) - 1:
            total = add(total, other)
    results = attach(total, other, results)
    back = lax.all_to_all(results, "seq", split_axis=0, concat_axis=0, tiled=True)
    attended, grad_query, grad_key, grad_value, q_total, k_total = unpack(
        first_back, back, query_raw[0], key_raw[0], query_gain, key_gain
    )
    return (
        attended[None],
        grad_query[None],
        grad_key[None],
        grad_value[None],
        q_total,
        k_total,
    )


def solution(mesh):
    tokens = P("clip", "seq", None)
    return jax.shard_map(
        shards,
        mesh=mesh,
        in_specs=(tokens,) * 4 + (P(), P(), P("clip", None, None, None), P("clip", None)),
        out_specs=(tokens,) * 4 + (P(), P()),
        check_vma=False,
    )
```

time: 149 us -> 145 us (0.973)
  blocking collectives: 114 us -> 104 us
  starting transfers between devices: 4.24 us -> 8.76 us
  Pallas kernels: 26.8 us -> 23.4 us
  waiting for transfers between devices: 3.09 us -> 5.49 us
  local copies, waits for them, and re-layouts: 0.03 us -> 1.62 us
    all_to_all x1, blocking collectives: 55.7 us -> 45.8 us  [shards(): lax.all_to_all(results, 'seq', split_axis=0, concat_axis=0, tiled=True)]
    all_to_all x0 -> x1, starting transfers between devices: none -> 4.36 us  [shards(): lax.all_to_all(first, 'seq', split_axis=0, concat_axis=0, tiled=True)]
    ppermute x3, waiting for transfers between devices: 3.09 us -> 5.49 us  [shards(): other = lax.ppermute(total, 'clip', [(i, i ^ flip) for i in range(clips)])]
    pallas_call x6, Pallas kernels: 21.7 us -> 19.7 us  [the longest x1 8.02 us: first_head(): pl.pallas_call(first_head_kernel, in_specs=[smem, smem, smem, vmem], out_...]
    unnamed x12 -> x14, local copies, waits for them, and re-layouts: 0.03 us -> 1.62 us
  transfers between devices with their start and end apart: 3 -> 4, of which waited for: 2 -> 3; matrix products, arithmetic and copies ran while one was open for 0% -> 0% of each run, Pallas kernels for 4% -> 4%
where the time goes in v6:
time: 145 us
  blocking collectives  104 us (72%)
  Pallas kernels  23.4 us (16%)
  starting transfers between devices  8.76 us (6%)
  waiting for transfers between devices  5.49 us (4%)
  local copies, waits for them, and re-layouts  1.62 us (1%)
    all_to_all x1, blocking collectives, shards(): lax.all_to_all(packed, 'seq', split_axis=0, concat_axis=0, tiled=True)  58.6 us
    all_to_all x1, blocking collectives, shards(): lax.all_to_all(results, 'seq', split_axis=0, concat_axis=0, tiled=True)  45.8 us
    pallas_call x1, Pallas kernels, first_head(): pl.pallas_call(first_head_kernel, in_specs=[smem, smem, smem, vmem], out_...  8.02 us
    pallas_call x1, Pallas kernels, unpack(): pl.pallas_call(unpack_kernel, in_specs=[vmem] * 8, out_specs=[hbm] * 4 +...  5.79 us
    pallas_call x1, Pallas kernels, second_head(): pl.pallas_call(second_head_kernel, in_specs=[smem, smem, smem, vmem, pl.B...  5.59 us
    ppermute x3, waiting for transfers between devices, shards(): other = lax.ppermute(total, 'clip', [(i, i ^ flip) for i in range(clips)])  5.49 us
    ppermute x3, starting transfers between devices, shards(): other = lax.ppermute(total, 'clip', [(i, i ^ flip) for i in range(clips)])  4.4 us
    all_to_all x1, starting transfers between devices, shards(): lax.all_to_all(first, 'seq', split_axis=0, concat_axis=0, tiled=True)  4.36 us
  transfers between devices with their start and end apart: 4, of which 3 were waited for; matrix products, arithmetic and copies ran while one was open for 0% of the time, Pallas kernels for 4%

profile of v6, /device:TPU:0, one launch (start us, length us, event | category | flops | bytes accessed | tf_op | source)
XLA Modules:
  0.0 144.6 jit_solution(17415861932664860921)
XLA Ops:
  0.6 3.8 %pack.1 = bf16[16,512,256]{2,1,0:T(8,128)(2,1)S(1)} custom-call(bf16[128,4096]{1,0:T(8,128)(2,1)} %bitcast.18, bf16[128,4096]{1,0:T(8,128)(2,1)} %bitcast.20, bf16[128,4096]{1,0:T(8,128)(2,1)} %bitcast.30, bf16[128,4096]{1,0:T(8,128)(2,1)} %bitcast.31, f32[1,4096]{1,0:T(1,128)} %bitcast.22, f32[1,4096]{1,0:T(1,128)} %bitcast.25), custom_call_target="tpu_custom_call" | custom-call | tf_op jit(solution)/shard_map/pack/pallas_call | solution.py:104
  4.4 0.0 copy-start.5
  4.4 0.0 copy-start.6
  4.4 58.6 %all_to_all.15.in_ref = bf16[16,512,256]{2,1,0:T(8,128)(2,1)S(1)} all-to-all(bf16[16,512,256]{2,1,0:T(8,128)(2,1)S(1)} %pack.1), channel_id=1, replica_groups=mesh['clip'=8,'seq'=16] {'seq'}, dimensions={0} | all-to-all | bytes 8388608 | tf_op jit(solution)/shard_map/all_to_all | solution.py:521
  63.1 0.0 copy-done.5
  63.1 0.0 copy-done.6
  63.1 8.0 %first_head.1 = (bf16[16,128,256]{2,1,0:T(8,128)(2,1)}, bf16[16,256,256]{2,1,0:T(8,128)(2,1)}, bf16[16,128,256]{2,1,0:T(8,128)(2,1)}, f32[1,128]{1,0:T(1,128)S(1)}) custom-call(s32[1]{0:T(128)} %bitcast.6.mine_ref, s32[16,4,32]{2,1,0:T(4,128)S(1)} %bitcast.28, s32[1,32]{1,0:T(1,128)S(1)} %copy-done.6, bf16[16,512,256]{2,1,0:T(8,128)(2,1)S(1)} %all_to_all.15.in_ref), custom_call_target="tpu_custom_call" | custom-call | tf_op jit(solution)/shard_map/first_head/pallas_call | solution.py:306
  71.1 4.4 %all-to-all-start.1 = ((bf16[16,128,256]{2,1,0:T(8,128)(2,1)}), bf16[16,128,256]{2,1,0:T(8,128)(2,1)}, u32[]{:S(2)}, u32[]{:S(2)}) async-start(bf16[16,128,256]{2,1,0:T(8,128)(2,1)} %get-tuple-element.22), calls=%async_computation.1 | async-start | bytes 2097152 | tf_op jit(solution)/shard_map/all_to_all | solution.py:523
  75.5 0.0 copy-start.2
  75.5 1.6 %copy-done.2 = bf16[16,256,256]{2,1,0:T(8,128)(2,1)S(1)} copy-done((bf16[16,256,256]{2,1,0:T(8,128)(2,1)S(1)}, bf16[16,256,256]{2,1,0:T(8,128)(2,1)}, u32[]{:S(2)}) %copy-start.2) | copy-done | bytes 2097176
  77.1 5.6 %second_head.1 = (bf16[16,392,256]{2,1,0:T(8,128)(2,1)S(1)}, f32[2,128]{1,0:T(2,128)S(1)}) custom-call(s32[1]{0:T(128)} %bitcast.6.mine_ref, s32[16,4,32]{2,1,0:T(4,128)S(1)} %bitcast.29, s32[1,32]{1,0:T(1,128)S(1)} %copy-done.6, bf16[16,256,256]{2,1,0:T(8,128)(2,1)S(1)} %copy-done.2, bf16[16,128,256]{2,1,0:T(8,128)(2,1)} %get-tuple-element.24.keys_hbm, ...), custom_call_target="tpu_custom_call" | custom-call | tf_op jit(solution)/shard_map/second_head/pallas_call | solution.py:333
  82.7 0.1 collective-permute-start
  82.8 1.1 collective-permute-done.b_ref
  83.9 0.8 collective-permute-start.1
  84.7 2.8 %collective-permute-done.1.b_ref = f32[2,128]{1,0:T(2,128)S(1)} collective-permute-done((f32[2,128]{1,0:T(2,128)S(1)}, f32[2,128]{1,0:T(2,128)S(1)}, u32[]{:S(2)}, u32[]{:S(2)}) %collective-permute-start.1) | collective-permute-done | bytes 1056 | tf_op jit(solution)/shard_map/ppermute | solution.py:527
  87.5 3.5 %collective-permute-start.2 = (f32[2,128]{1,0:T(2,128)S(1)}, f32[2,128]{1,0:T(2,128)S(1)}, u32[]{:S(2)}, u32[]{:S(2)}) collective-permute-start(f32[2,128]{1,0:T(2,128)S(1)} %add.3.a_ref), channel_id=1, source_target_pairs={{0,96},{16,112},{32,64},{48,80},{64,32},{80,48},{96,0},{112,16},{1... | collective-permute-start | bytes 3080 | tf_op jit(solution)/shard_map/ppermute | solution.py:527
  91.0 1.6 %collective-permute-done.2.b_ref = f32[2,128]{1,0:T(2,128)S(1)} collective-permute-done((f32[2,128]{1,0:T(2,128)S(1)}, f32[2,128]{1,0:T(2,128)S(1)}, u32[]{:S(2)}, u32[]{:S(2)}) %collective-permute-start.2) | collective-permute-done | bytes 1056 | tf_op jit(solution)/shard_map/ppermute | solution.py:527
  92.6 0.3 attach.1
  92.8 0.0 copy-start.3
  92.9 0.0 copy-start.4
  92.9 0.0 all-to-all-done.1.first_ref
  92.9 0.0 copy-start
  92.9 0.0 copy-start.1
  92.9 45.8 %all_to_all.16.back_ref = bf16[16,392,256]{2,1,0:T(8,128)(2,1)S(1)} all-to-all(bf16[16,392,256]{2,1,0:T(8,128)(2,1)S(1)} %attach.1), channel_id=1, replica_groups=mesh['clip'=8,'seq'=16] {'seq'}, dimensions={0} | all-to-all | bytes 6422528 | tf_op jit(solution)/shard_map/all_to_all | solution.py:531
  138.7 0.0 copy-done.3
  138.7 0.0 copy-done.4
  138.7 0.0 copy-done
  138.7 0.0 copy-done.1
  138.7 5.8 %unpack.1 = (bf16[128,4096]{1,0:T(8,128)(2,1)}, bf16[128,4096]{1,0:T(8,128)(2,1)}, bf16[128,4096]{1,0:T(8,128)(2,1)}, bf16[128,4096]{1,0:T(8,128)(2,1)}, f32[32,128]{1,0:T(8,128)}, /*index=5*/f32[32,128]{1,0:T(8,128)}) custom-call(bf16[16,128,256]{2,1,0:T(8,128)(2,1)} %all-to-all-done.1.first_ref, bf16[16,392,256]{2,1,0:T(8,128)(2,1)S(1)} %all_to_all.16.back_ref, ...), custom_call_target="tpu_custom_call" | custom-call | tf_op jit(solution)/shard_map/unpack/pallas_call | solution.py:485
  (2 shorter events, 0.0 us)
Async XLA Ops:
  4.4 58.7 %copy-start.5 = (s32[1,32,16,4]{1,3,2,0:T(4,128)S(1)}, s32[1,32,16,4]{1,3,2,0:T(4,128)}, u32[]{:S(2)}) copy-start(s32[1,32,16,4]{1,3,2,0:T(4,128)} %param.14) | copy-start | bytes 24580
  4.4 58.7 %copy-start.6 = (s32[1,32]{1,0:T(1,128)S(1)}, s32[1,32]{1,0:T(1,128)}, u32[]{:S(2)}) copy-start(s32[1,32]{1,0:T(1,128)} %live_ref.3) | copy-start | bytes 388
  71.1 21.8 %all-to-all-start.1 = ((bf16[16,128,256]{2,1,0:T(8,128)(2,1)}), bf16[16,128,256]{2,1,0:T(8,128)(2,1)}, u32[]{:S(2)}, u32[]{:S(2)}) async-start(bf16[16,128,256]{2,1,0:T(8,128)(2,1)} %get-tuple-element.22), calls=%async_computation.1 | async-start | bytes 2097152 | tf_op jit(solution)/shard_map/all_to_all | solution.py:523
  75.5 1.6 %copy-start.2 = (bf16[16,256,256]{2,1,0:T(8,128)(2,1)S(1)}, bf16[16,256,256]{2,1,0:T(8,128)(2,1)}, u32[]{:S(2)}) copy-start(bf16[16,256,256]{2,1,0:T(8,128)(2,1)} %get-tuple-element.23.in_ref) | copy-start | bytes 6291460
  82.7 1.2 collective-permute-start
  83.9 3.6 %collective-permute-start.1 = (f32[2,128]{1,0:T(2,128)S(1)}, f32[2,128]{1,0:T(2,128)S(1)}, u32[]{:S(2)}, u32[]{:S(2)}) collective-permute-start(f32[2,128]{1,0:T(2,128)S(1)} %add.2.a_ref), channel_id=1, source_target_pairs={{0,32},{16,48},{32,0},{48,16},{64,96},{80,112},{96,64},{112,80},{1... | collective-permute-start | bytes 3080 | tf_op jit(solution)/shard_map/ppermute | solution.py:527
  87.5 5.1 %collective-permute-start.2 = (f32[2,128]{1,0:T(2,128)S(1)}, f32[2,128]{1,0:T(2,128)S(1)}, u32[]{:S(2)}, u32[]{:S(2)}) collective-permute-start(f32[2,128]{1,0:T(2,128)S(1)} %add.3.a_ref), channel_id=1, source_target_pairs={{0,96},{16,112},{32,64},{48,80},{64,32},{80,48},{96,0},{112,16},{1... | collective-permute-start | bytes 3080 | tf_op jit(solution)/shard_map/ppermute | solution.py:527
  92.8 45.8 %copy-start.3 = (f32[4096]{0:T(1024)S(1)}, f32[4096]{0:T(1024)}, u32[]{:S(2)}) copy-start(f32[4096]{0:T(1024)} %param.12) | copy-start | bytes 49156
  92.9 45.8 %copy-start.4 = (f32[4096]{0:T(1024)S(1)}, f32[4096]{0:T(1024)}, u32[]{:S(2)}) copy-start(f32[4096]{0:T(1024)} %param.13) | copy-start | bytes 49156
  92.9 45.8 %copy-start = (bf16[1,128,4096]{2,1,0:T(8,128)(2,1)S(1)}, bf16[1,128,4096]{2,1,0:T(8,128)(2,1)}, u32[]{:S(2)}) copy-start(bf16[1,128,4096]{2,1,0:T(8,128)(2,1)} %param.8) | copy-start | bytes 3145732
  92.9 45.8 %copy-start.1 = (bf16[1,128,4096]{2,1,0:T(8,128)(2,1)S(1)}, bf16[1,128,4096]{2,1,0:T(8,128)(2,1)}, u32[]{:S(2)}) copy-start(bf16[1,128,4096]{2,1,0:T(8,128)(2,1)} %param.9) | copy-start | bytes 3145732

commit v7 on v5

--- a/solution.py
+++ b/solution.py
@@ -27,24 +27,17 @@
 
 def rank_heads(live_ref, table_ref):
     count = table_ref.shape[1]
-    most = lax.fori_loop(0, count, lambda h, n: n + (live_ref[0, h] >= 4).astype(jnp.int32), 0)
-    some = lax.fori_loop(0, count, lambda h, n: n + (live_ref[0, h] >= 3).astype(jnp.int32), 0)
-
-    def put(h, counts):
-        four, three, two = counts
-        is_four = live_ref[0, h] >= 4
-        is_three = jnp.logical_and(live_ref[0, h] >= 3, jnp.logical_not(is_four))
-        rank = jnp.where(is_four, four, jnp.where(is_three, three, two))
+    lives = [live_ref[0, h] for h in range(count)]
+    fours = [(n >= 4).astype(jnp.int32) for n in lives]
+    somes = [(n >= 3).astype(jnp.int32) for n in lives]
+    four, three, two = jnp.int32(0), sum(fours), sum(somes)
+    for h in range(count):
+        rank = jnp.where(fours[h] == 1, four, jnp.where(somes[h] == 1, three, two))
         table_ref[PLACE, h] = rank
         table_ref[ORDER, rank] = h
-        step = jnp.logical_not(jnp.logical_or(is_four, is_three))
-        return (
-            four + is_four.astype(jnp.int32),
-            three + is_three.astype(jnp.int32),
-            two + step.astype(jnp.int32),
-        )
-
-    lax.fori_loop(0, count, put, (jnp.int32(0), most, some))
+        four = four + fours[h]
+        three = three + somes[h] - fours[h]
+        two = two + 1 - somes[h]
 
 
 def group_and_slot(rank, groups):
@@ -168,7 +161,10 @@
     )(*(in_hbm(x) for x in (live, q, k, v, u, q_gain[None], k_gain[None])))
 
 
-def attention_kernel(mine_ref, table_ref, lists_ref, live_ref, in_ref, out_ref, *scratch):
+def attention_kernel(mine_ref, table_ref, live_ref, lists_any, in_ref, out_ref, *scratch):
+    *scratch, lists_ref, lists_sem = scratch
+    lists_load = pltpu.make_async_copy(lists_any, lists_ref, lists_sem)
+    lists_load.start()
     blocks, span, both = in_ref.shape
     heads = len(scratch) // 3
     width = both // 2
@@ -195,6 +191,7 @@
         return carry
 
     lax.fori_loop(0, blocks, prepare, 0, unroll=4)
+    lists_load.wait()
 
     def start(b, head, slots):
         q = in_ref[b, place(0, head), :width]
@@ -294,69 +291,95 @@
     smem = pl.BlockSpec(memory_space=pltpu.SMEM)
     return pl.pallas_call(
         attention_kernel,
-        in_specs=[smem, smem, smem, smem, vmem],
+        in_specs=[smem, smem, smem, pl.BlockSpec(memory_space=pl.ANY), vmem],
         out_specs=vmem,
         out_shape=jax.ShapeDtypeStruct((blocks, span + SPARE, both), jnp.bfloat16),
         scratch_shapes=[pltpu.VMEM((blocks, both, BLK), jnp.bfloat16)] * heads
         + [pltpu.VMEM((blocks, BLK, both), jnp.float32)] * heads
         + [pltpu.VMEM((2, lists.shape[1], BLK, BLK), jnp.float32)] * heads
-        + [pltpu.VMEM((heads, both // 2), jnp.float32)],
+        + [pltpu.VMEM((heads, both // 2), jnp.float32)]
+        + [pltpu.SMEM(lists.shape, jnp.int32), pltpu.SemaphoreType.DMA(())],
         compiler_params=pltpu.CompilerParams(vmem_limit_bytes=24 << 20),
         name="attention",
-    )(mine, table, lists, live, arrived)
+    )(mine, table, live, lists, arrived)
 
 
 def unpack_kernel(
     table_ref,
-    back_ref,
-    q_ref,
-    k_ref,
-    qg_ref,
-    kg_ref,
+    back_hbm,
+    q_hbm,
+    k_hbm,
+    qg_hbm,
+    kg_hbm,
     out_hbm,
     dq_hbm,
     dk_hbm,
     dv_hbm,
+    raw_ref,
+    back_ref,
+    gain_ref,
     done_ref,
+    raw_sems,
+    grad_sems,
+    gain_sems,
     sems,
     copy_sems,
 ):
-    groups, _, both = back_ref.shape
+    groups, _, both = back_hbm.shape
     width = both // 2
-    tokens, features = q_ref.shape
+    tokens, features = q_hbm.shape
     heads = features // (groups * width)
     step = tokens // CHUNKS
-    moves, spots = [], []
-    for head in range(groups * heads):
-        group, slot = group_and_slot(table_ref[PLACE, head], groups)
-        spots.append((group, slot))
-        for n, hbm in enumerate((out_hbm, dv_hbm)):
+    loads = {}
+    for n, raw_hbm in enumerate((q_hbm, k_hbm)):
+        for c in range(CHUNKS):
+            rows = pl.ds(c * step, step)
+            some = [
+                pltpu.make_async_copy(raw_hbm.at[rows], raw_ref.at[n, rows], raw_sems.at[n, c])
+            ]
+            for slot in range(heads):
+                some.append(
+                    pltpu.make_async_copy(
+                        back_hbm.at[:, pl.ds((n * heads + slot) * tokens + c * step, step)],
+                        back_ref.at[:, pl.ds((n * heads + slot) * tokens + c * step, step)],
+                        grad_sems.at[n, c, slot],
+                    )
+                )
+            if c == 0:
+                gain_hbm = (qg_hbm, kg_hbm)[n]
+                some.append(pltpu.make_async_copy(gain_hbm, gain_ref.at[n], gain_sems.at[n]))
+            loads[n, c] = some
+            for load in some:
+                load.start()
+    spots = [group_and_slot(table_ref[PLACE, h], groups) for h in range(groups * heads)]
+    moves = []
+    for n, (moved_hbm, hbm) in enumerate(((out_hbm, dq_hbm), (dv_hbm, dk_hbm))):
+        places = []
+        for c in range(CHUNKS):
+            for load in loads[n, c]:
+                load.wait()
+        for head, (group, slot) in enumerate(spots):
             first = pl.multiple_of((n * heads + slot) * tokens, tokens)
-            moves.append(
-                pltpu.make_async_copy(
-                    back_ref.at[group, pl.ds(first, tokens), pl.ds(width, width)],
-                    hbm.at[:, pl.ds(head * width, width)],
-                    copy_sems.at[head, n],
-                )
+            places.append((group, first))
+            move = pltpu.make_async_copy(
+                back_ref.at[group, pl.ds(first, tokens), pl.ds(width, width)],
+                moved_hbm.at[:, pl.ds(head * width, width)],
+                copy_sems.at[head, n],
             )
-    for move in moves:
-        move.start()
-    for c in range(CHUNKS):
-        for n, (raw_ref, gain_ref, hbm) in enumerate(
-            ((q_ref, qg_ref, dq_hbm), (k_ref, kg_ref, dk_hbm))
-        ):
+            move.start()
+            moves.append(move)
+        for c in range(CHUNKS):
 
             def some_rows(i, carry):
                 row = pl.multiple_of(c * step + i * ROWS, ROWS)
-                x = raw_ref[pl.ds(row, ROWS)].astype(jnp.float32)
+                x = raw_ref[n, pl.ds(row, ROWS)].astype(jnp.float32)
                 inverse = inverse_rms(x)
                 unit = x * inverse
                 pieces = []
-                for group, slot in spots:
-                    first = pl.multiple_of((n * heads + slot) * tokens + row, ROWS)
-                    pieces.append(back_ref[group, pl.ds(first, ROWS), :width])
-                grads = jnp.concatenate(pieces, axis=-1)
-                g = grads.astype(jnp.float32) * gain_ref[...]
+                for group, first in places:
+                    at = pl.multiple_of(first + row, ROWS)
+                    pieces.append(back_ref[group, pl.ds(at, ROWS), :width])
+                g = jnp.concatenate(pieces, axis=-1).astype(jnp.float32) * gain_ref[n]
                 mean = jnp.mean(g * unit, axis=-1, keepdims=True)
                 done_ref[n, pl.ds(row, ROWS)] = (inverse * (g - unit * mean)).astype(jnp.bfloat16)
                 return carry
@@ -374,81 +397,81 @@
 def unpack(table, back, q, k, q_gain, k_gain):
     groups, _, both = back.shape
     tokens, features = q.shape
+    heads = 2 * features // (groups * both)
     hbm = pl.BlockSpec(memory_space=pltpu.HBM)
-    vmem = pl.BlockSpec(memory_space=pltpu.VMEM)
     return pl.pallas_call(
         unpack_kernel,
-        in_specs=[pl.BlockSpec(memory_space=pltpu.SMEM)] + [vmem] * 5,
+        in_specs=[pl.BlockSpec(memory_space=pltpu.SMEM)] + [hbm] * 5,
         out_specs=[hbm] * 4,
         out_shape=[jax.ShapeDtypeStruct((tokens, features), jnp.bfloat16)] * 4,
         scratch_shapes=[
             pltpu.VMEM((2, tokens, features), jnp.bfloat16),
+            pltpu.VMEM((groups, 2 * heads * tokens, both), jnp.bfloat16),
+            pltpu.VMEM((2, 1, features), jnp.float32),
+            pltpu.VMEM((2, tokens, features), jnp.bfloat16),
             pltpu.SemaphoreType.DMA((2, CHUNKS)),
-            pltpu.SemaphoreType.DMA((2 * features // both, 2)),
+            pltpu.SemaphoreType.DMA((2, CHUNKS, heads)),
+            pltpu.SemaphoreType.DMA((2,)),
+            pltpu.SemaphoreType.DMA((2, CHUNKS)),
+            pltpu.SemaphoreType.DMA((groups * heads, 2)),
         ],
-        compiler_params=pltpu.CompilerParams(vmem_limit_bytes=12 << 20),
+        compiler_params=pltpu.CompilerParams(vmem_limit_bytes=16 << 20),
         name="unpack",
-    )(table, back, q, k, q_gain[None], k_gain[None])
-
-
-def gains_kernel(table_ref, back_ref, out_ref):
-    groups, rows, _ = back_ref.shape
-    heads, width = out_ref.shape
+    )(table, *(in_hbm(x) for x in (back, q, k, q_gain[None], k_gain[None])))
+
+
+def gains_kernel(table_ref, back_hbm, out_ref, extra_ref, sem):
+    groups, rows, _ = back_hbm.shape
+    copies, heads, width = out_ref.shape
+    load = pltpu.make_async_copy(back_hbm.at[:, pl.ds(rows - SPARE, SPARE)], extra_ref, sem)
+    load.start()
+    load.wait()
     for head in range(heads):
         group, slot = group_and_slot(table_ref[PLACE, head], groups)
-        extra = back_ref[group, rows - SPARE :].astype(jnp.float32)
+        extra = extra_ref[group].astype(jnp.float32)
         total = extra[0:1]
         for n in range(1, PARTS):
             total = total + extra[n : n + 1]
-        out_ref[head : head + 1] = jnp.where(slot == 0, total[:, :width], total[:, width:])
-
-
-def add_kernel(a_ref, b_ref, out_ref):
-    out_ref[...] = a_ref[...] + b_ref[...]
-
-
-def last_kernel(a_ref, b_ref, qg_ref, kg_ref, q_ref, k_ref):
-    total = a_ref[...] + b_ref[...]
+        out_ref[0, head : head + 1] = jnp.where(slot == 0, total[:, :width], total[:, width:])
+    for copy in range(1, copies):
+        out_ref[copy] = out_ref[0]
+
+
+def gain_sums(table, back, copies):
+    groups, _, both = back.shape
+    return pl.pallas_call(
+        gains_kernel,
+        in_specs=[pl.BlockSpec(memory_space=pltpu.SMEM), pl.BlockSpec(memory_space=pltpu.HBM)],
+        out_specs=pl.BlockSpec(memory_space=pltpu.VMEM),
+        out_shape=jax.ShapeDtypeStruct((copies, table.shape[1], BLK), jnp.float32),
+        scratch_shapes=[
+            pltpu.VMEM((groups, SPARE, both), jnp.bfloat16),
+            pltpu.SemaphoreType.DMA(()),
+        ],
+        compiler_params=pltpu.CompilerParams(vmem_limit_bytes=2 << 20),
+        name="gains",
+    )(table, in_hbm(back))
+
+
+def last_kernel(terms_ref, qg_ref, kg_ref, q_ref, k_ref):
+    total = terms_ref[0]
+    for n in range(1, terms_ref.shape[0]):
+        total = total + terms_ref[n]
     q_ref[...] = total / qg_ref[...]
     k_ref[...] = total / kg_ref[...]
 
 
-def small_call(kernel, shapes, name, *args):
-    return pl.pallas_call(
-        kernel,
-        in_specs=[pl.BlockSpec(memory_space=pltpu.VMEM)] * len(args),
-        out_specs=[pl.BlockSpec(memory_space=pltpu.VMEM)] * len(shapes),
-        out_shape=[jax.ShapeDtypeStruct(shape, jnp.float32) for shape in shapes],
+def last(terms, q_gain, k_gain):
+    shape = terms.shape[1:]
+    vmem = pl.BlockSpec(memory_space=pltpu.VMEM)
+    q, k = pl.pallas_call(
+        last_kernel,
+        in_specs=[vmem] * 3,
+        out_specs=[vmem] * 2,
+        out_shape=[jax.ShapeDtypeStruct(shape, jnp.float32)] * 2,
         compiler_params=pltpu.CompilerParams(vmem_limit_bytes=2 << 20),
-        name=name,
-    )(*args)
-
-
-def clip_gains(table, back, q_gain, k_gain):
-    size = lax.axis_size("clip")
-    rows = q_gain.shape[0] // BLK
-    total = pl.pallas_call(
-        gains_kernel,
-        in_specs=[pl.BlockSpec(memory_space=pltpu.SMEM), pl.BlockSpec(memory_space=pltpu.VMEM)],
-        out_specs=pl.BlockSpec(memory_space=pltpu.VMEM),
-        out_shape=jax.ShapeDtypeStruct((rows, BLK), jnp.float32),
-        compiler_params=pltpu.CompilerParams(vmem_limit_bytes=2 << 20),
-        name="gains",
-    )(table, back)
-    flips = [1, 2, 6]
-    for n, flip in enumerate(flips):
-        other = lax.ppermute(total, "clip", [(i, i ^ flip) for i in range(size)])
-        if n < len(flips) - 1:
-            (total,) = small_call(add_kernel, [(rows, BLK)], "add", total, other)
-    q, k = small_call(
-        last_kernel,
-        [(rows, BLK)] * 2,
-        "last",
-        total,
-        other,
-        q_gain.reshape(rows, BLK),
-        k_gain.reshape(rows, BLK),
-    )
+        name="last",
+    )(terms, q_gain.reshape(shape), k_gain.reshape(shape))
     return q.reshape(-1), k.reshape(-1)
 
 
@@ -464,10 +487,12 @@
     arrived = lax.all_to_all(packed, "seq", split_axis=0, concat_axis=0, tiled=True)
     results = attention(mine, table, lists, live, arrived, heads)
     back = lax.all_to_all(results, "seq", split_axis=0, concat_axis=0, tiled=True)
+    copies = gain_sums(table, back, lax.axis_size("clip"))
+    terms = lax.all_to_all(copies, "clip", split_axis=0, concat_axis=0, tiled=True)
     attended, grad_query, grad_key, grad_value = unpack(
         table, back, query_raw[0], key_raw[0], query_gain, key_gain
     )
-    q_total, k_total = clip_gains(table, back, query_gain, key_gain)
+    q_total, k_total = last(terms, query_gain, key_gain)
     return (
         attended[None],
         grad_query[None],

time: 143 us -> 145 us (1.014); the launches traced: 143 us -> 143 us
  waiting for transfers between devices: 3.45 us -> 0.01 us
  Pallas kernels: 21.6 us -> 24.3 us
    ppermute x3 -> x0, starting transfers between devices: 4.43 us -> none  [clip_gains(): other = lax.ppermute(total, 'clip', [(i, i ^ flip) for i in range(size)])]
    all_to_all x0 -> x1, starting transfers between devices: none -> 4.36 us  [shards(): lax.all_to_all(copies, 'clip', split_axis=0, concat_axis=0, tiled=True)]
    ppermute x3 -> x0, waiting for transfers between devices: 3.45 us -> none  [clip_gains(): other = lax.ppermute(total, 'clip', [(i, i ^ flip) for i in range(size)])]
    pallas_call x1, Pallas kernels: 4.68 us -> 6.72 us  [unpack(): pl.pallas_call(unpack_kernel, in_specs=[pl.BlockSpec(memory_space=pltpu.S...]
    pallas_call x5 -> x3, Pallas kernels: 12.3 us -> 13.6 us  [the longest x1 10.8 us: attention(): pl.pallas_call(attention_kernel, in_specs=[smem, smem, smem, pl.BlockSpec...]
  transfers between devices with their start and end apart: 3 -> 1, of which waited for: 2 -> 0; matrix products, arithmetic and copies ran while one was open for 0% -> 0% of each run, Pallas kernels for 3% -> 5%
where the time goes in v7:
time: 145 us; the launch traced here: 143 us
  blocking collectives  113 us (78%)
  Pallas kernels  24.3 us (17%)
  starting transfers between devices  4.36 us (3%)
    all_to_all x1, blocking collectives, shards(): lax.all_to_all(packed, 'seq', split_axis=0, concat_axis=0, tiled=True)  58.6 us
    all_to_all x1, blocking collectives, shards(): lax.all_to_all(results, 'seq', split_axis=0, concat_axis=0, tiled=True)  54.6 us
    pallas_call x1, Pallas kernels, attention(): pl.pallas_call(attention_kernel, in_specs=[smem, smem, smem, pl.BlockSpec...  10.8 us
    pallas_call x1, Pallas kernels, unpack(): pl.pallas_call(unpack_kernel, in_specs=[pl.BlockSpec(memory_space=pltpu.S...  6.72 us
    all_to_all x1, starting transfers between devices, shards(): lax.all_to_all(copies, 'clip', split_axis=0, concat_axis=0, tiled=True)  4.36 us
    pallas_call x1, Pallas kernels, pack(): pl.pallas_call(pack_kernel, in_specs=[hbm] * 7, out_specs=[vmem, pl.Block...  4 us
  transfers between devices with their start and end apart: 1, of which 0 were waited for; matrix products, arithmetic and copies ran while one was open for 0% of the time, Pallas kernels for 5%

profile of v7, /device:TPU:0, one launch (start us, length us, event | category | flops | bytes accessed | tf_op | source)
XLA Modules:
  0.0 142.7 jit_solution(9386592786055139367)
XLA Ops:
  0.6 4.0 %pack.1 = (bf16[16,512,256]{2,1,0:T(8,128)(2,1)S(1)}, s32[2,32]{1,0:T(2,128)S(1)}) custom-call(s32[1,32]{1,0:T(1,128)} %live_ref.1, bf16[128,4096]{1,0:T(8,128)(2,1)} %bitcast.25, bf16[128,4096]{1,0:T(8,128)(2,1)} %bitcast.27, bf16[128,4096]{1,0:T(8,128)(2,1)} %bitcast.29, bf16[128,4096]{1,0:T(8,128)(2,1)} %bitcast.30, f32[1,4096]{1,0:T(1,128)} %bitcast.18, ...), custom_call_target="tpu_custom_call" | custom-call | tf_op jit(solution)/shard_map/pack/pallas_call | solution.py:142
  4.6 0.0 copy-start.2
  4.7 0.0 copy-start.3
  4.7 58.6 %all_to_all.15.in_ref = bf16[16,512,256]{2,1,0:T(8,128)(2,1)S(1)} all-to-all(bf16[16,512,256]{2,1,0:T(8,128)(2,1)S(1)} %get-tuple-element.19), channel_id=1, replica_groups=mesh['clip'=8,'seq'=16] {'seq'}, dimensions={0} | all-to-all | bytes 8388608 | tf_op jit(solution)/shard_map/all_to_all | solution.py:487
  63.3 0.0 copy-done.2
  63.3 0.0 copy-done.3
  63.3 10.8 %attention.1 = bf16[16,520,256]{2,1,0:T(8,128)(2,1)S(1)} custom-call(s32[1]{0:T(128)} %bitcast.6.mine_ref, s32[2,32]{1,0:T(2,128)S(1)} %get-tuple-element.16.table_ref, s32[1,32]{1,0:T(1,128)S(1)} %copy-done.3, s32[16,4,32]{2,1,0:T(4,128)S(1)} %bitcast.24, bf16[16,512,256]{2,1,0:T(8,128)(2,1)S(1)} %all_to_all.15.in_ref), custom_call_target="tpu_custom_call" | custom-call | tf_op jit(solution)/shard_map/attention/pallas_call | solution.py:292
  74.1 54.6 %all_to_all.16.back_hbm = bf16[16,520,256]{2,1,0:T(8,128)(2,1)} all-to-all(bf16[16,520,256]{2,1,0:T(8,128)(2,1)S(1)} %attention.1), channel_id=1, replica_groups=mesh['clip'=8,'seq'=16] {'seq'}, dimensions={0} | all-to-all | bytes 8519680 | tf_op jit(solution)/shard_map/all_to_all | solution.py:489
  128.8 2.2 %gains.1 = f32[8,32,128]{2,1,0:T(8,128)} custom-call(s32[2,32]{1,0:T(2,128)S(1)} %get-tuple-element.16.table_ref, bf16[16,520,256]{2,1,0:T(8,128)(2,1)} %all_to_all.16.back_hbm), custom_call_target="tpu_custom_call" | custom-call | tf_op jit(solution)/shard_map/gains/pallas_call | solution.py:442
  130.9 0.0 copy-start
  130.9 0.0 copy-start.1
  130.9 4.4 %all-to-all-start.2 = ((f32[8,32,128]{2,1,0:T(8,128)}), f32[8,32,128]{2,1,0:T(8,128)S(1)}, u32[]{:S(2)}, u32[]{:S(2)}) async-start(f32[8,32,128]{2,1,0:T(8,128)} %gains.1), calls=%async_computation.2 | async-start | bytes 262144 | tf_op jit(solution)/shard_map/all_to_all | solution.py:491
  135.3 6.7 %unpack.1 = (bf16[128,4096]{1,0:T(8,128)(2,1)}, bf16[128,4096]{1,0:T(8,128)(2,1)}, bf16[128,4096]{1,0:T(8,128)(2,1)}, bf16[128,4096]{1,0:T(8,128)(2,1)}) custom-call(s32[2,32]{1,0:T(2,128)S(1)} %get-tuple-element.16.table_ref, bf16[16,520,256]{2,1,0:T(8,128)(2,1)} %all_to_all.16.back_hbm, bf16[128,4096]{1,0:T(8,128)(2,1)} %bitcast.26, ...), custom_call_target="tpu_custom_call" | custom-call | tf_op jit(solution)/shard_map/unpack/pallas_call | solution.py:402
  142.0 0.0 all-to-all-done.2.terms_ref
  142.1 0.0 copy-done
  142.1 0.0 copy-done.1
  142.1 0.6 last.1
Async XLA Ops:
  4.6 58.7 %copy-start.2 = (s32[1,32,16,4]{1,3,2,0:T(4,128)S(1)}, s32[1,32,16,4]{1,3,2,0:T(4,128)}, u32[]{:S(2)}) copy-start(s32[1,32,16,4]{1,3,2,0:T(4,128)} %param.14) | copy-start | bytes 24580
  4.7 58.7 %copy-start.3 = (s32[1,32]{1,0:T(1,128)S(1)}, s32[1,32]{1,0:T(1,128)}, u32[]{:S(2)}) copy-start(s32[1,32]{1,0:T(1,128)} %live_ref.1) | copy-start | bytes 388
  130.9 11.1 %copy-start = (f32[4096]{0:T(1024)S(1)}, f32[4096]{0:T(1024)}, u32[]{:S(2)}) copy-start(f32[4096]{0:T(1024)} %param.12) | copy-start | bytes 49156
  130.9 11.1 %copy-start.1 = (f32[4096]{0:T(1024)S(1)}, f32[4096]{0:T(1024)}, u32[]{:S(2)}) copy-start(f32[4096]{0:T(1024)} %param.13) | copy-start | bytes 49156
  130.9 11.1 %all-to-all-start.2 = ((f32[8,32,128]{2,1,0:T(8,128)}), f32[8,32,128]{2,1,0:T(8,128)S(1)}, u32[]{:S(2)}, u32[]{:S(2)}) async-start(f32[8,32,128]{2,1,0:T(8,128)} %gains.1), calls=%async_computation.2 | async-start | bytes 262144 | tf_op jit(solution)/shard_map/all_to_all | solution.py:491
